TPU v7x, 768 devices: a whole 4x8x12 slice. The times are simulated.
768 devices in a mesh: gx: 4 (over x_lo, core), gy: 12 (over z), gz: 16 (over y, x_hi).
Axes of the slice: x: 4 (x_hi: 2, x_lo: 2; x = x_hi * 2 + x_lo), y: 8, z: 12, core: 2. Of those that a mesh axis runs over, the one named last changes fastest.
Arguments:
- gauge_links: float32 [4, 3, 3, 2, 8, 24, 16, 128], P(None, None, None, None, 'gx', 'gy', 'gz'), may hold values from -1 to 1, as said below
- momenta: float32 [4, 3, 3, 2, 8, 24, 16, 128], P(None, None, None, None, 'gx', 'gy', 'gz'), may hold values from -6 to 6, as said below
Outputs:
- new_links: float32 [4, 3, 3, 2, 8, 24, 16, 128], P(None, None, None, None, 'gx', 'gy', 'gz')
- new_momenta: float32 [4, 3, 3, 2, 8, 24, 16, 128], P(None, None, None, None, 'gx', 'gy', 'gz')
Inputs may be any that keep to these rules, and one draw needn't show every extreme that they name: `gauge_links`: every link is a unitary 3 x 3 matrix of determinant one. `momenta`: every momentum is an anti-Hermitian 3 x 3 matrix of trace zero.
All inputs are finite; a program needn't handle non-finite values.
Results may differ from a plain program's by a relative error of at most 0.0001.
Values sent between devices are 32-bit elements; how exact they have to be, the bound alone decides.
No kernel may reach another device: no remote copies, remote signals or barrier semaphores. Data moves between devices by JAX's collectives and lax.ppermute only.
A program may use at most 32 MiB of HBM per device.

v0:
```python
import jax
import jax.numpy as jnp
from jax import lax
from jax.sharding import PartitionSpec as P

BETA = 5.7
STEP = 0.25


def shifted(value, axis, steps):
    count = lax.axis_size(axis)
    pairs = [(source, (source + steps) % count) for source in range(count)]
    return lax.ppermute(value, axis, pairs)


def product(left, right):
    left_real = left[:, :, 0]
    left_imag = left[:, :, 1]
    right_real = right[:, :, 0]
    right_imag = right[:, :, 1]
    real_part = jnp.sum(
        left_real[:, :, None] * right_real[None] - left_imag[:, :, None] * right_imag[None], axis=1
    )
    imag_part = jnp.sum(
        left_real[:, :, None] * right_imag[None] + left_imag[:, :, None] * right_real[None], axis=1
    )
    return jnp.stack([real_part, imag_part], axis=2)


def dagger(matrix):
    return jnp.stack(
        [jnp.swapaxes(matrix[:, :, 0], 0, 1), -jnp.swapaxes(matrix[:, :, 1], 0, 1)], axis=2
    )


def add_identity(matrix):
    identity = jnp.eye(3, dtype=jnp.float32).reshape((3, 3) + (1,) * (matrix.ndim - 3))
    return jnp.stack([matrix[:, :, 0] + identity, matrix[:, :, 1]], axis=2)


def exponent(generator):
    series = add_identity(generator / 4.0)
    series = add_identity(product(generator, series) / 3.0)
    series = add_identity(product(generator, series) / 2.0)
    return add_identity(product(generator, series))


def project(omega):
    real_part = 0.5 * (omega[:, :, 0] - jnp.swapaxes(omega[:, :, 0], 0, 1))
    imag_part = 0.5 * (omega[:, :, 1] + jnp.swapaxes(omega[:, :, 1], 0, 1))
    trace = (omega[0, 0, 1] + omega[1, 1, 1] + omega[2, 2, 1]) / 3.0
    identity = jnp.eye(3, dtype=jnp.float32).reshape((3, 3) + (1,) * trace.ndim)
    imag_part = imag_part - identity * trace
    return jnp.stack([real_part, imag_part], axis=2)


def send_ahead(slab, axis):
    if axis == 0:
        return shifted(slab, "gx", -1)
    if axis == 1:
        return shifted(slab, "gy", -1)
    return shifted(slab, "gz", -1)


def send_back(slab, axis):
    if axis == 0:
        return shifted(slab, "gx", 1)
    if axis == 1:
        return shifted(slab, "gy", 1)
    return shifted(slab, "gz", 1)


def ahead_faces(field):
    faces = {}
    for axis in range(3):
        others = [direction for direction in range(4) if direction != axis]
        slab = jnp.stack(
            [lax.slice_in_dim(field[direction], 0, 1, axis=3 + axis) for direction in others]
        )
        received = send_ahead(slab, axis)
        faces[axis] = {direction: received[number] for number, direction in enumerate(others)}
    return faces


def ahead_link(field, faces, direction, axis):
    if axis == 3:
        return jnp.roll(field[direction], -1, axis=6)
    extent = field[direction].shape[3 + axis]
    inner = lax.slice_in_dim(field[direction], 1, extent, axis=3 + axis)
    return jnp.concatenate([inner, faces[axis][direction]], axis=3 + axis)


def returned_forces(field):
    faces = ahead_faces(field)
    uppers = {}
    lower_sites = {}
    for along in range(4):
        for across in range(4):
            if across == along:
                continue
            step_along = ahead_link(field, faces, across, along)
            step_across = ahead_link(field, faces, along, across)
            uppers[along, across] = product(
                product(step_along, dagger(step_across)), dagger(field[across])
            )
            lower_sites[along, across] = product(
                product(dagger(step_along), dagger(field[along])), field[across]
            )
    lowers = {}
    for across in range(4):
        alongs = [along for along in range(4) if along != across]
        if across == 3:
            for along in alongs:
                lowers[along, across] = jnp.roll(lower_sites[along, across], 1, axis=6)
            continue
        extent = field[0].shape[3 + across]
        slab = jnp.stack(
            [
                lax.slice_in_dim(lower_sites[along, across], extent - 1, extent, axis=3 + across)
                for along in alongs
            ]
        )
        received = send_back(slab, across)
        for number, along in enumerate(alongs):
            inner = lax.slice_in_dim(lower_sites[along, across], 0, extent - 1, axis=3 + across)
            lowers[along, across] = jnp.concatenate([received[number], inner], axis=3 + across)
    result = []
    for along in range(4):
        running = jnp.zeros_like(field[along])
        for across in range(4):
            if across == along:
                continue
            running = running + uppers[along, across] + lowers[along, across]
        omega = product(field[along], running)
        result.append(BETA / 3.0 * project(omega))
    return result


def forces(field):
    return returned_forces(field)


def body(gauge_links, momenta):
    field = [gauge_links[direction] for direction in range(4)]
    moment = [momenta[direction] for direction in range(4)]
    kick = forces(field)
    moment = [moment[direction] - 0.5 * STEP * kick[direction] for direction in range(4)]
    for repeat in range(2):
        field = [
            product(exponent(STEP * moment[direction]), field[direction]) for direction in range(4)
        ]
        kick = forces(field)
        factor = STEP if repeat == 0 else 0.5 * STEP
        moment = [moment[direction] - factor * kick[direction] for direction in range(4)]
    return (jnp.stack(field), jnp.stack(moment))


def solution(mesh):
    placed = (
        P(None, None, None, None, "gx", "gy", "gz", None),
        P(None, None, None, None, "gx", "gy", "gz", None),
    )
    return jax.shard_map(
        body,
        mesh=mesh,
        in_specs=placed,
        out_specs=(
            P(None, None, None, None, "gx", "gy", "gz", None),
            P(None, None, None, None, "gx", "gy", "gz", None),
        ),
        check_vma=False,
    )
```

profile of v0, /device:TPU:1, one launch (start us, length us, event | category | flops | bytes accessed | tf_op | source)
XLA Modules:
  0.0 145.1 jit_solution(6757854130821435959)
XLA Ops:
  0.6 0.8 fusion.286
  1.6 15.3 %collective-permute-start.1 = (f32[3,3,3,2,2,1,1,128]{7,3,2,1,4,6,5,0:T(2,128)S(1)}, f32[3,3,3,2,2,1,1,128]{7,3,2,1,4,6,5,0:T(2,128)S(1)}, u32[]{:S(2)}, u32[]{:S(2)}) collective-permute-start(f32[3,3,3,2,2,1,1,128]{7,3,2,1,4,6,5,0:T(2,128)S(1)} %pad_maximum_fusion.9), channel_id=1, source_target_pairs={{0,176},{16,0},{32,16},{48,32},{64,48},{80,64},{96,80},{112,96},{1... | collective-permute-start | bytes 165896 | tf_op jit(solution)/shard_map/ppermute | solution.py:13
  17.0 2.9 %collective-permute-start = (f32[3,3,3,2,1,2,1,128]{7,5,3,2,1,6,4,0:T(2,128)S(1)}, f32[3,3,3,2,1,2,1,128]{7,5,3,2,1,6,4,0:T(2,128)S(1)}, u32[]{:S(2)}, u32[]{:S(2)}) collective-permute-start(f32[3,3,3,2,1,2,1,128]{7,5,3,2,1,6,4,0:T(2,128)S(1)} %pad_maximum_fusion.8), channel_id=1, source_target_pairs={{0,576},{192,0},{384,192},{576,384},{1,577},{193,1},{385,193},{577... | collective-permute-start | bytes 165896 | tf_op jit(solution)/shard_map/ppermute | solution.py:13
  20.0 7.6 %collective-permute-start.2 = (f32[3,3,3,2,2,2,1,128]{7,6,5,4,3,2,1,0:T(1,128)S(1)}, f32[3,3,3,2,2,2,1,128]{7,6,5,4,3,2,1,0:T(1,128)S(1)}, u32[]{:S(2)}, u32[]{:S(2)}) collective-permute-start(f32[3,3,3,2,2,2,1,128]{7,6,5,4,3,2,1,0:T(1,128)S(1)} %pad_maximum_fusion.2), channel_id=1, source_target_pairs={{0,15},{1,0},{2,1},{3,2},{4,3},{5,4},{6,5},{7,6},{8,7},{9,8},{10,9... | collective-permute-start | bytes 331784 | tf_op jit(solution)/shard_map/ppermute | solution.py:13
  28.1 0.8 copy-done.1
  30.8 0.6 subtract_reduce_fusion.151
  31.8 0.6 subtract_reduce_fusion.153
  32.4 0.6 subtract_reduce_fusion.161
  33.0 0.6 subtract_reduce_fusion.150
  33.6 0.3 subtract_reduce_fusion.149
  34.0 0.3 add_reduce_fusion.160
  34.7 2.4 %collective-permute-start.5 = (f32[3,3,3,2,1,2,1,128]{7,5,2,1,3,6,4,0:T(2,128)S(1)}, f32[3,3,3,2,1,2,1,128]{7,5,2,1,3,6,4,0:T(2,128)S(1)}, u32[]{:S(2)}, u32[]{:S(2)}) collective-permute-start(f32[3,3,3,2,1,2,1,128]{7,5,2,1,3,6,4,0:T(2,128)S(1)} %pad_maximum_fusion.11), channel_id=1, source_target_pairs={{0,192},{192,384},{384,576},{576,0},{1,193},{193,385},{385,577},{5... | collective-permute-start | bytes 165896 | tf_op jit(solution)/shard_map/ppermute | solution.py:13
  37.5 4.1 %collective-permute-start.4 = (f32[3,3,3,2,2,2,1,128]{7,5,4,2,1,3,6,0:T(2,128)S(1)}, f32[3,3,3,2,2,2,1,128]{7,5,4,2,1,3,6,0:T(2,128)S(1)}, u32[]{:S(2)}, u32[]{:S(2)}) collective-permute-start(f32[3,3,3,2,2,2,1,128]{7,5,4,2,1,3,6,0:T(2,128)S(1)} %pad_maximum_fusion.3), channel_id=1, source_target_pairs={{0,1},{1,2},{2,3},{3,4},{4,5},{5,6},{6,7},{7,8},{8,9},{9,10},{10,1... | collective-permute-start | bytes 331784 | tf_op jit(solution)/shard_map/ppermute | solution.py:13
  42.3 6.2 %collective-permute-done.4 = f32[3,3,3,2,2,2,1,128]{7,5,4,2,1,3,6,0:T(2,128)S(1)} collective-permute-done((f32[3,3,3,2,2,2,1,128]{7,5,4,2,1,3,6,0:T(2,128)S(1)}, f32[3,3,3,2,2,2,1,128]{7,5,4,2,1,3,6,0:T(2,128)S(1)}, u32[]{:S(2)}, u32[]{:S(2)}) %collective-permute-start.4) | collective-permute-done | bytes 110624 | tf_op jit(solution)/shard_map/ppermute | solution.py:13
  49.6 0.3 subtract_reduce_fusion.144
  50.4 2.1 %collective-permute-start.3 = (f32[3,3,3,2,2,1,1,128]{7,4,2,1,3,6,5,0:T(2,128)S(1)}, f32[3,3,3,2,2,1,1,128]{7,4,2,1,3,6,5,0:T(2,128)S(1)}, u32[]{:S(2)}, u32[]{:S(2)}) collective-permute-start(f32[3,3,3,2,2,1,1,128]{7,4,2,1,3,6,5,0:T(2,128)S(1)} %pad_maximum_fusion.10), channel_id=1, source_target_pairs={{0,16},{16,32},{32,48},{48,64},{64,80},{80,96},{96,112},{112,128},... | collective-permute-start | bytes 165896 | tf_op jit(solution)/shard_map/ppermute | solution.py:13
  52.7 4.1 %collective-permute-done.3 = f32[3,3,3,2,2,1,1,128]{7,4,2,1,3,6,5,0:T(2,128)S(1)} collective-permute-done((f32[3,3,3,2,2,1,1,128]{7,4,2,1,3,6,5,0:T(2,128)S(1)}, f32[3,3,3,2,2,1,1,128]{7,4,2,1,3,6,5,0:T(2,128)S(1)}, u32[]{:S(2)}, u32[]{:S(2)}) %collective-permute-start.3) | collective-permute-done | bytes 55328 | tf_op jit(solution)/shard_map/ppermute | solution.py:13
  61.0 1.9 %collective-permute-start.7 = (f32[3,3,3,2,2,1,1,128]{7,4,2,1,3,6,5,0:T(2,128)S(1)}, f32[3,3,3,2,2,1,1,128]{7,4,2,1,3,6,5,0:T(2,128)S(1)}, u32[]{:S(2)}, u32[]{:S(2)}) collective-permute-start(f32[3,3,3,2,2,1,1,128]{7,4,2,1,3,6,5,0:T(2,128)S(1)} %pad_maximum_fusion.13), channel_id=1, source_target_pairs={{0,176},{16,0},{32,16},{48,32},{64,48},{80,64},{96,80},{112,96},{1... | collective-permute-start | bytes 165896 | tf_op jit(solution)/shard_map/ppermute | solution.py:13
  63.0 2.9 %collective-permute-start.6 = (f32[3,3,3,2,1,2,1,128]{7,5,3,2,1,6,4,0:T(2,128)S(1)}, f32[3,3,3,2,1,2,1,128]{7,5,3,2,1,6,4,0:T(2,128)S(1)}, u32[]{:S(2)}, u32[]{:S(2)}) collective-permute-start(f32[3,3,3,2,1,2,1,128]{7,5,3,2,1,6,4,0:T(2,128)S(1)} %pad_maximum_fusion.12), channel_id=1, source_target_pairs={{0,576},{192,0},{384,192},{576,384},{1,577},{193,1},{385,193},{577... | collective-permute-start | bytes 165896 | tf_op jit(solution)/shard_map/ppermute | solution.py:13
  65.9 5.3 %collective-permute-start.8 = (f32[3,3,3,2,2,2,1,128]{7,4,2,1,3,5,6,0:T(2,128)S(1)}, f32[3,3,3,2,2,2,1,128]{7,4,2,1,3,5,6,0:T(2,128)S(1)}, u32[]{:S(2)}, u32[]{:S(2)}) collective-permute-start(f32[3,3,3,2,2,2,1,128]{7,4,2,1,3,5,6,0:T(2,128)S(1)} %pad_maximum_fusion.4), channel_id=1, source_target_pairs={{0,15},{1,0},{2,1},{3,2},{4,3},{5,4},{6,5},{7,6},{8,7},{9,8},{10,9... | collective-permute-start | bytes 331784 | tf_op jit(solution)/shard_map/ppermute | solution.py:13
  72.4 1.5 %collective-permute-done.8 = f32[3,3,3,2,2,2,1,128]{7,4,2,1,3,5,6,0:T(2,128)S(1)} collective-permute-done((f32[3,3,3,2,2,2,1,128]{7,4,2,1,3,5,6,0:T(2,128)S(1)}, f32[3,3,3,2,2,2,1,128]{7,4,2,1,3,5,6,0:T(2,128)S(1)}, u32[]{:S(2)}, u32[]{:S(2)}) %collective-permute-start.8) | collective-permute-done | bytes 110624 | tf_op jit(solution)/shard_map/ppermute | solution.py:13
  74.5 0.7 subtract_reduce_fusion.101
  75.1 0.7 subtract_reduce_fusion.102
  75.8 0.6 subtract_reduce_fusion.110
  76.7 0.6 subtract_reduce_fusion.118
  77.8 3.6 %collective-permute-start.9 = (f32[3,3,3,2,2,1,1,128]{7,4,2,1,3,6,5,0:T(2,128)S(1)}, f32[3,3,3,2,2,1,1,128]{7,4,2,1,3,6,5,0:T(2,128)S(1)}, u32[]{:S(2)}, u32[]{:S(2)}) collective-permute-start(f32[3,3,3,2,2,1,1,128]{7,4,2,1,3,6,5,0:T(2,128)S(1)} %pad_maximum_fusion.14), channel_id=1, source_target_pairs={{0,16},{16,32},{32,48},{48,64},{64,80},{80,96},{96,112},{112,128},... | collective-permute-start | bytes 165896 | tf_op jit(solution)/shard_map/ppermute | solution.py:13
  82.9 2.1 %collective-permute-start.10 = (f32[3,3,3,2,2,2,1,128]{7,5,4,2,1,3,6,0:T(2,128)S(1)}, f32[3,3,3,2,2,2,1,128]{7,5,4,2,1,3,6,0:T(2,128)S(1)}, u32[]{:S(2)}, u32[]{:S(2)}) collective-permute-start(f32[3,3,3,2,2,2,1,128]{7,5,4,2,1,3,6,0:T(2,128)S(1)} %pad_maximum_fusion.5), channel_id=1, source_target_pairs={{0,1},{1,2},{2,3},{3,4},{4,5},{5,6},{6,7},{7,8},{8,9},{9,10},{10,1... | collective-permute-start | bytes 331784 | tf_op jit(solution)/shard_map/ppermute | solution.py:13
  85.1 7.4 %collective-permute-done.10 = f32[3,3,3,2,2,2,1,128]{7,5,4,2,1,3,6,0:T(2,128)S(1)} collective-permute-done((f32[3,3,3,2,2,2,1,128]{7,5,4,2,1,3,6,0:T(2,128)S(1)}, f32[3,3,3,2,2,2,1,128]{7,5,4,2,1,3,6,0:T(2,128)S(1)}, u32[]{:S(2)}, u32[]{:S(2)}) %collective-permute-start.10) | collective-permute-done | bytes 110624 | tf_op jit(solution)/shard_map/ppermute | solution.py:13
  93.6 0.3 add_reduce_fusion.95
  94.4 4.6 %collective-permute-start.11 = (f32[3,3,3,2,1,2,1,128]{7,5,2,1,3,6,4,0:T(2,128)S(1)}, f32[3,3,3,2,1,2,1,128]{7,5,2,1,3,6,4,0:T(2,128)S(1)}, u32[]{:S(2)}, u32[]{:S(2)}) collective-permute-start(f32[3,3,3,2,1,2,1,128]{7,5,2,1,3,6,4,0:T(2,128)S(1)} %pad_maximum_fusion.15), channel_id=1, source_target_pairs={{0,192},{192,384},{384,576},{576,0},{1,193},{193,385},{385,577},{5... | collective-permute-start | bytes 165896 | tf_op jit(solution)/shard_map/ppermute | solution.py:13
  99.2 0.8 collective-permute-done.11
  104.0 3.8 %collective-permute-start.12 = (f32[3,3,3,2,1,2,1,128]{7,5,2,1,3,6,4,0:T(2,128)S(1)}, f32[3,3,3,2,1,2,1,128]{7,5,2,1,3,6,4,0:T(2,128)S(1)}, u32[]{:S(2)}, u32[]{:S(2)}) collective-permute-start(f32[3,3,3,2,1,2,1,128]{7,5,2,1,3,6,4,0:T(2,128)S(1)} %pad_maximum_fusion.16), channel_id=1, source_target_pairs={{0,576},{192,0},{384,192},{576,384},{1,577},{193,1},{385,193},{577... | collective-permute-start | bytes 165896 | tf_op jit(solution)/shard_map/ppermute | solution.py:13
  107.8 2.9 %collective-permute-start.13 = (f32[3,3,3,2,2,1,1,128]{7,4,2,1,3,6,5,0:T(2,128)S(1)}, f32[3,3,3,2,2,1,1,128]{7,4,2,1,3,6,5,0:T(2,128)S(1)}, u32[]{:S(2)}, u32[]{:S(2)}) collective-permute-start(f32[3,3,3,2,2,1,1,128]{7,4,2,1,3,6,5,0:T(2,128)S(1)} %pad_maximum_fusion.17), channel_id=1, source_target_pairs={{0,176},{16,0},{32,16},{48,32},{64,48},{80,64},{96,80},{112,96},{1... | collective-permute-start | bytes 165896 | tf_op jit(solution)/shard_map/ppermute | solution.py:13
  110.9 0.8 copy.5647
  111.8 5.1 %collective-permute-start.14 = (f32[3,3,3,2,2,2,1,128]{7,5,4,2,1,3,6,0:T(2,128)S(1)}, f32[3,3,3,2,2,2,1,128]{7,5,4,2,1,3,6,0:T(2,128)S(1)}, u32[]{:S(2)}, u32[]{:S(2)}) collective-permute-start(f32[3,3,3,2,2,2,1,128]{7,5,4,2,1,3,6,0:T(2,128)S(1)} %pad_maximum_fusion.6), channel_id=1, source_target_pairs={{0,15},{1,0},{2,1},{3,2},{4,3},{5,4},{6,5},{7,6},{8,7},{9,8},{10,9... | collective-permute-start | bytes 331784 | tf_op jit(solution)/shard_map/ppermute | solution.py:13
  118.0 1.5 %collective-permute-done.14 = f32[3,3,3,2,2,2,1,128]{7,5,4,2,1,3,6,0:T(2,128)S(1)} collective-permute-done((f32[3,3,3,2,2,2,1,128]{7,5,4,2,1,3,6,0:T(2,128)S(1)}, f32[3,3,3,2,2,2,1,128]{7,5,4,2,1,3,6,0:T(2,128)S(1)}, u32[]{:S(2)}, u32[]{:S(2)}) %collective-permute-start.14) | collective-permute-done | bytes 110624 | tf_op jit(solution)/shard_map/ppermute | solution.py:13
  119.8 0.6 subtract_reduce_fusion.34
  120.4 0.6 subtract_reduce_fusion.33
  121.0 0.7 subtract_reduce_fusion.42
  122.1 0.6 subtract_reduce_fusion.50
  123.1 2.4 %collective-permute-start.15 = (f32[3,3,3,2,2,1,1,128]{7,4,2,1,3,6,5,0:T(2,128)S(1)}, f32[3,3,3,2,2,1,1,128]{7,4,2,1,3,6,5,0:T(2,128)S(1)}, u32[]{:S(2)}, u32[]{:S(2)}) collective-permute-start(f32[3,3,3,2,2,1,1,128]{7,4,2,1,3,6,5,0:T(2,128)S(1)} %pad_maximum_fusion.18), channel_id=1, source_target_pairs={{0,16},{16,32},{32,48},{48,64},{64,80},{80,96},{96,112},{112,128},... | collective-permute-start | bytes 165896 | tf_op jit(solution)/shard_map/ppermute | solution.py:13
  127.0 1.9 %collective-permute-start.16 = (f32[3,3,3,2,2,2,1,128]{7,5,4,2,1,3,6,0:T(2,128)S(1)}, f32[3,3,3,2,2,2,1,128]{7,5,4,2,1,3,6,0:T(2,128)S(1)}, u32[]{:S(2)}, u32[]{:S(2)}) collective-permute-start(f32[3,3,3,2,2,2,1,128]{7,5,4,2,1,3,6,0:T(2,128)S(1)} %pad_maximum_fusion.7), channel_id=1, source_target_pairs={{0,1},{1,2},{2,3},{3,4},{4,5},{5,6},{6,7},{7,8},{8,9},{9,10},{10,1... | collective-permute-start | bytes 331784 | tf_op jit(solution)/shard_map/ppermute | solution.py:13
  128.9 0.3 collective-permute-done.15
  129.3 7.1 %collective-permute-done.16 = f32[3,3,3,2,2,2,1,128]{7,5,4,2,1,3,6,0:T(2,128)S(1)} collective-permute-done((f32[3,3,3,2,2,2,1,128]{7,5,4,2,1,3,6,0:T(2,128)S(1)}, f32[3,3,3,2,2,2,1,128]{7,5,4,2,1,3,6,0:T(2,128)S(1)}, u32[]{:S(2)}, u32[]{:S(2)}) %collective-permute-start.16) | collective-permute-done | bytes 110624 | tf_op jit(solution)/shard_map/ppermute | solution.py:13
  136.5 0.3 subtract_reduce_fusion.31
  137.1 4.7 %collective-permute-start.17 = (f32[3,3,3,2,1,2,1,128]{7,5,2,1,3,6,4,0:T(2,128)S(1)}, f32[3,3,3,2,1,2,1,128]{7,5,2,1,3,6,4,0:T(2,128)S(1)}, u32[]{:S(2)}, u32[]{:S(2)}) collective-permute-start(f32[3,3,3,2,1,2,1,128]{7,5,2,1,3,6,4,0:T(2,128)S(1)} %pad_maximum_fusion.19), channel_id=1, source_target_pairs={{0,192},{192,384},{384,576},{576,0},{1,193},{193,385},{385,577},{5... | collective-permute-start | bytes 165896 | tf_op jit(solution)/shard_map/ppermute | solution.py:13
  141.8 1.2 collective-permute-done.17
  144.3 0.8 copy.5648
  (583 shorter events, 22.5 us)
Async XLA Ops:
  1.6 15.3 %copy-start = (f32[4,3,3,2,2,2,1,128]{7,6,5,4,3,2,1,0:T(1,128)S(1)}, f32[4,3,3,2,2,2,1,128]{7,6,5,4,3,2,1,0:T(1,128)}, u32[]{:S(2)}) copy-start(f32[4,3,3,2,2,2,1,128]{7,6,5,4,3,2,1,0:T(1,128)} %param.2) | copy-start | bytes 442372
  1.6 28.0 %collective-permute-start.1 = (f32[3,3,3,2,2,1,1,128]{7,3,2,1,4,6,5,0:T(2,128)S(1)}, f32[3,3,3,2,2,1,1,128]{7,3,2,1,4,6,5,0:T(2,128)S(1)}, u32[]{:S(2)}, u32[]{:S(2)}) collective-permute-start(f32[3,3,3,2,2,1,1,128]{7,3,2,1,4,6,5,0:T(2,128)S(1)} %pad_maximum_fusion.9), channel_id=1, source_target_pairs={{0,176},{16,0},{32,16},{48,32},{64,48},{80,64},{96,80},{112,96},{1... | collective-permute-start | bytes 165896 | tf_op jit(solution)/shard_map/ppermute | solution.py:13
  17.0 12.8 %collective-permute-start = (f32[3,3,3,2,1,2,1,128]{7,5,3,2,1,6,4,0:T(2,128)S(1)}, f32[3,3,3,2,1,2,1,128]{7,5,3,2,1,6,4,0:T(2,128)S(1)}, u32[]{:S(2)}, u32[]{:S(2)}) collective-permute-start(f32[3,3,3,2,1,2,1,128]{7,5,3,2,1,6,4,0:T(2,128)S(1)} %pad_maximum_fusion.8), channel_id=1, source_target_pairs={{0,576},{192,0},{384,192},{576,384},{1,577},{193,1},{385,193},{577... | collective-permute-start | bytes 165896 | tf_op jit(solution)/shard_map/ppermute | solution.py:13
  20.0 10.7 %collective-permute-start.2 = (f32[3,3,3,2,2,2,1,128]{7,6,5,4,3,2,1,0:T(1,128)S(1)}, f32[3,3,3,2,2,2,1,128]{7,6,5,4,3,2,1,0:T(1,128)S(1)}, u32[]{:S(2)}, u32[]{:S(2)}) collective-permute-start(f32[3,3,3,2,2,2,1,128]{7,6,5,4,3,2,1,0:T(1,128)S(1)} %pad_maximum_fusion.2), channel_id=1, source_target_pairs={{0,15},{1,0},{2,1},{3,2},{4,3},{5,4},{6,5},{7,6},{8,7},{9,8},{10,9... | collective-permute-start | bytes 331784 | tf_op jit(solution)/shard_map/ppermute | solution.py:13
  27.9 0.9 copy-start.1
  34.7 7.5 %collective-permute-start.5 = (f32[3,3,3,2,1,2,1,128]{7,5,2,1,3,6,4,0:T(2,128)S(1)}, f32[3,3,3,2,1,2,1,128]{7,5,2,1,3,6,4,0:T(2,128)S(1)}, u32[]{:S(2)}, u32[]{:S(2)}) collective-permute-start(f32[3,3,3,2,1,2,1,128]{7,5,2,1,3,6,4,0:T(2,128)S(1)} %pad_maximum_fusion.11), channel_id=1, source_target_pairs={{0,192},{192,384},{384,576},{576,0},{1,193},{193,385},{385,577},{5... | collective-permute-start | bytes 165896 | tf_op jit(solution)/shard_map/ppermute | solution.py:13
  37.5 10.9 %collective-permute-start.4 = (f32[3,3,3,2,2,2,1,128]{7,5,4,2,1,3,6,0:T(2,128)S(1)}, f32[3,3,3,2,2,2,1,128]{7,5,4,2,1,3,6,0:T(2,128)S(1)}, u32[]{:S(2)}, u32[]{:S(2)}) collective-permute-start(f32[3,3,3,2,2,2,1,128]{7,5,4,2,1,3,6,0:T(2,128)S(1)} %pad_maximum_fusion.3), channel_id=1, source_target_pairs={{0,1},{1,2},{2,3},{3,4},{4,5},{5,6},{6,7},{7,8},{8,9},{9,10},{10,1... | collective-permute-start | bytes 331784 | tf_op jit(solution)/shard_map/ppermute | solution.py:13
  50.4 6.4 %collective-permute-start.3 = (f32[3,3,3,2,2,1,1,128]{7,4,2,1,3,6,5,0:T(2,128)S(1)}, f32[3,3,3,2,2,1,1,128]{7,4,2,1,3,6,5,0:T(2,128)S(1)}, u32[]{:S(2)}, u32[]{:S(2)}) collective-permute-start(f32[3,3,3,2,2,1,1,128]{7,4,2,1,3,6,5,0:T(2,128)S(1)} %pad_maximum_fusion.10), channel_id=1, source_target_pairs={{0,16},{16,32},{32,48},{48,64},{64,80},{80,96},{96,112},{112,128},... | collective-permute-start | bytes 165896 | tf_op jit(solution)/shard_map/ppermute | solution.py:13
  61.0 10.3 %collective-permute-start.7 = (f32[3,3,3,2,2,1,1,128]{7,4,2,1,3,6,5,0:T(2,128)S(1)}, f32[3,3,3,2,2,1,1,128]{7,4,2,1,3,6,5,0:T(2,128)S(1)}, u32[]{:S(2)}, u32[]{:S(2)}) collective-permute-start(f32[3,3,3,2,2,1,1,128]{7,4,2,1,3,6,5,0:T(2,128)S(1)} %pad_maximum_fusion.13), channel_id=1, source_target_pairs={{0,176},{16,0},{32,16},{48,32},{64,48},{80,64},{96,80},{112,96},{1... | collective-permute-start | bytes 165896 | tf_op jit(solution)/shard_map/ppermute | solution.py:13
  63.0 8.5 %collective-permute-start.6 = (f32[3,3,3,2,1,2,1,128]{7,5,3,2,1,6,4,0:T(2,128)S(1)}, f32[3,3,3,2,1,2,1,128]{7,5,3,2,1,6,4,0:T(2,128)S(1)}, u32[]{:S(2)}, u32[]{:S(2)}) collective-permute-start(f32[3,3,3,2,1,2,1,128]{7,5,3,2,1,6,4,0:T(2,128)S(1)} %pad_maximum_fusion.12), channel_id=1, source_target_pairs={{0,576},{192,0},{384,192},{576,384},{1,577},{193,1},{385,193},{577... | collective-permute-start | bytes 165896 | tf_op jit(solution)/shard_map/ppermute | solution.py:13
  65.9 8.0 %collective-permute-start.8 = (f32[3,3,3,2,2,2,1,128]{7,4,2,1,3,5,6,0:T(2,128)S(1)}, f32[3,3,3,2,2,2,1,128]{7,4,2,1,3,5,6,0:T(2,128)S(1)}, u32[]{:S(2)}, u32[]{:S(2)}) collective-permute-start(f32[3,3,3,2,2,2,1,128]{7,4,2,1,3,5,6,0:T(2,128)S(1)} %pad_maximum_fusion.4), channel_id=1, source_target_pairs={{0,15},{1,0},{2,1},{3,2},{4,3},{5,4},{6,5},{7,6},{8,7},{9,8},{10,9... | collective-permute-start | bytes 331784 | tf_op jit(solution)/shard_map/ppermute | solution.py:13
  77.8 7.2 %collective-permute-start.9 = (f32[3,3,3,2,2,1,1,128]{7,4,2,1,3,6,5,0:T(2,128)S(1)}, f32[3,3,3,2,2,1,1,128]{7,4,2,1,3,6,5,0:T(2,128)S(1)}, u32[]{:S(2)}, u32[]{:S(2)}) collective-permute-start(f32[3,3,3,2,2,1,1,128]{7,4,2,1,3,6,5,0:T(2,128)S(1)} %pad_maximum_fusion.14), channel_id=1, source_target_pairs={{0,16},{16,32},{32,48},{48,64},{64,80},{80,96},{96,112},{112,128},... | collective-permute-start | bytes 165896 | tf_op jit(solution)/shard_map/ppermute | solution.py:13
  82.9 9.6 %collective-permute-start.10 = (f32[3,3,3,2,2,2,1,128]{7,5,4,2,1,3,6,0:T(2,128)S(1)}, f32[3,3,3,2,2,2,1,128]{7,5,4,2,1,3,6,0:T(2,128)S(1)}, u32[]{:S(2)}, u32[]{:S(2)}) collective-permute-start(f32[3,3,3,2,2,2,1,128]{7,5,4,2,1,3,6,0:T(2,128)S(1)} %pad_maximum_fusion.5), channel_id=1, source_target_pairs={{0,1},{1,2},{2,3},{3,4},{4,5},{5,6},{6,7},{7,8},{8,9},{9,10},{10,1... | collective-permute-start | bytes 331784 | tf_op jit(solution)/shard_map/ppermute | solution.py:13
  94.4 5.6 %collective-permute-start.11 = (f32[3,3,3,2,1,2,1,128]{7,5,2,1,3,6,4,0:T(2,128)S(1)}, f32[3,3,3,2,1,2,1,128]{7,5,2,1,3,6,4,0:T(2,128)S(1)}, u32[]{:S(2)}, u32[]{:S(2)}) collective-permute-start(f32[3,3,3,2,1,2,1,128]{7,5,2,1,3,6,4,0:T(2,128)S(1)} %pad_maximum_fusion.15), channel_id=1, source_target_pairs={{0,192},{192,384},{384,576},{576,0},{1,193},{193,385},{385,577},{5... | collective-permute-start | bytes 165896 | tf_op jit(solution)/shard_map/ppermute | solution.py:13
  104.0 12.9 %collective-permute-start.12 = (f32[3,3,3,2,1,2,1,128]{7,5,2,1,3,6,4,0:T(2,128)S(1)}, f32[3,3,3,2,1,2,1,128]{7,5,2,1,3,6,4,0:T(2,128)S(1)}, u32[]{:S(2)}, u32[]{:S(2)}) collective-permute-start(f32[3,3,3,2,1,2,1,128]{7,5,2,1,3,6,4,0:T(2,128)S(1)} %pad_maximum_fusion.16), channel_id=1, source_target_pairs={{0,576},{192,0},{384,192},{576,384},{1,577},{193,1},{385,193},{577... | collective-permute-start | bytes 165896 | tf_op jit(solution)/shard_map/ppermute | solution.py:13
  107.8 9.3 %collective-permute-start.13 = (f32[3,3,3,2,2,1,1,128]{7,4,2,1,3,6,5,0:T(2,128)S(1)}, f32[3,3,3,2,2,1,1,128]{7,4,2,1,3,6,5,0:T(2,128)S(1)}, u32[]{:S(2)}, u32[]{:S(2)}) collective-permute-start(f32[3,3,3,2,2,1,1,128]{7,4,2,1,3,6,5,0:T(2,128)S(1)} %pad_maximum_fusion.17), channel_id=1, source_target_pairs={{0,176},{16,0},{32,16},{48,32},{64,48},{80,64},{96,80},{112,96},{1... | collective-permute-start | bytes 165896 | tf_op jit(solution)/shard_map/ppermute | solution.py:13
  111.8 7.7 %collective-permute-start.14 = (f32[3,3,3,2,2,2,1,128]{7,5,4,2,1,3,6,0:T(2,128)S(1)}, f32[3,3,3,2,2,2,1,128]{7,5,4,2,1,3,6,0:T(2,128)S(1)}, u32[]{:S(2)}, u32[]{:S(2)}) collective-permute-start(f32[3,3,3,2,2,2,1,128]{7,5,4,2,1,3,6,0:T(2,128)S(1)} %pad_maximum_fusion.6), channel_id=1, source_target_pairs={{0,15},{1,0},{2,1},{3,2},{4,3},{5,4},{6,5},{7,6},{8,7},{9,8},{10,9... | collective-permute-start | bytes 331784 | tf_op jit(solution)/shard_map/ppermute | solution.py:13
  123.1 6.1 %collective-permute-start.15 = (f32[3,3,3,2,2,1,1,128]{7,4,2,1,3,6,5,0:T(2,128)S(1)}, f32[3,3,3,2,2,1,1,128]{7,4,2,1,3,6,5,0:T(2,128)S(1)}, u32[]{:S(2)}, u32[]{:S(2)}) collective-permute-start(f32[3,3,3,2,2,1,1,128]{7,4,2,1,3,6,5,0:T(2,128)S(1)} %pad_maximum_fusion.18), channel_id=1, source_target_pairs={{0,16},{16,32},{32,48},{48,64},{64,80},{80,96},{96,112},{112,128},... | collective-permute-start | bytes 165896 | tf_op jit(solution)/shard_map/ppermute | solution.py:13
  127.0 9.4 %collective-permute-start.16 = (f32[3,3,3,2,2,2,1,128]{7,5,4,2,1,3,6,0:T(2,128)S(1)}, f32[3,3,3,2,2,2,1,128]{7,5,4,2,1,3,6,0:T(2,128)S(1)}, u32[]{:S(2)}, u32[]{:S(2)}) collective-permute-start(f32[3,3,3,2,2,2,1,128]{7,5,4,2,1,3,6,0:T(2,128)S(1)} %pad_maximum_fusion.7), channel_id=1, source_target_pairs={{0,1},{1,2},{2,3},{3,4},{4,5},{5,6},{6,7},{7,8},{8,9},{9,10},{10,1... | collective-permute-start | bytes 331784 | tf_op jit(solution)/shard_map/ppermute | solution.py:13
  137.1 5.9 %collective-permute-start.17 = (f32[3,3,3,2,1,2,1,128]{7,5,2,1,3,6,4,0:T(2,128)S(1)}, f32[3,3,3,2,1,2,1,128]{7,5,2,1,3,6,4,0:T(2,128)S(1)}, u32[]{:S(2)}, u32[]{:S(2)}) collective-permute-start(f32[3,3,3,2,1,2,1,128]{7,5,2,1,3,6,4,0:T(2,128)S(1)} %pad_maximum_fusion.19), channel_id=1, source_target_pairs={{0,192},{192,384},{384,576},{576,0},{1,193},{193,385},{385,577},{5... | collective-permute-start | bytes 165896 | tf_op jit(solution)/shard_map/ppermute | solution.py:13
where the time goes:
time: 146 us; the launch traced here: 145 us
  starting transfers between devices  75.6 us (52%)
  waiting for transfers between devices  30.1 us (21%)
  other arithmetic  27.5 us (19%)
  local copies, waits for them, and re-layouts  7.25 us (5%)
  between operations  4.69 us (3%)
    ppermute x18, starting transfers between devices, shifted(): return lax.ppermute(value, axis, pairs)  75.6 us
    ppermute x18, waiting for transfers between devices, shifted(): return lax.ppermute(value, axis, pairs)  30.1 us
    reduce_sum x91, other arithmetic, product(): jnp.sum(left_real[:, :, None] * right_real[None] - left_imag[:, :, None]...  16.6 us
  transfers between devices with their start and end apart: 18, of which 9 were waited for; matrix products, arithmetic and copies ran while one was open for 6% of the time, Pallas kernels for 0%

commit v1 on v0

v1 whole, which is shorter than its diff:
```python
import functools

import jax
import jax.numpy as jnp
from jax import lax
from jax.experimental import pallas as pl
from jax.experimental.pallas import tpu as pltpu
from jax.sharding import PartitionSpec as P

BETA = 5.7
STEP = 0.25
F32 = jnp.float32

OTHERS = ((1, 2, 3), (0, 2, 3), (0, 1, 3))
PLANES = ((0, 1), (0, 2), (0, 3), (1, 2), (1, 3), (2, 3))
PAIRS = ((0, 1), (0, 2), (1, 2))


def mat(ref, base):
    return [[(ref[base + 6 * i + 2 * j], ref[base + 6 * i + 2 * j + 1]) for j in range(3)] for i in range(3)]


def put(ref, base, m):
    for i in range(3):
        for j in range(3):
            ref[base + 6 * i + 2 * j] = m[i][j][0]
            ref[base + 6 * i + 2 * j + 1] = m[i][j][1]


def dag(m):
    return [[(m[j][i][0], -m[j][i][1]) for j in range(3)] for i in range(3)]


def total(terms):
    out = terms[0]
    for t in terms[1:]:
        out = out + t
    return out


def re_dot(a, b, ca, cb):
    if ca == cb:
        return total([x[0] * y[0] - x[1] * y[1] for x, y in zip(a, b)])
    return total([x[0] * y[0] + x[1] * y[1] for x, y in zip(a, b)])


def im_dot(a, b, ca, cb):
    if not ca and not cb:
        return total([x[0] * y[1] + x[1] * y[0] for x, y in zip(a, b)])
    if ca and not cb:
        return total([x[0] * y[1] - x[1] * y[0] for x, y in zip(a, b)])
    if cb and not ca:
        return total([x[1] * y[0] - x[0] * y[1] for x, y in zip(a, b)])
    return -total([x[0] * y[1] + x[1] * y[0] for x, y in zip(a, b)])


def row(m, i, d):
    return [m[k][i] for k in range(3)] if d else [m[i][k] for k in range(3)]


def col(m, j, d):
    return [m[j][k] for k in range(3)] if d else [m[k][j] for k in range(3)]


def mul(a, b, da=False, db=False):
    return [
        [(re_dot(row(a, i, da), col(b, j, db), da, db), im_dot(row(a, i, da), col(b, j, db), da, db)) for j in range(3)]
        for i in range(3)
    ]


def anti(a, b, da=False, db=False):
    out = []
    for i, j in PAIRS:
        ri, cj, rj, ci = row(a, i, da), col(b, j, db), row(a, j, da), col(b, i, db)
        out.append(re_dot(ri, cj, da, db) - re_dot(rj, ci, da, db))
        out.append(im_dot(ri, cj, da, db) + im_dot(rj, ci, da, db))
    for i in range(3):
        out.append(im_dot(row(a, i, da), col(b, i, db), da, db))
    return out


def expand(h):
    m = [[None] * 3 for _ in range(3)]
    for n, (i, j) in enumerate(PAIRS):
        m[i][j] = (h[2 * n], h[2 * n + 1])
        m[j][i] = (-h[2 * n], h[2 * n + 1])
    for i in range(3):
        m[i][i] = (None, h[6 + i])
    return m


def step_x(own, halo):
    return jnp.concatenate([own[2:4], halo], axis=0)


def step_y(own, halo):
    return jnp.concatenate([own[1:2], halo[0:1], own[3:4], halo[1:2]], axis=0)


def back_x(own, halo):
    return jnp.concatenate([halo, own[0:2]], axis=0)


def back_y(own, halo):
    return jnp.concatenate([halo[0:1], own[0:1], halo[1:2], own[2:3]], axis=0)


def faces(u_ref, mz, my, mx):
    for n, d in enumerate(OTHERS[2]):
        for c in range(18):
            mz[18 * n + c] = u_ref[18 * d + c]
    for n, d in enumerate(OTHERS[1]):
        for c in range(18):
            my[18 * n + c, 0:1] = u_ref[18 * d + c, 0:1]
            my[18 * n + c, 1:2] = u_ref[18 * d + c, 2:3]
    for n, d in enumerate(OTHERS[0]):
        for c in range(18):
            mx[18 * n + c] = u_ref[18 * d + c, 0:2]


def first_kernel(u_ref, mz, my, mx):
    faces(u_ref, mz, my, mx)


def local_kernel(u_ref, r_ref):
    for n, (mu, nu) in enumerate(PLANES):
        put(r_ref, 18 * n, mul(mat(u_ref, 18 * mu), mat(u_ref, 18 * nu), da=True))


def lower_kernel(u_ref, r_ref, rz, ry, rx, tz, ty, tx, sx, sy, st, own_x, own_y, own_t):
    for n, d in enumerate(OTHERS[0]):
        for c in range(18):
            sx[18 * n + c] = step_x(u_ref[18 * d + c], rx[18 * n + c])
    for n, d in enumerate(OTHERS[1]):
        for c in range(18):
            sy[18 * n + c] = step_y(u_ref[18 * d + c], ry[18 * n + c])
    for d in range(3):
        for c in range(18):
            st[18 * d + c] = pltpu.roll(u_ref[18 * d + c], 127, 1)
    moved = (sx, sy, rz, st)

    def at(direction, axis):
        where = OTHERS[axis].index(direction) if axis < 3 else direction
        return mat(moved[axis], 18 * where)

    lows = (own_x, own_y, tz, own_t)
    for n, (mu, nu) in enumerate(PLANES):
        q = mul(at(mu, nu), at(nu, mu), db=True)
        r = mat(r_ref, 18 * n)
        for along, across, d in ((mu, nu, False), (nu, mu, True)):
            where = OTHERS[across].index(along) if across < 3 else along
            for c, v in enumerate(anti(q, r, da=d, db=d)):
                lows[across][9 * where + c] = v
    for k in range(27):
        ty[k, 0:1] = own_y[k, 1:2]
        ty[k, 1:2] = own_y[k, 3:4]
        tx[k] = own_x[k, 2:4]


def upper_kernel(u_ref, rz, sx, sy, st, own_t, f_ref):
    moved = (sx, sy, rz, st)

    def at(direction, axis):
        where = OTHERS[axis].index(direction) if axis < 3 else direction
        return mat(moved[axis], 18 * where)

    for k in range(27):
        f_ref[k] = pltpu.roll(own_t[k], 1, 1)
    for k in range(9):
        f_ref[27 + k] = jnp.zeros((4, 128), F32)
    for mu, nu in PLANES:
        first = mul(mat(u_ref, 18 * mu), at(nu, mu))
        second = mul(mat(u_ref, 18 * nu), at(mu, nu))
        for c, v in enumerate(anti(first, second, db=True)):
            f_ref[9 * mu + c] = f_ref[9 * mu + c] + v
            f_ref[9 * nu + c] = f_ref[9 * nu + c] - v


def force_of(d, f_ref, tz, ty, tx, own_x, own_y):
    out = []
    for c in range(9):
        v = f_ref[9 * d + c]
        if d != 0:
            k = 9 * OTHERS[0].index(d) + c
            v = v + back_x(own_x[k], tx[k])
        if d != 1:
            k = 9 * OTHERS[1].index(d) + c
            v = v + back_y(own_y[k], ty[k])
        if d != 2:
            k = 9 * OTHERS[2].index(d) + c
            v = v + tz[k]
        out.append(v)
    mean = (out[6] + out[7] + out[8]) * (1.0 / 3.0)
    return [0.5 * v for v in out[:6]] + [v - mean for v in out[6:]]


def read_momenta(p_ref, d, full):
    if not full:
        return [p_ref[9 * d + c] for c in range(9)]
    out = []
    for i, j in PAIRS:
        out += [p_ref[18 * d + 6 * i + 2 * j], p_ref[18 * d + 6 * i + 2 * j + 1]]
    return out + [p_ref[18 * d + 8 * i + 1] for i in range(3)]


def square(x):
    h = [[None] * 3 for _ in range(3)]
    m = expand(x)
    for i in range(3):
        for j in range(i, 3):
            re, im = [], []
            for k in range(3):
                a, b = m[i][k], m[k][j]
                if a[0] is not None and b[0] is not None:
                    re.append(a[0] * b[0])
                re.append(-(a[1] * b[1]))
                if a[0] is not None:
                    im.append(a[0] * b[1])
                if b[0] is not None:
                    im.append(a[1] * b[0])
            h[i][j] = (total(re), total(im) if i != j else None)
            if i != j:
                h[j][i] = (h[i][j][0], -h[i][j][1])
    return h


def exponent(x):
    h, m = square(x), expand(x)
    k = [[None] * 3 for _ in range(3)]
    for i in range(3):
        for j in range(3):
            if i == j:
                k[i][j] = (h[i][j][0] * (1.0 / 24.0) + 0.5, m[i][j][1] * (1.0 / 6.0))
            else:
                k[i][j] = tuple(h[i][j][c] * (1.0 / 24.0) + m[i][j][c] * (1.0 / 6.0) for c in range(2))
    e = [[None] * 3 for _ in range(3)]
    for i in range(3):
        for j in range(3):
            re, im = [], []
            for n in range(3):
                a, b = h[i][n], k[n][j]
                re.append(a[0] * b[0])
                im.append(a[0] * b[1])
                if a[1] is not None:
                    re.append(-(a[1] * b[1]))
                    im.append(a[1] * b[0])
            re, im = total(re), total(im)
            if i == j:
                e[i][j] = (re + 1.0, im + m[i][j][1])
            else:
                e[i][j] = (re + m[i][j][0], im + m[i][j][1])
    return e


def drift_kernel(factor, full, u_ref, p_ref, f_ref, tz, ty, tx, own_x, own_y, q_ref, v_ref, mz, my, mx):
    for d in range(4):
        force = force_of(d, f_ref, tz, ty, tx, own_x, own_y)
        p = [a - (factor * BETA / 3.0) * b for a, b in zip(read_momenta(p_ref, d, full), force)]
        for c in range(9):
            q_ref[9 * d + c] = p[c]
        put(v_ref, 18 * d, mul(exponent([STEP * a for a in p]), mat(u_ref, 18 * d)))
    faces(v_ref, mz, my, mx)


def last_kernel(factor, p_ref, f_ref, tz, ty, tx, own_x, own_y, q_ref):
    for d in range(4):
        force = force_of(d, f_ref, tz, ty, tx, own_x, own_y)
        p = [a - (factor * BETA / 3.0) * b for a, b in zip(read_momenta(p_ref, d, False), force)]
        m = expand(p)
        for i in range(3):
            for j in range(3):
                re = jnp.zeros((4, 128), F32) if m[i][j][0] is None else m[i][j][0]
                q_ref[18 * d + 6 * i + 2 * j] = re
                q_ref[18 * d + 6 * i + 2 * j + 1] = m[i][j][1]


def call(kernel, outs, name, products):
    vm = pl.BlockSpec(memory_space=pltpu.VMEM)

    def run(*args):
        size = sum(a.size for a in args) + sum(o[0] * o[1] * 128 for o in outs)
        return pl.pallas_call(
            kernel,
            out_shape=[jax.ShapeDtypeStruct((o[0], o[1], 128), F32) for o in outs],
            in_specs=[vm] * len(args),
            out_specs=[vm] * len(outs),
            name=name,
            cost_estimate=pl.CostEstimate(flops=products * 200 * 512, bytes_accessed=4 * size, transcendentals=0),
            compiler_params=pltpu.CompilerParams(vmem_limit_bytes=8 * 1024 * 1024),
        )(*args)

    return run


def shifted(value, axis, steps):
    count = lax.axis_size(axis)
    return lax.ppermute(value, axis, [(source, (source + steps) % count) for source in range(count)])


def exchange(z, y, x, steps):
    return shifted(z, "gz", steps), shifted(y, "gy", steps), shifted(x, "gx", steps)


FACES = ((54, 4), (54, 2), (54, 2))


def body(gauge_links, momenta):
    u = gauge_links.reshape(72, 4, 128)
    p = momenta.reshape(72, 4, 128)
    sent = call(first_kernel, FACES, "first", 1)(u)
    for repeat in range(3):
        rz, ry, rx = exchange(*sent, -1)
        r = call(local_kernel, ((108, 4),), "local", 6)(u)[0]
        tz, ty, tx, sx, sy, st, own_x, own_y, own_t = call(
            lower_kernel,
            ((27, 4), (27, 2), (27, 2), (54, 4), (54, 4), (54, 4), (27, 4), (27, 4), (27, 4)),
            "lower",
            18,
        )(u, r, rz, ry, rx)
        gz, gy, gx = exchange(tz, ty, tx, 1)
        f = call(upper_kernel, ((36, 4),), "upper", 18)(u, rz, sx, sy, st, own_t)[0]
        factor = STEP if repeat == 1 else 0.5 * STEP
        if repeat < 2:
            p, u, *sent = call(
                functools.partial(drift_kernel, factor, repeat == 0), ((36, 4), (72, 4)) + FACES, "drift", 16
            )(u, p, f, gz, gy, gx, own_x, own_y)
        else:
            p = call(functools.partial(last_kernel, factor), ((72, 4),), "last", 2)(p, f, gz, gy, gx, own_x, own_y)[0]
    shape = gauge_links.shape
    return u.reshape(shape), p.reshape(shape)


def solution(mesh):
    placed = P(None, None, None, None, "gx", "gy", "gz", None)
    return jax.shard_map(
        body, mesh=mesh, in_specs=(placed, placed), out_specs=(placed, placed), check_vma=False
    )
```

time: 146 us -> 94.5 us (0.65)
  other arithmetic: 27.5 us -> 0 us
  waiting for transfers between devices: 30.1 us -> 14.4 us
  Pallas kernels: 0 us -> 5.96 us
  local copies, waits for them, and re-layouts: 7.25 us -> 1.82 us
  starting transfers between devices: 75.6 us -> 70.9 us
  between operations: 4.69 us -> 0.88 us
    reduce_sum x97 -> x0, other arithmetic: 17.9 us -> none  [the longest x91 16.6 us: product(): jnp.sum(left_real[:, :, None] * right_real[None] - left_imag[:, :, None]...]
    ppermute x18, waiting for transfers between devices: 30.1 us -> 14.4 us  [shifted(): lax.ppermute(value, axis, [(source, (source + steps) % count) for source...]
    pallas_call x0 -> x13, Pallas kernels: none -> 5.96 us  [run(): pl.pallas_call(kernel, out_shape=[jax.ShapeDtypeStruct((o[0], o[1], 128),...]
    ppermute x18, starting transfers between devices: 75.6 us -> 70.9 us  [shifted(): lax.ppermute(value, axis, [(source, (source + steps) % count) for source...]
    add x38 -> x0, other arithmetic: 3.31 us -> none  [the longest x26 2.01 us: add_identity(): return jnp.stack([matrix[:, :, 0] + identity, matrix[:, :, 1]], axis=2)]
    slice x89 -> x0, local copies, waits for them, and re-layouts: 2.81 us -> none  [the longest x2 0.82 us: body(): field = [gauge_links[direction] for direction in range(4)]]
    another operation x73 -> x0, other arithmetic: 2.7 us -> none  [the longest x16 0.96 us: product(): return jnp.stack([real_part, imag_part], axis=2)]
    mul x49 -> x0, other arithmetic: 1.83 us -> none  [the longest x29 1.18 us: product(): left_imag[:, :, None] * right_imag[None]]
  transfers between devices with their start and end apart: 18 -> 18, of which waited for: 9 -> 9; matrix products, arithmetic and copies ran while one was open for 6% -> 0% of each run, Pallas kernels for 0% -> 2%
where the time goes in v1:
time: 94.5 us; the launch traced here: 93.9 us
  starting transfers between devices  70.9 us (75%)
  waiting for transfers between devices  14.4 us (15%)
  Pallas kernels  5.96 us (6%)
  local copies, waits for them, and re-layouts  1.82 us (2%)
    ppermute x18, starting transfers between devices, shifted(): lax.ppermute(value, axis, [(source, (source + steps) % count) for source...  70.9 us
    ppermute x18, waiting for transfers between devices, shifted(): lax.ppermute(value, axis, [(source, (source + steps) % count) for source...  14.4 us
    pallas_call x13, Pallas kernels, run(): pl.pallas_call(kernel, out_shape=[jax.ShapeDtypeStruct((o[0], o[1], 128),...  5.96 us
  transfers between devices with their start and end apart: 18, of which 9 were waited for; matrix products, arithmetic and copies ran while one was open for 0% of the time, Pallas kernels for 2%

profile of v1, /device:TPU:1, one launch (start us, length us, event | category | flops | bytes accessed | tf_op | source)
XLA Modules:
  0.0 93.9 jit_solution(6245764655559357451)
XLA Ops:
  0.6 0.9 copy-done
  1.5 0.1 first.1
  1.6 8.4 %collective-permute-start = (f32[54,4,128]{2,1,0:T(4,128)S(1)}, f32[54,4,128]{2,1,0:T(4,128)S(1)}, u32[]{:S(2)}, u32[]{:S(2)}) collective-permute-start(f32[54,4,128]{2,1,0:T(4,128)S(1)} %get-tuple-element.42), channel_id=1, source_target_pairs={{0,15},{1,0},{2,1},{3,2},{4,3},{5,4},{6,5},{7,6},{8,7},{9,8},{10,9... | collective-permute-start | bytes 331784 | tf_op jit(solution)/shard_map/ppermute | solution.py:298
  10.0 14.3 %collective-permute-start.1 = (f32[54,2,128]{2,1,0:T(2,128)S(1)}, f32[54,2,128]{2,1,0:T(2,128)S(1)}, u32[]{:S(2)}, u32[]{:S(2)}) collective-permute-start(f32[54,2,128]{2,1,0:T(2,128)S(1)} %get-tuple-element.43), channel_id=1, source_target_pairs={{0,176},{16,0},{32,16},{48,32},{64,48},{80,64},{96,80},{112,96},{1... | collective-permute-start | bytes 165896 | tf_op jit(solution)/shard_map/ppermute | solution.py:298
  24.3 3.1 %collective-permute-start.2 = (f32[54,2,128]{2,1,0:T(2,128)S(1)}, f32[54,2,128]{2,1,0:T(2,128)S(1)}, u32[]{:S(2)}, u32[]{:S(2)}) collective-permute-start(f32[54,2,128]{2,1,0:T(2,128)S(1)} %get-tuple-element.44), channel_id=1, source_target_pairs={{0,576},{192,0},{384,192},{576,384},{1,577},{193,1},{385,193},{577... | collective-permute-start | bytes 165896 | tf_op jit(solution)/shard_map/ppermute | solution.py:298
  27.5 0.2 local.3.r_ref
  27.6 0.0 collective-permute-done.1.ry
  27.6 2.1 %collective-permute-done.2.rx = f32[54,2,128]{2,1,0:T(2,128)S(1)} collective-permute-done((f32[54,2,128]{2,1,0:T(2,128)S(1)}, f32[54,2,128]{2,1,0:T(2,128)S(1)}, u32[]{:S(2)}, u32[]{:S(2)}) %collective-permute-start.2) | collective-permute-done | bytes 55328 | tf_op jit(solution)/shard_map/ppermute | solution.py:298
  29.8 0.0 collective-permute-done.rz
  29.8 0.6 lower.3
  30.4 1.9 %collective-permute-start.3 = (f32[27,4,128]{2,1,0:T(4,128)S(1)}, f32[27,4,128]{2,1,0:T(4,128)S(1)}, u32[]{:S(2)}, u32[]{:S(2)}) collective-permute-start(f32[27,4,128]{2,1,0:T(4,128)S(1)} %get-tuple-element.49), channel_id=1, source_target_pairs={{0,1},{1,2},{2,3},{3,4},{4,5},{5,6},{6,7},{7,8},{8,9},{9,10},{10,1... | collective-permute-start | bytes 165896 | tf_op jit(solution)/shard_map/ppermute | solution.py:298
  32.3 1.9 %collective-permute-start.4 = (f32[27,2,128]{2,1,0:T(2,128)S(1)}, f32[27,2,128]{2,1,0:T(2,128)S(1)}, u32[]{:S(2)}, u32[]{:S(2)}) collective-permute-start(f32[27,2,128]{2,1,0:T(2,128)S(1)} %get-tuple-element.50), channel_id=1, source_target_pairs={{0,16},{16,32},{32,48},{48,64},{64,80},{80,96},{96,112},{112,128},... | collective-permute-start | bytes 82952 | tf_op jit(solution)/shard_map/ppermute | solution.py:298
  34.2 1.9 %collective-permute-start.5 = (f32[27,2,128]{2,1,0:T(2,128)S(1)}, f32[27,2,128]{2,1,0:T(2,128)S(1)}, u32[]{:S(2)}, u32[]{:S(2)}) collective-permute-start(f32[27,2,128]{2,1,0:T(2,128)S(1)} %get-tuple-element.51), channel_id=1, source_target_pairs={{0,192},{192,384},{384,576},{576,0},{1,193},{193,385},{385,577},{5... | collective-permute-start | bytes 82952 | tf_op jit(solution)/shard_map/ppermute | solution.py:298
  36.2 0.0 copy-start.2
  36.2 0.5 upper.3.f_ref
  36.7 2.0 %collective-permute-done.4.ty = f32[27,2,128]{2,1,0:T(2,128)S(1)} collective-permute-done((f32[27,2,128]{2,1,0:T(2,128)S(1)}, f32[27,2,128]{2,1,0:T(2,128)S(1)}, u32[]{:S(2)}, u32[]{:S(2)}) %collective-permute-start.4) | collective-permute-done | bytes 27680 | tf_op jit(solution)/shard_map/ppermute | solution.py:298
  38.7 0.0 collective-permute-done.5.tx
  38.7 1.0 %collective-permute-done.3.tz = f32[27,4,128]{2,1,0:T(4,128)S(1)} collective-permute-done((f32[27,4,128]{2,1,0:T(4,128)S(1)}, f32[27,4,128]{2,1,0:T(4,128)S(1)}, u32[]{:S(2)}, u32[]{:S(2)}) %collective-permute-start.3) | collective-permute-done | bytes 55328 | tf_op jit(solution)/shard_map/ppermute | solution.py:298
  39.7 0.4 drift.2
  40.0 5.8 %collective-permute-start.6 = (f32[54,4,128]{2,1,0:T(4,128)S(1)}, f32[54,4,128]{2,1,0:T(4,128)S(1)}, u32[]{:S(2)}, u32[]{:S(2)}) collective-permute-start(f32[54,4,128]{2,1,0:T(4,128)S(1)} %get-tuple-element.56), channel_id=1, source_target_pairs={{0,15},{1,0},{2,1},{3,2},{4,3},{5,4},{6,5},{7,6},{8,7},{9,8},{10,9... | collective-permute-start | bytes 331784 | tf_op jit(solution)/shard_map/ppermute | solution.py:298
  45.9 4.3 %collective-permute-start.7 = (f32[54,2,128]{2,1,0:T(2,128)S(1)}, f32[54,2,128]{2,1,0:T(2,128)S(1)}, u32[]{:S(2)}, u32[]{:S(2)}) collective-permute-start(f32[54,2,128]{2,1,0:T(2,128)S(1)} %get-tuple-element.57), channel_id=1, source_target_pairs={{0,176},{16,0},{32,16},{48,32},{64,48},{80,64},{96,80},{112,96},{1... | collective-permute-start | bytes 165896 | tf_op jit(solution)/shard_map/ppermute | solution.py:298
  50.2 3.8 %collective-permute-start.8 = (f32[54,2,128]{2,1,0:T(2,128)S(1)}, f32[54,2,128]{2,1,0:T(2,128)S(1)}, u32[]{:S(2)}, u32[]{:S(2)}) collective-permute-start(f32[54,2,128]{2,1,0:T(2,128)S(1)} %get-tuple-element.58), channel_id=1, source_target_pairs={{0,576},{192,0},{384,192},{576,384},{1,577},{193,1},{385,193},{577... | collective-permute-start | bytes 165896 | tf_op jit(solution)/shard_map/ppermute | solution.py:298
  54.0 0.2 local.4.r_ref
  54.1 2.1 %collective-permute-done.8.rx = f32[54,2,128]{2,1,0:T(2,128)S(1)} collective-permute-done((f32[54,2,128]{2,1,0:T(2,128)S(1)}, f32[54,2,128]{2,1,0:T(2,128)S(1)}, u32[]{:S(2)}, u32[]{:S(2)}) %collective-permute-start.8) | collective-permute-done | bytes 55328 | tf_op jit(solution)/shard_map/ppermute | solution.py:298
  56.2 0.0 collective-permute-done.6.rz
  56.2 0.6 lower.4
  56.8 1.9 %collective-permute-start.9 = (f32[27,4,128]{2,1,0:T(4,128)S(1)}, f32[27,4,128]{2,1,0:T(4,128)S(1)}, u32[]{:S(2)}, u32[]{:S(2)}) collective-permute-start(f32[27,4,128]{2,1,0:T(4,128)S(1)} %get-tuple-element.63), channel_id=1, source_target_pairs={{0,1},{1,2},{2,3},{3,4},{4,5},{5,6},{6,7},{7,8},{8,9},{9,10},{10,1... | collective-permute-start | bytes 165896 | tf_op jit(solution)/shard_map/ppermute | solution.py:298
  58.7 1.9 %collective-permute-start.10 = (f32[27,2,128]{2,1,0:T(2,128)S(1)}, f32[27,2,128]{2,1,0:T(2,128)S(1)}, u32[]{:S(2)}, u32[]{:S(2)}) collective-permute-start(f32[27,2,128]{2,1,0:T(2,128)S(1)} %get-tuple-element.64), channel_id=1, source_target_pairs={{0,16},{16,32},{32,48},{48,64},{64,80},{80,96},{96,112},{112,128},... | collective-permute-start | bytes 82952 | tf_op jit(solution)/shard_map/ppermute | solution.py:298
  60.7 1.9 %collective-permute-start.11 = (f32[27,2,128]{2,1,0:T(2,128)S(1)}, f32[27,2,128]{2,1,0:T(2,128)S(1)}, u32[]{:S(2)}, u32[]{:S(2)}) collective-permute-start(f32[27,2,128]{2,1,0:T(2,128)S(1)} %get-tuple-element.65), channel_id=1, source_target_pairs={{0,192},{192,384},{384,576},{576,0},{1,193},{193,385},{385,577},{5... | collective-permute-start | bytes 82952 | tf_op jit(solution)/shard_map/ppermute | solution.py:298
  62.6 0.5 upper.4.f_ref
  63.1 2.0 %collective-permute-done.10.ty = f32[27,2,128]{2,1,0:T(2,128)S(1)} collective-permute-done((f32[27,2,128]{2,1,0:T(2,128)S(1)}, f32[27,2,128]{2,1,0:T(2,128)S(1)}, u32[]{:S(2)}, u32[]{:S(2)}) %collective-permute-start.10) | collective-permute-done | bytes 27680 | tf_op jit(solution)/shard_map/ppermute | solution.py:298
  65.1 1.1 %collective-permute-done.9.tz = f32[27,4,128]{2,1,0:T(4,128)S(1)} collective-permute-done((f32[27,4,128]{2,1,0:T(4,128)S(1)}, f32[27,4,128]{2,1,0:T(4,128)S(1)}, u32[]{:S(2)}, u32[]{:S(2)}) %collective-permute-start.9) | collective-permute-done | bytes 55328 | tf_op jit(solution)/shard_map/ppermute | solution.py:298
  66.2 1.0 %drift.3 = (f32[36,4,128]{2,1,0:T(4,128)S(1)}, f32[72,4,128]{2,1,0:T(4,128)}, f32[54,4,128]{2,1,0:T(4,128)S(1)}, f32[54,2,128]{2,1,0:T(2,128)S(1)}, f32[54,2,128]{2,1,0:T(2,128)S(1)}) custom-call(f32[72,4,128]{2,1,0:T(4,128)S(1)} %get-tuple-element.54.u_ref, f32[36,4,128]{2,1,0:T(4,128)S(1)} %get-tuple-element.55.p_ref, f32[36,4,128]{2,1,0:T(4,128)S(1)} %upper.4.f_ref, ...), custom_call_target="tpu_custom_call" | custom-call | flops 1638400 | bytes 958464 | tf_op jit(solution)/shard_map/drift/pallas_call | solution.py:283
  67.2 5.3 %collective-permute-start.12 = (f32[54,4,128]{2,1,0:T(4,128)S(1)}, f32[54,4,128]{2,1,0:T(4,128)S(1)}, u32[]{:S(2)}, u32[]{:S(2)}) collective-permute-start(f32[54,4,128]{2,1,0:T(4,128)S(1)} %get-tuple-element.70), channel_id=1, source_target_pairs={{0,15},{1,0},{2,1},{3,2},{4,3},{5,4},{6,5},{7,6},{8,7},{9,8},{10,9... | collective-permute-start | bytes 331784 | tf_op jit(solution)/shard_map/ppermute | solution.py:298
  72.6 4.7 %collective-permute-start.13 = (f32[54,2,128]{2,1,0:T(2,128)S(1)}, f32[54,2,128]{2,1,0:T(2,128)S(1)}, u32[]{:S(2)}, u32[]{:S(2)}) collective-permute-start(f32[54,2,128]{2,1,0:T(2,128)S(1)} %get-tuple-element.71), channel_id=1, source_target_pairs={{0,176},{16,0},{32,16},{48,32},{64,48},{80,64},{96,80},{112,96},{1... | collective-permute-start | bytes 165896 | tf_op jit(solution)/shard_map/ppermute | solution.py:298
  77.3 3.8 %collective-permute-start.14 = (f32[54,2,128]{2,1,0:T(2,128)S(1)}, f32[54,2,128]{2,1,0:T(2,128)S(1)}, u32[]{:S(2)}, u32[]{:S(2)}) collective-permute-start(f32[54,2,128]{2,1,0:T(2,128)S(1)} %get-tuple-element.72), channel_id=1, source_target_pairs={{0,576},{192,0},{384,192},{576,384},{1,577},{193,1},{385,193},{577... | collective-permute-start | bytes 165896 | tf_op jit(solution)/shard_map/ppermute | solution.py:298
  81.1 0.0 copy-start.1
  81.1 0.9 copy-done.1
  82.0 0.2 local.5.r_ref
  82.2 1.1 %collective-permute-done.14.rx = f32[54,2,128]{2,1,0:T(2,128)S(1)} collective-permute-done((f32[54,2,128]{2,1,0:T(2,128)S(1)}, f32[54,2,128]{2,1,0:T(2,128)S(1)}, u32[]{:S(2)}, u32[]{:S(2)}) %collective-permute-start.14) | collective-permute-done | bytes 55328 | tf_op jit(solution)/shard_map/ppermute | solution.py:298
  83.3 0.6 lower.5
  83.9 1.9 %collective-permute-start.15 = (f32[27,4,128]{2,1,0:T(4,128)S(1)}, f32[27,4,128]{2,1,0:T(4,128)S(1)}, u32[]{:S(2)}, u32[]{:S(2)}) collective-permute-start(f32[27,4,128]{2,1,0:T(4,128)S(1)} %get-tuple-element.77), channel_id=1, source_target_pairs={{0,1},{1,2},{2,3},{3,4},{4,5},{5,6},{6,7},{7,8},{8,9},{9,10},{10,1... | collective-permute-start | bytes 165896 | tf_op jit(solution)/shard_map/ppermute | solution.py:298
  85.8 1.9 %collective-permute-start.16 = (f32[27,2,128]{2,1,0:T(2,128)S(1)}, f32[27,2,128]{2,1,0:T(2,128)S(1)}, u32[]{:S(2)}, u32[]{:S(2)}) collective-permute-start(f32[27,2,128]{2,1,0:T(2,128)S(1)} %get-tuple-element.78), channel_id=1, source_target_pairs={{0,16},{16,32},{32,48},{48,64},{64,80},{80,96},{96,112},{112,128},... | collective-permute-start | bytes 82952 | tf_op jit(solution)/shard_map/ppermute | solution.py:298
  87.7 1.9 %collective-permute-start.17 = (f32[27,2,128]{2,1,0:T(2,128)S(1)}, f32[27,2,128]{2,1,0:T(2,128)S(1)}, u32[]{:S(2)}, u32[]{:S(2)}) collective-permute-start(f32[27,2,128]{2,1,0:T(2,128)S(1)} %get-tuple-element.79), channel_id=1, source_target_pairs={{0,192},{192,384},{384,576},{576,0},{1,193},{193,385},{385,577},{5... | collective-permute-start | bytes 82952 | tf_op jit(solution)/shard_map/ppermute | solution.py:298
  89.7 0.5 upper.5.f_ref
  90.2 1.9 %collective-permute-done.16.ty = f32[27,2,128]{2,1,0:T(2,128)S(1)} collective-permute-done((f32[27,2,128]{2,1,0:T(2,128)S(1)}, f32[27,2,128]{2,1,0:T(2,128)S(1)}, u32[]{:S(2)}, u32[]{:S(2)}) %collective-permute-start.16) | collective-permute-done | bytes 27680 | tf_op jit(solution)/shard_map/ppermute | solution.py:298
  92.1 1.1 %collective-permute-done.15.tz = f32[27,4,128]{2,1,0:T(4,128)S(1)} collective-permute-done((f32[27,4,128]{2,1,0:T(4,128)S(1)}, f32[27,4,128]{2,1,0:T(4,128)S(1)}, u32[]{:S(2)}, u32[]{:S(2)}) %collective-permute-start.15) | collective-permute-done | bytes 55328 | tf_op jit(solution)/shard_map/ppermute | solution.py:298
  93.2 0.7 last.1
  (7 shorter events, 0.0 us)
Async XLA Ops:
  0.6 0.9 copy-start
  1.6 28.2 %collective-permute-start = (f32[54,4,128]{2,1,0:T(4,128)S(1)}, f32[54,4,128]{2,1,0:T(4,128)S(1)}, u32[]{:S(2)}, u32[]{:S(2)}) collective-permute-start(f32[54,4,128]{2,1,0:T(4,128)S(1)} %get-tuple-element.42), channel_id=1, source_target_pairs={{0,15},{1,0},{2,1},{3,2},{4,3},{5,4},{6,5},{7,6},{8,7},{9,8},{10,9... | collective-permute-start | bytes 331784 | tf_op jit(solution)/shard_map/ppermute | solution.py:298
  10.0 17.6 %collective-permute-start.1 = (f32[54,2,128]{2,1,0:T(2,128)S(1)}, f32[54,2,128]{2,1,0:T(2,128)S(1)}, u32[]{:S(2)}, u32[]{:S(2)}) collective-permute-start(f32[54,2,128]{2,1,0:T(2,128)S(1)} %get-tuple-element.43), channel_id=1, source_target_pairs={{0,176},{16,0},{32,16},{48,32},{64,48},{80,64},{96,80},{112,96},{1... | collective-permute-start | bytes 165896 | tf_op jit(solution)/shard_map/ppermute | solution.py:298
  24.3 5.5 %collective-permute-start.2 = (f32[54,2,128]{2,1,0:T(2,128)S(1)}, f32[54,2,128]{2,1,0:T(2,128)S(1)}, u32[]{:S(2)}, u32[]{:S(2)}) collective-permute-start(f32[54,2,128]{2,1,0:T(2,128)S(1)} %get-tuple-element.44), channel_id=1, source_target_pairs={{0,576},{192,0},{384,192},{576,384},{1,577},{193,1},{385,193},{577... | collective-permute-start | bytes 165896 | tf_op jit(solution)/shard_map/ppermute | solution.py:298
  30.4 9.3 %collective-permute-start.3 = (f32[27,4,128]{2,1,0:T(4,128)S(1)}, f32[27,4,128]{2,1,0:T(4,128)S(1)}, u32[]{:S(2)}, u32[]{:S(2)}) collective-permute-start(f32[27,4,128]{2,1,0:T(4,128)S(1)} %get-tuple-element.49), channel_id=1, source_target_pairs={{0,1},{1,2},{2,3},{3,4},{4,5},{5,6},{6,7},{7,8},{8,9},{9,10},{10,1... | collective-permute-start | bytes 165896 | tf_op jit(solution)/shard_map/ppermute | solution.py:298
  32.3 6.3 %collective-permute-start.4 = (f32[27,2,128]{2,1,0:T(2,128)S(1)}, f32[27,2,128]{2,1,0:T(2,128)S(1)}, u32[]{:S(2)}, u32[]{:S(2)}) collective-permute-start(f32[27,2,128]{2,1,0:T(2,128)S(1)} %get-tuple-element.50), channel_id=1, source_target_pairs={{0,16},{16,32},{32,48},{48,64},{64,80},{80,96},{96,112},{112,128},... | collective-permute-start | bytes 82952 | tf_op jit(solution)/shard_map/ppermute | solution.py:298
  34.2 4.4 %collective-permute-start.5 = (f32[27,2,128]{2,1,0:T(2,128)S(1)}, f32[27,2,128]{2,1,0:T(2,128)S(1)}, u32[]{:S(2)}, u32[]{:S(2)}) collective-permute-start(f32[27,2,128]{2,1,0:T(2,128)S(1)} %get-tuple-element.51), channel_id=1, source_target_pairs={{0,192},{192,384},{384,576},{576,0},{1,193},{193,385},{385,577},{5... | collective-permute-start | bytes 82952 | tf_op jit(solution)/shard_map/ppermute | solution.py:298
  36.2 3.5 %copy-start.2 = (f32[4,3,3,2,2,2,1,128]{7,6,5,4,3,2,1,0:T(1,128)S(1)}, f32[4,3,3,2,2,2,1,128]{7,6,5,4,3,2,1,0:T(1,128)}, u32[]{:S(2)}) copy-start(f32[4,3,3,2,2,2,1,128]{7,6,5,4,3,2,1,0:T(1,128)} %param.3) | copy-start | bytes 442372
  40.0 16.2 %collective-permute-start.6 = (f32[54,4,128]{2,1,0:T(4,128)S(1)}, f32[54,4,128]{2,1,0:T(4,128)S(1)}, u32[]{:S(2)}, u32[]{:S(2)}) collective-permute-start(f32[54,4,128]{2,1,0:T(4,128)S(1)} %get-tuple-element.56), channel_id=1, source_target_pairs={{0,15},{1,0},{2,1},{3,2},{4,3},{5,4},{6,5},{7,6},{8,7},{9,8},{10,9... | collective-permute-start | bytes 331784 | tf_op jit(solution)/shard_map/ppermute | solution.py:298
  45.9 8.3 %collective-permute-start.7 = (f32[54,2,128]{2,1,0:T(2,128)S(1)}, f32[54,2,128]{2,1,0:T(2,128)S(1)}, u32[]{:S(2)}, u32[]{:S(2)}) collective-permute-start(f32[54,2,128]{2,1,0:T(2,128)S(1)} %get-tuple-element.57), channel_id=1, source_target_pairs={{0,176},{16,0},{32,16},{48,32},{64,48},{80,64},{96,80},{112,96},{1... | collective-permute-start | bytes 165896 | tf_op jit(solution)/shard_map/ppermute | solution.py:298
  50.2 6.0 %collective-permute-start.8 = (f32[54,2,128]{2,1,0:T(2,128)S(1)}, f32[54,2,128]{2,1,0:T(2,128)S(1)}, u32[]{:S(2)}, u32[]{:S(2)}) collective-permute-start(f32[54,2,128]{2,1,0:T(2,128)S(1)} %get-tuple-element.58), channel_id=1, source_target_pairs={{0,576},{192,0},{384,192},{576,384},{1,577},{193,1},{385,193},{577... | collective-permute-start | bytes 165896 | tf_op jit(solution)/shard_map/ppermute | solution.py:298
  56.8 9.4 %collective-permute-start.9 = (f32[27,4,128]{2,1,0:T(4,128)S(1)}, f32[27,4,128]{2,1,0:T(4,128)S(1)}, u32[]{:S(2)}, u32[]{:S(2)}) collective-permute-start(f32[27,4,128]{2,1,0:T(4,128)S(1)} %get-tuple-element.63), channel_id=1, source_target_pairs={{0,1},{1,2},{2,3},{3,4},{4,5},{5,6},{6,7},{7,8},{8,9},{9,10},{10,1... | collective-permute-start | bytes 165896 | tf_op jit(solution)/shard_map/ppermute | solution.py:298
  58.7 6.4 %collective-permute-start.10 = (f32[27,2,128]{2,1,0:T(2,128)S(1)}, f32[27,2,128]{2,1,0:T(2,128)S(1)}, u32[]{:S(2)}, u32[]{:S(2)}) collective-permute-start(f32[27,2,128]{2,1,0:T(2,128)S(1)} %get-tuple-element.64), channel_id=1, source_target_pairs={{0,16},{16,32},{32,48},{48,64},{64,80},{80,96},{96,112},{112,128},... | collective-permute-start | bytes 82952 | tf_op jit(solution)/shard_map/ppermute | solution.py:298
  60.7 4.5 %collective-permute-start.11 = (f32[27,2,128]{2,1,0:T(2,128)S(1)}, f32[27,2,128]{2,1,0:T(2,128)S(1)}, u32[]{:S(2)}, u32[]{:S(2)}) collective-permute-start(f32[27,2,128]{2,1,0:T(2,128)S(1)} %get-tuple-element.65), channel_id=1, source_target_pairs={{0,192},{192,384},{384,576},{576,0},{1,193},{193,385},{385,577},{5... | collective-permute-start | bytes 82952 | tf_op jit(solution)/shard_map/ppermute | solution.py:298
  67.2 16.1 %collective-permute-start.12 = (f32[54,4,128]{2,1,0:T(4,128)S(1)}, f32[54,4,128]{2,1,0:T(4,128)S(1)}, u32[]{:S(2)}, u32[]{:S(2)}) collective-permute-start(f32[54,4,128]{2,1,0:T(4,128)S(1)} %get-tuple-element.70), channel_id=1, source_target_pairs={{0,15},{1,0},{2,1},{3,2},{4,3},{5,4},{6,5},{7,6},{8,7},{9,8},{10,9... | collective-permute-start | bytes 331784 | tf_op jit(solution)/shard_map/ppermute | solution.py:298
  72.6 9.6 %collective-permute-start.13 = (f32[54,2,128]{2,1,0:T(2,128)S(1)}, f32[54,2,128]{2,1,0:T(2,128)S(1)}, u32[]{:S(2)}, u32[]{:S(2)}) collective-permute-start(f32[54,2,128]{2,1,0:T(2,128)S(1)} %get-tuple-element.71), channel_id=1, source_target_pairs={{0,176},{16,0},{32,16},{48,32},{64,48},{80,64},{96,80},{112,96},{1... | collective-permute-start | bytes 165896 | tf_op jit(solution)/shard_map/ppermute | solution.py:298
  77.3 6.0 %collective-permute-start.14 = (f32[54,2,128]{2,1,0:T(2,128)S(1)}, f32[54,2,128]{2,1,0:T(2,128)S(1)}, u32[]{:S(2)}, u32[]{:S(2)}) collective-permute-start(f32[54,2,128]{2,1,0:T(2,128)S(1)} %get-tuple-element.72), channel_id=1, source_target_pairs={{0,576},{192,0},{384,192},{576,384},{1,577},{193,1},{385,193},{577... | collective-permute-start | bytes 165896 | tf_op jit(solution)/shard_map/ppermute | solution.py:298
  81.1 0.9 copy-start.1
  83.9 9.3 %collective-permute-start.15 = (f32[27,4,128]{2,1,0:T(4,128)S(1)}, f32[27,4,128]{2,1,0:T(4,128)S(1)}, u32[]{:S(2)}, u32[]{:S(2)}) collective-permute-start(f32[27,4,128]{2,1,0:T(4,128)S(1)} %get-tuple-element.77), channel_id=1, source_target_pairs={{0,1},{1,2},{2,3},{3,4},{4,5},{5,6},{6,7},{7,8},{8,9},{9,10},{10,1... | collective-permute-start | bytes 165896 | tf_op jit(solution)/shard_map/ppermute | solution.py:298
  85.8 6.3 %collective-permute-start.16 = (f32[27,2,128]{2,1,0:T(2,128)S(1)}, f32[27,2,128]{2,1,0:T(2,128)S(1)}, u32[]{:S(2)}, u32[]{:S(2)}) collective-permute-start(f32[27,2,128]{2,1,0:T(2,128)S(1)} %get-tuple-element.78), channel_id=1, source_target_pairs={{0,16},{16,32},{32,48},{48,64},{64,80},{80,96},{96,112},{112,128},... | collective-permute-start | bytes 82952 | tf_op jit(solution)/shard_map/ppermute | solution.py:298
  87.7 4.4 %collective-permute-start.17 = (f32[27,2,128]{2,1,0:T(2,128)S(1)}, f32[27,2,128]{2,1,0:T(2,128)S(1)}, u32[]{:S(2)}, u32[]{:S(2)}) collective-permute-start(f32[27,2,128]{2,1,0:T(2,128)S(1)} %get-tuple-element.79), channel_id=1, source_target_pairs={{0,192},{192,384},{384,576},{576,0},{1,193},{193,385},{385,577},{5... | collective-permute-start | bytes 82952 | tf_op jit(solution)/shard_map/ppermute | solution.py:298

commit v2 on v1

--- a/solution.py
+++ b/solution.py
@@ -7,6 +7,7 @@
 from jax.experimental.pallas import tpu as pltpu
 from jax.sharding import PartitionSpec as P
 
+
 BETA = 5.7
 STEP = 0.25
 F32 = jnp.float32
@@ -14,6 +15,7 @@
 OTHERS = ((1, 2, 3), (0, 2, 3), (0, 1, 3))
 PLANES = ((0, 1), (0, 2), (0, 3), (1, 2), (1, 3), (2, 3))
 PAIRS = ((0, 1), (0, 2), (1, 2))
+INNER = ((1, 2), (2, 1), (1, 3), (3, 1), (2, 3), (3, 2))
 
 
 def mat(ref, base):
@@ -25,10 +27,6 @@
         for j in range(3):
             ref[base + 6 * i + 2 * j] = m[i][j][0]
             ref[base + 6 * i + 2 * j + 1] = m[i][j][1]
-
-
-def dag(m):
-    return [[(m[j][i][0], -m[j][i][1]) for j in range(3)] for i in range(3)]
 
 
 def total(terms):
@@ -106,10 +104,13 @@
     return jnp.concatenate([halo[0:1], own[0:1], halo[1:2], own[2:3]], axis=0)
 
 
-def faces(u_ref, mz, my, mx):
+def face_z(u_ref, mz):
     for n, d in enumerate(OTHERS[2]):
         for c in range(18):
             mz[18 * n + c] = u_ref[18 * d + c]
+
+
+def faces(u_ref, my, mx):
     for n, d in enumerate(OTHERS[1]):
         for c in range(18):
             my[18 * n + c, 0:1] = u_ref[18 * d + c, 0:1]
@@ -119,39 +120,62 @@
             mx[18 * n + c] = u_ref[18 * d + c, 0:2]
 
 
-def first_kernel(u_ref, mz, my, mx):
-    faces(u_ref, mz, my, mx)
-
-
-def local_kernel(u_ref, r_ref):
+def first_kernel(u_ref, my, mx):
+    faces(u_ref, my, mx)
+
+
+def local_kernel(u_ref, r_ref, copy_ref=None):
+    if copy_ref is not None:
+        copy_ref[...] = u_ref[...]
     for n, (mu, nu) in enumerate(PLANES):
         put(r_ref, 18 * n, mul(mat(u_ref, 18 * mu), mat(u_ref, 18 * nu), da=True))
 
 
-def lower_kernel(u_ref, r_ref, rz, ry, rx, tz, ty, tx, sx, sy, st, own_x, own_y, own_t):
-    for n, d in enumerate(OTHERS[0]):
-        for c in range(18):
-            sx[18 * n + c] = step_x(u_ref[18 * d + c], rx[18 * n + c])
+def reader(sx, sy, rz, st):
+    def at(direction, axis):
+        ref = (sx, sy, rz, st)[axis]
+        where = direction if axis == 3 or ref.shape[0] == 72 else OTHERS[axis].index(direction)
+        return mat(ref, 18 * where)
+
+    return at
+
+
+def lower_terms(planes, at, r_ref, out):
+    for mu, nu in planes:
+        q = mul(at(mu, nu), at(nu, mu), db=True)
+        r = mat(r_ref, 18 * PLANES.index((mu, nu)))
+        for along, across, d in ((mu, nu, False), (nu, mu, True)):
+            for c, v in enumerate(anti(q, r, da=d, db=d)):
+                out(along, across, c, v)
+
+
+def lower_yzt_kernel(u_ref, r_ref, rz, ry, sy, st, part):
     for n, d in enumerate(OTHERS[1]):
         for c in range(18):
             sy[18 * n + c] = step_y(u_ref[18 * d + c], ry[18 * n + c])
     for d in range(3):
         for c in range(18):
             st[18 * d + c] = pltpu.roll(u_ref[18 * d + c], 127, 1)
-    moved = (sx, sy, rz, st)
-
-    def at(direction, axis):
-        where = OTHERS[axis].index(direction) if axis < 3 else direction
-        return mat(moved[axis], 18 * where)
-
-    lows = (own_x, own_y, tz, own_t)
-    for n, (mu, nu) in enumerate(PLANES):
-        q = mul(at(mu, nu), at(nu, mu), db=True)
-        r = mat(r_ref, 18 * n)
-        for along, across, d in ((mu, nu, False), (nu, mu, True)):
-            where = OTHERS[across].index(along) if across < 3 else along
-            for c, v in enumerate(anti(q, r, da=d, db=d)):
-                lows[across][9 * where + c] = v
+
+    def out(along, across, c, v):
+        part[9 * INNER.index((along, across)) + c] = v
+
+    lower_terms(PLANES[3:], reader(None, sy, rz, st), r_ref, out)
+
+
+def lower_x_kernel(u_ref, r_ref, rz, rx, sy, st, part, tz, ty, tx, sx, own_x, own_y, own_t):
+    for n, d in enumerate(OTHERS[0]):
+        for c in range(18):
+            sx[18 * n + c] = step_x(u_ref[18 * d + c], rx[18 * n + c])
+
+    def out(along, across, c, v):
+        where = OTHERS[across].index(along) if across < 3 else along
+        (own_x, own_y, tz, own_t)[across][9 * where + c] = v
+
+    for n, (along, across) in enumerate(INNER):
+        for c in range(9):
+            out(along, across, c, part[9 * n + c])
+    lower_terms(PLANES[:3], reader(sx, sy, rz, st), r_ref, out)
     for k in range(27):
         ty[k, 0:1] = own_y[k, 1:2]
         ty[k, 1:2] = own_y[k, 3:4]
@@ -159,12 +183,7 @@
 
 
 def upper_kernel(u_ref, rz, sx, sy, st, own_t, f_ref):
-    moved = (sx, sy, rz, st)
-
-    def at(direction, axis):
-        where = OTHERS[axis].index(direction) if axis < 3 else direction
-        return mat(moved[axis], 18 * where)
-
+    at = reader(sx, sy, rz, st)
     for k in range(27):
         f_ref[k] = pltpu.roll(own_t[k], 1, 1)
     for k in range(9):
@@ -260,7 +279,8 @@
         for c in range(9):
             q_ref[9 * d + c] = p[c]
         put(v_ref, 18 * d, mul(exponent([STEP * a for a in p]), mat(u_ref, 18 * d)))
-    faces(v_ref, mz, my, mx)
+    face_z(v_ref, mz)
+    faces(v_ref, my, mx)
 
 
 def last_kernel(factor, p_ref, f_ref, tz, ty, tx, own_x, own_y, q_ref):
@@ -275,7 +295,7 @@
                 q_ref[18 * d + 6 * i + 2 * j + 1] = m[i][j][1]
 
 
-def call(kernel, outs, name, products):
+def call(kernel, outs, products):
     vm = pl.BlockSpec(memory_space=pltpu.VMEM)
 
     def run(*args):
@@ -285,7 +305,6 @@
             out_shape=[jax.ShapeDtypeStruct((o[0], o[1], 128), F32) for o in outs],
             in_specs=[vm] * len(args),
             out_specs=[vm] * len(outs),
-            name=name,
             cost_estimate=pl.CostEstimate(flops=products * 200 * 512, bytes_accessed=4 * size, transcendentals=0),
             compiler_params=pltpu.CompilerParams(vmem_limit_bytes=8 * 1024 * 1024),
         )(*args)
@@ -299,7 +318,10 @@
 
 
 def exchange(z, y, x, steps):
-    return shifted(z, "gz", steps), shifted(y, "gy", steps), shifted(x, "gx", steps)
+    z = shifted(z, "gz", steps)
+    y = shifted(y, "gy", steps)
+    x = shifted(x, "gx", steps)
+    return z, y, x
 
 
 FACES = ((54, 4), (54, 2), (54, 2))
@@ -308,27 +330,28 @@
 def body(gauge_links, momenta):
     u = gauge_links.reshape(72, 4, 128)
     p = momenta.reshape(72, 4, 128)
-    sent = call(first_kernel, FACES, "first", 1)(u)
+    sent = (u, *call(first_kernel, FACES[1:], 1)(u))
     for repeat in range(3):
         rz, ry, rx = exchange(*sent, -1)
-        r = call(local_kernel, ((108, 4),), "local", 6)(u)[0]
-        tz, ty, tx, sx, sy, st, own_x, own_y, own_t = call(
-            lower_kernel,
-            ((27, 4), (27, 2), (27, 2), (54, 4), (54, 4), (54, 4), (27, 4), (27, 4), (27, 4)),
-            "lower",
-            18,
-        )(u, r, rz, ry, rx)
+        if repeat < 2:
+            r = call(local_kernel, ((108, 4),), 6)(u)[0]
+        else:
+            r, new_links = call(local_kernel, ((108, 4), (72, 4)), 6)(u)
+        sy, st, part = call(lower_yzt_kernel, ((54, 4), (54, 4), (54, 4)), 9)(u, r, rz, ry)
+        tz, ty, tx, sx, own_x, own_y, own_t = call(
+            lower_x_kernel, ((27, 4), (27, 2), (27, 2), (54, 4), (27, 4), (27, 4), (27, 4)), 9
+        )(u, r, rz, rx, sy, st, part)
         gz, gy, gx = exchange(tz, ty, tx, 1)
-        f = call(upper_kernel, ((36, 4),), "upper", 18)(u, rz, sx, sy, st, own_t)[0]
+        f = call(upper_kernel, ((36, 4),), 18)(u, rz, sx, sy, st, own_t)[0]
         factor = STEP if repeat == 1 else 0.5 * STEP
         if repeat < 2:
             p, u, *sent = call(
-                functools.partial(drift_kernel, factor, repeat == 0), ((36, 4), (72, 4)) + FACES, "drift", 16
+                functools.partial(drift_kernel, factor, repeat == 0), ((36, 4), (72, 4)) + FACES, 16
             )(u, p, f, gz, gy, gx, own_x, own_y)
         else:
-            p = call(functools.partial(last_kernel, factor), ((72, 4),), "last", 2)(p, f, gz, gy, gx, own_x, own_y)[0]
+            p = call(functools.partial(last_kernel, factor), ((72, 4),), 2)(p, f, gz, gy, gx, own_x, own_y)[0]
     shape = gauge_links.shape
-    return u.reshape(shape), p.reshape(shape)
+    return new_links.reshape(shape), p.reshape(shape)
 
 
 def solution(mesh):

time: 94.5 us -> 92.9 us (0.983)
    pallas_call x13 -> x16, Pallas kernels: 5.96 us -> 5.91 us  [run(): pl.pallas_call(kernel, out_shape=[jax.ShapeDtypeStruct((o[0], o[1], 128),...]
  transfers between devices with their start and end apart: 18 -> 18, of which waited for: 9 -> 9; matrix products, arithmetic and copies ran while one was open for 0% -> 0% of each run, Pallas kernels for 2% -> 4%
where the time goes in v2:
time: 92.9 us; the launch traced here: 92.3 us
  starting transfers between devices  70.9 us (76%)
  waiting for transfers between devices  13.7 us (15%)
  Pallas kernels  5.91 us (6%)
    ppermute x18, starting transfers between devices, shifted(): lax.ppermute(value, axis, [(source, (source + steps) % count) for source...  70.9 us
    ppermute x18, waiting for transfers between devices, shifted(): lax.ppermute(value, axis, [(source, (source + steps) % count) for source...  13.7 us
    pallas_call x16, Pallas kernels, run(): pl.pallas_call(kernel, out_shape=[jax.ShapeDtypeStruct((o[0], o[1], 128),...  5.91 us
  transfers between devices with their start and end apart: 18, of which 9 were waited for; matrix products, arithmetic and copies ran while one was open for 0% of the time, Pallas kernels for 4%

profile of v2, /device:TPU:1, one launch (start us, length us, event | category | flops | bytes accessed | tf_op | source)
XLA Modules:
  0.0 92.3 jit_solution(15158307516569778285)
XLA Ops:
  0.6 8.4 %collective-permute-start = (f32[72,4,128]{2,1,0:T(4,128)}, f32[72,4,128]{2,1,0:T(4,128)S(1)}, u32[]{:S(2)}, u32[]{:S(2)}) collective-permute-start(f32[72,4,128]{2,1,0:T(4,128)} %bitcast.8), channel_id=1, source_target_pairs={{0,15},{1,0},{2,1},{3,2},{4,3},{5,4},{6,5},{7,6},{8,7},{9,8},{10,9... | collective-permute-start | bytes 442376 | tf_op jit(solution)/shard_map/ppermute | solution.py:317
  9.0 0.9 copy-done
  9.9 0.1 shard_map.42
  10.0 14.3 %collective-permute-start.2 = (f32[54,2,128]{2,1,0:T(2,128)S(1)}, f32[54,2,128]{2,1,0:T(2,128)S(1)}, u32[]{:S(2)}, u32[]{:S(2)}) collective-permute-start(f32[54,2,128]{2,1,0:T(2,128)S(1)} %get-tuple-element.47), channel_id=1, source_target_pairs={{0,176},{16,0},{32,16},{48,32},{64,48},{80,64},{96,80},{112,96},{1... | collective-permute-start | bytes 165896 | tf_op jit(solution)/shard_map/ppermute | solution.py:317
  24.3 3.1 %collective-permute-start.1 = (f32[54,2,128]{2,1,0:T(2,128)S(1)}, f32[54,2,128]{2,1,0:T(2,128)S(1)}, u32[]{:S(2)}, u32[]{:S(2)}) collective-permute-start(f32[54,2,128]{2,1,0:T(2,128)S(1)} %get-tuple-element.46), channel_id=1, source_target_pairs={{0,576},{192,0},{384,192},{576,384},{1,577},{193,1},{385,193},{577... | collective-permute-start | bytes 165896 | tf_op jit(solution)/shard_map/ppermute | solution.py:317
  27.5 0.2 shard_map.41.r_ref
  27.6 0.3 shard_map.43
  28.0 1.8 %collective-permute-done.1.rx = f32[54,2,128]{2,1,0:T(2,128)S(1)} collective-permute-done((f32[54,2,128]{2,1,0:T(2,128)S(1)}, f32[54,2,128]{2,1,0:T(2,128)S(1)}, u32[]{:S(2)}, u32[]{:S(2)}) %collective-permute-start.1) | collective-permute-done | bytes 55328 | tf_op jit(solution)/shard_map/ppermute | solution.py:317
  29.8 0.3 shard_map.44
  30.1 1.9 %collective-permute-start.3 = (f32[27,4,128]{2,1,0:T(4,128)S(1)}, f32[27,4,128]{2,1,0:T(4,128)S(1)}, u32[]{:S(2)}, u32[]{:S(2)}) collective-permute-start(f32[27,4,128]{2,1,0:T(4,128)S(1)} %get-tuple-element.53), channel_id=1, source_target_pairs={{0,1},{1,2},{2,3},{3,4},{4,5},{5,6},{6,7},{7,8},{8,9},{9,10},{10,1... | collective-permute-start | bytes 165896 | tf_op jit(solution)/shard_map/ppermute | solution.py:317
  32.0 1.9 %collective-permute-start.4 = (f32[27,2,128]{2,1,0:T(2,128)S(1)}, f32[27,2,128]{2,1,0:T(2,128)S(1)}, u32[]{:S(2)}, u32[]{:S(2)}) collective-permute-start(f32[27,2,128]{2,1,0:T(2,128)S(1)} %get-tuple-element.54), channel_id=1, source_target_pairs={{0,16},{16,32},{32,48},{48,64},{64,80},{80,96},{96,112},{112,128},... | collective-permute-start | bytes 82952 | tf_op jit(solution)/shard_map/ppermute | solution.py:317
  33.9 1.9 %collective-permute-start.5 = (f32[27,2,128]{2,1,0:T(2,128)S(1)}, f32[27,2,128]{2,1,0:T(2,128)S(1)}, u32[]{:S(2)}, u32[]{:S(2)}) collective-permute-start(f32[27,2,128]{2,1,0:T(2,128)S(1)} %get-tuple-element.55), channel_id=1, source_target_pairs={{0,192},{192,384},{384,576},{576,0},{1,193},{193,385},{385,577},{5... | collective-permute-start | bytes 82952 | tf_op jit(solution)/shard_map/ppermute | solution.py:317
  35.9 0.0 copy-start.1
  35.9 0.5 shard_map.45.f_ref
  36.4 2.0 %collective-permute-done.4.ty = f32[27,2,128]{2,1,0:T(2,128)S(1)} collective-permute-done((f32[27,2,128]{2,1,0:T(2,128)S(1)}, f32[27,2,128]{2,1,0:T(2,128)S(1)}, u32[]{:S(2)}, u32[]{:S(2)}) %collective-permute-start.4) | collective-permute-done | bytes 27680 | tf_op jit(solution)/shard_map/ppermute | solution.py:317
  38.3 0.0 collective-permute-done.5.tx
  38.3 1.0 %collective-permute-done.3.tz = f32[27,4,128]{2,1,0:T(4,128)S(1)} collective-permute-done((f32[27,4,128]{2,1,0:T(4,128)S(1)}, f32[27,4,128]{2,1,0:T(4,128)S(1)}, u32[]{:S(2)}, u32[]{:S(2)}) %collective-permute-start.3) | collective-permute-done | bytes 55328 | tf_op jit(solution)/shard_map/ppermute | solution.py:317
  39.3 0.4 shard_map.46
  39.7 5.8 %collective-permute-start.6 = (f32[54,4,128]{2,1,0:T(4,128)S(1)}, f32[54,4,128]{2,1,0:T(4,128)S(1)}, u32[]{:S(2)}, u32[]{:S(2)}) collective-permute-start(f32[54,4,128]{2,1,0:T(4,128)S(1)} %get-tuple-element.60), channel_id=1, source_target_pairs={{0,15},{1,0},{2,1},{3,2},{4,3},{5,4},{6,5},{7,6},{8,7},{9,8},{10,9... | collective-permute-start | bytes 331784 | tf_op jit(solution)/shard_map/ppermute | solution.py:317
  45.6 4.3 %collective-permute-start.8 = (f32[54,2,128]{2,1,0:T(2,128)S(1)}, f32[54,2,128]{2,1,0:T(2,128)S(1)}, u32[]{:S(2)}, u32[]{:S(2)}) collective-permute-start(f32[54,2,128]{2,1,0:T(2,128)S(1)} %get-tuple-element.62), channel_id=1, source_target_pairs={{0,176},{16,0},{32,16},{48,32},{64,48},{80,64},{96,80},{112,96},{1... | collective-permute-start | bytes 165896 | tf_op jit(solution)/shard_map/ppermute | solution.py:317
  49.9 3.8 %collective-permute-start.7 = (f32[54,2,128]{2,1,0:T(2,128)S(1)}, f32[54,2,128]{2,1,0:T(2,128)S(1)}, u32[]{:S(2)}, u32[]{:S(2)}) collective-permute-start(f32[54,2,128]{2,1,0:T(2,128)S(1)} %get-tuple-element.61), channel_id=1, source_target_pairs={{0,576},{192,0},{384,192},{576,384},{1,577},{193,1},{385,193},{577... | collective-permute-start | bytes 165896 | tf_op jit(solution)/shard_map/ppermute | solution.py:317
  53.6 0.2 shard_map.47.r_ref
  53.8 0.3 shard_map.48
  54.2 1.7 %collective-permute-done.7.rx = f32[54,2,128]{2,1,0:T(2,128)S(1)} collective-permute-done((f32[54,2,128]{2,1,0:T(2,128)S(1)}, f32[54,2,128]{2,1,0:T(2,128)S(1)}, u32[]{:S(2)}, u32[]{:S(2)}) %collective-permute-start.7) | collective-permute-done | bytes 55328 | tf_op jit(solution)/shard_map/ppermute | solution.py:317
  55.9 0.3 shard_map.49
  56.2 1.9 %collective-permute-start.9 = (f32[27,4,128]{2,1,0:T(4,128)S(1)}, f32[27,4,128]{2,1,0:T(4,128)S(1)}, u32[]{:S(2)}, u32[]{:S(2)}) collective-permute-start(f32[27,4,128]{2,1,0:T(4,128)S(1)} %get-tuple-element.68), channel_id=1, source_target_pairs={{0,1},{1,2},{2,3},{3,4},{4,5},{5,6},{6,7},{7,8},{8,9},{9,10},{10,1... | collective-permute-start | bytes 165896 | tf_op jit(solution)/shard_map/ppermute | solution.py:317
  58.1 1.9 %collective-permute-start.10 = (f32[27,2,128]{2,1,0:T(2,128)S(1)}, f32[27,2,128]{2,1,0:T(2,128)S(1)}, u32[]{:S(2)}, u32[]{:S(2)}) collective-permute-start(f32[27,2,128]{2,1,0:T(2,128)S(1)} %get-tuple-element.69), channel_id=1, source_target_pairs={{0,16},{16,32},{32,48},{48,64},{64,80},{80,96},{96,112},{112,128},... | collective-permute-start | bytes 82952 | tf_op jit(solution)/shard_map/ppermute | solution.py:317
  60.0 1.9 %collective-permute-start.11 = (f32[27,2,128]{2,1,0:T(2,128)S(1)}, f32[27,2,128]{2,1,0:T(2,128)S(1)}, u32[]{:S(2)}, u32[]{:S(2)}) collective-permute-start(f32[27,2,128]{2,1,0:T(2,128)S(1)} %get-tuple-element.70), channel_id=1, source_target_pairs={{0,192},{192,384},{384,576},{576,0},{1,193},{193,385},{385,577},{5... | collective-permute-start | bytes 82952 | tf_op jit(solution)/shard_map/ppermute | solution.py:317
  62.0 0.5 shard_map.50.f_ref
  62.4 2.0 %collective-permute-done.10.ty = f32[27,2,128]{2,1,0:T(2,128)S(1)} collective-permute-done((f32[27,2,128]{2,1,0:T(2,128)S(1)}, f32[27,2,128]{2,1,0:T(2,128)S(1)}, u32[]{:S(2)}, u32[]{:S(2)}) %collective-permute-start.10) | collective-permute-done | bytes 27680 | tf_op jit(solution)/shard_map/ppermute | solution.py:317
  64.5 0.0 collective-permute-done.11.tx
  64.5 1.1 %collective-permute-done.9.tz = f32[27,4,128]{2,1,0:T(4,128)S(1)} collective-permute-done((f32[27,4,128]{2,1,0:T(4,128)S(1)}, f32[27,4,128]{2,1,0:T(4,128)S(1)}, u32[]{:S(2)}, u32[]{:S(2)}) %collective-permute-start.9) | collective-permute-done | bytes 55328 | tf_op jit(solution)/shard_map/ppermute | solution.py:317
  65.5 0.4 shard_map.51
  65.9 5.3 %collective-permute-start.12 = (f32[54,4,128]{2,1,0:T(4,128)S(1)}, f32[54,4,128]{2,1,0:T(4,128)S(1)}, u32[]{:S(2)}, u32[]{:S(2)}) collective-permute-start(f32[54,4,128]{2,1,0:T(4,128)S(1)} %get-tuple-element.76), channel_id=1, source_target_pairs={{0,15},{1,0},{2,1},{3,2},{4,3},{5,4},{6,5},{7,6},{8,7},{9,8},{10,9... | collective-permute-start | bytes 331784 | tf_op jit(solution)/shard_map/ppermute | solution.py:317
  71.3 4.7 %collective-permute-start.14 = (f32[54,2,128]{2,1,0:T(2,128)S(1)}, f32[54,2,128]{2,1,0:T(2,128)S(1)}, u32[]{:S(2)}, u32[]{:S(2)}) collective-permute-start(f32[54,2,128]{2,1,0:T(2,128)S(1)} %get-tuple-element.79), channel_id=1, source_target_pairs={{0,176},{16,0},{32,16},{48,32},{64,48},{80,64},{96,80},{112,96},{1... | collective-permute-start | bytes 165896 | tf_op jit(solution)/shard_map/ppermute | solution.py:317
  76.0 3.8 %collective-permute-start.13 = (f32[54,2,128]{2,1,0:T(2,128)S(1)}, f32[54,2,128]{2,1,0:T(2,128)S(1)}, u32[]{:S(2)}, u32[]{:S(2)}) collective-permute-start(f32[54,2,128]{2,1,0:T(2,128)S(1)} %get-tuple-element.78), channel_id=1, source_target_pairs={{0,576},{192,0},{384,192},{576,384},{1,577},{193,1},{385,193},{577... | collective-permute-start | bytes 165896 | tf_op jit(solution)/shard_map/ppermute | solution.py:317
  79.8 0.7 shard_map.52
  80.5 0.3 shard_map.53
  80.9 1.1 %collective-permute-done.13.rx = f32[54,2,128]{2,1,0:T(2,128)S(1)} collective-permute-done((f32[54,2,128]{2,1,0:T(2,128)S(1)}, f32[54,2,128]{2,1,0:T(2,128)S(1)}, u32[]{:S(2)}, u32[]{:S(2)}) %collective-permute-start.13) | collective-permute-done | bytes 55328 | tf_op jit(solution)/shard_map/ppermute | solution.py:317
  82.0 0.3 shard_map.54
  82.3 1.9 %collective-permute-start.15 = (f32[27,4,128]{2,1,0:T(4,128)S(1)}, f32[27,4,128]{2,1,0:T(4,128)S(1)}, u32[]{:S(2)}, u32[]{:S(2)}) collective-permute-start(f32[27,4,128]{2,1,0:T(4,128)S(1)} %get-tuple-element.85), channel_id=1, source_target_pairs={{0,1},{1,2},{2,3},{3,4},{4,5},{5,6},{6,7},{7,8},{8,9},{9,10},{10,1... | collective-permute-start | bytes 165896 | tf_op jit(solution)/shard_map/ppermute | solution.py:317
  84.2 1.9 %collective-permute-start.16 = (f32[27,2,128]{2,1,0:T(2,128)S(1)}, f32[27,2,128]{2,1,0:T(2,128)S(1)}, u32[]{:S(2)}, u32[]{:S(2)}) collective-permute-start(f32[27,2,128]{2,1,0:T(2,128)S(1)} %get-tuple-element.86), channel_id=1, source_target_pairs={{0,16},{16,32},{32,48},{48,64},{64,80},{80,96},{96,112},{112,128},... | collective-permute-start | bytes 82952 | tf_op jit(solution)/shard_map/ppermute | solution.py:317
  86.1 1.9 %collective-permute-start.17 = (f32[27,2,128]{2,1,0:T(2,128)S(1)}, f32[27,2,128]{2,1,0:T(2,128)S(1)}, u32[]{:S(2)}, u32[]{:S(2)}) collective-permute-start(f32[27,2,128]{2,1,0:T(2,128)S(1)} %get-tuple-element.87), channel_id=1, source_target_pairs={{0,192},{192,384},{384,576},{576,0},{1,193},{193,385},{385,577},{5... | collective-permute-start | bytes 82952 | tf_op jit(solution)/shard_map/ppermute | solution.py:317
  88.1 0.5 shard_map.55.f_ref
  88.6 1.9 %collective-permute-done.16.ty = f32[27,2,128]{2,1,0:T(2,128)S(1)} collective-permute-done((f32[27,2,128]{2,1,0:T(2,128)S(1)}, f32[27,2,128]{2,1,0:T(2,128)S(1)}, u32[]{:S(2)}, u32[]{:S(2)}) %collective-permute-start.16) | collective-permute-done | bytes 27680 | tf_op jit(solution)/shard_map/ppermute | solution.py:317
  90.5 0.0 collective-permute-done.17.tx
  90.5 1.1 %collective-permute-done.15.tz = f32[27,4,128]{2,1,0:T(4,128)S(1)} collective-permute-done((f32[27,4,128]{2,1,0:T(4,128)S(1)}, f32[27,4,128]{2,1,0:T(4,128)S(1)}, u32[]{:S(2)}, u32[]{:S(2)}) %collective-permute-start.15) | collective-permute-done | bytes 55328 | tf_op jit(solution)/shard_map/ppermute | solution.py:317
  91.6 0.7 shard_map.56
  (8 shorter events, 0.0 us)
Async XLA Ops:
  0.6 27.0 %collective-permute-start = (f32[72,4,128]{2,1,0:T(4,128)}, f32[72,4,128]{2,1,0:T(4,128)S(1)}, u32[]{:S(2)}, u32[]{:S(2)}) collective-permute-start(f32[72,4,128]{2,1,0:T(4,128)} %bitcast.8), channel_id=1, source_target_pairs={{0,15},{1,0},{2,1},{3,2},{4,3},{5,4},{6,5},{7,6},{8,7},{9,8},{10,9... | collective-permute-start | bytes 442376 | tf_op jit(solution)/shard_map/ppermute | solution.py:317
  9.0 0.9 copy-start
  10.0 17.6 %collective-permute-start.2 = (f32[54,2,128]{2,1,0:T(2,128)S(1)}, f32[54,2,128]{2,1,0:T(2,128)S(1)}, u32[]{:S(2)}, u32[]{:S(2)}) collective-permute-start(f32[54,2,128]{2,1,0:T(2,128)S(1)} %get-tuple-element.47), channel_id=1, source_target_pairs={{0,176},{16,0},{32,16},{48,32},{64,48},{80,64},{96,80},{112,96},{1... | collective-permute-start | bytes 165896 | tf_op jit(solution)/shard_map/ppermute | solution.py:317
  24.3 5.5 %collective-permute-start.1 = (f32[54,2,128]{2,1,0:T(2,128)S(1)}, f32[54,2,128]{2,1,0:T(2,128)S(1)}, u32[]{:S(2)}, u32[]{:S(2)}) collective-permute-start(f32[54,2,128]{2,1,0:T(2,128)S(1)} %get-tuple-element.46), channel_id=1, source_target_pairs={{0,576},{192,0},{384,192},{576,384},{1,577},{193,1},{385,193},{577... | collective-permute-start | bytes 165896 | tf_op jit(solution)/shard_map/ppermute | solution.py:317
  30.1 9.3 %collective-permute-start.3 = (f32[27,4,128]{2,1,0:T(4,128)S(1)}, f32[27,4,128]{2,1,0:T(4,128)S(1)}, u32[]{:S(2)}, u32[]{:S(2)}) collective-permute-start(f32[27,4,128]{2,1,0:T(4,128)S(1)} %get-tuple-element.53), channel_id=1, source_target_pairs={{0,1},{1,2},{2,3},{3,4},{4,5},{5,6},{6,7},{7,8},{8,9},{9,10},{10,1... | collective-permute-start | bytes 165896 | tf_op jit(solution)/shard_map/ppermute | solution.py:317
  32.0 6.3 %collective-permute-start.4 = (f32[27,2,128]{2,1,0:T(2,128)S(1)}, f32[27,2,128]{2,1,0:T(2,128)S(1)}, u32[]{:S(2)}, u32[]{:S(2)}) collective-permute-start(f32[27,2,128]{2,1,0:T(2,128)S(1)} %get-tuple-element.54), channel_id=1, source_target_pairs={{0,16},{16,32},{32,48},{48,64},{64,80},{80,96},{96,112},{112,128},... | collective-permute-start | bytes 82952 | tf_op jit(solution)/shard_map/ppermute | solution.py:317
  33.9 4.4 %collective-permute-start.5 = (f32[27,2,128]{2,1,0:T(2,128)S(1)}, f32[27,2,128]{2,1,0:T(2,128)S(1)}, u32[]{:S(2)}, u32[]{:S(2)}) collective-permute-start(f32[27,2,128]{2,1,0:T(2,128)S(1)} %get-tuple-element.55), channel_id=1, source_target_pairs={{0,192},{192,384},{384,576},{576,0},{1,193},{193,385},{385,577},{5... | collective-permute-start | bytes 82952 | tf_op jit(solution)/shard_map/ppermute | solution.py:317
  35.9 3.5 %copy-start.1 = (f32[4,3,3,2,2,2,1,128]{7,6,5,4,3,2,1,0:T(1,128)S(1)}, f32[4,3,3,2,2,2,1,128]{7,6,5,4,3,2,1,0:T(1,128)}, u32[]{:S(2)}) copy-start(f32[4,3,3,2,2,2,1,128]{7,6,5,4,3,2,1,0:T(1,128)} %param.3) | copy-start | bytes 442372
  39.7 14.1 %collective-permute-start.6 = (f32[54,4,128]{2,1,0:T(4,128)S(1)}, f32[54,4,128]{2,1,0:T(4,128)S(1)}, u32[]{:S(2)}, u32[]{:S(2)}) collective-permute-start(f32[54,4,128]{2,1,0:T(4,128)S(1)} %get-tuple-element.60), channel_id=1, source_target_pairs={{0,15},{1,0},{2,1},{3,2},{4,3},{5,4},{6,5},{7,6},{8,7},{9,8},{10,9... | collective-permute-start | bytes 331784 | tf_op jit(solution)/shard_map/ppermute | solution.py:317
  45.6 8.3 %collective-permute-start.8 = (f32[54,2,128]{2,1,0:T(2,128)S(1)}, f32[54,2,128]{2,1,0:T(2,128)S(1)}, u32[]{:S(2)}, u32[]{:S(2)}) collective-permute-start(f32[54,2,128]{2,1,0:T(2,128)S(1)} %get-tuple-element.62), channel_id=1, source_target_pairs={{0,176},{16,0},{32,16},{48,32},{64,48},{80,64},{96,80},{112,96},{1... | collective-permute-start | bytes 165896 | tf_op jit(solution)/shard_map/ppermute | solution.py:317
  49.9 6.0 %collective-permute-start.7 = (f32[54,2,128]{2,1,0:T(2,128)S(1)}, f32[54,2,128]{2,1,0:T(2,128)S(1)}, u32[]{:S(2)}, u32[]{:S(2)}) collective-permute-start(f32[54,2,128]{2,1,0:T(2,128)S(1)} %get-tuple-element.61), channel_id=1, source_target_pairs={{0,576},{192,0},{384,192},{576,384},{1,577},{193,1},{385,193},{577... | collective-permute-start | bytes 165896 | tf_op jit(solution)/shard_map/ppermute | solution.py:317
  56.2 9.4 %collective-permute-start.9 = (f32[27,4,128]{2,1,0:T(4,128)S(1)}, f32[27,4,128]{2,1,0:T(4,128)S(1)}, u32[]{:S(2)}, u32[]{:S(2)}) collective-permute-start(f32[27,4,128]{2,1,0:T(4,128)S(1)} %get-tuple-element.68), channel_id=1, source_target_pairs={{0,1},{1,2},{2,3},{3,4},{4,5},{5,6},{6,7},{7,8},{8,9},{9,10},{10,1... | collective-permute-start | bytes 165896 | tf_op jit(solution)/shard_map/ppermute | solution.py:317
  58.1 6.4 %collective-permute-start.10 = (f32[27,2,128]{2,1,0:T(2,128)S(1)}, f32[27,2,128]{2,1,0:T(2,128)S(1)}, u32[]{:S(2)}, u32[]{:S(2)}) collective-permute-start(f32[27,2,128]{2,1,0:T(2,128)S(1)} %get-tuple-element.69), channel_id=1, source_target_pairs={{0,16},{16,32},{32,48},{48,64},{64,80},{80,96},{96,112},{112,128},... | collective-permute-start | bytes 82952 | tf_op jit(solution)/shard_map/ppermute | solution.py:317
  60.0 4.5 %collective-permute-start.11 = (f32[27,2,128]{2,1,0:T(2,128)S(1)}, f32[27,2,128]{2,1,0:T(2,128)S(1)}, u32[]{:S(2)}, u32[]{:S(2)}) collective-permute-start(f32[27,2,128]{2,1,0:T(2,128)S(1)} %get-tuple-element.70), channel_id=1, source_target_pairs={{0,192},{192,384},{384,576},{576,0},{1,193},{193,385},{385,577},{5... | collective-permute-start | bytes 82952 | tf_op jit(solution)/shard_map/ppermute | solution.py:317
  65.9 14.6 %collective-permute-start.12 = (f32[54,4,128]{2,1,0:T(4,128)S(1)}, f32[54,4,128]{2,1,0:T(4,128)S(1)}, u32[]{:S(2)}, u32[]{:S(2)}) collective-permute-start(f32[54,4,128]{2,1,0:T(4,128)S(1)} %get-tuple-element.76), channel_id=1, source_target_pairs={{0,15},{1,0},{2,1},{3,2},{4,3},{5,4},{6,5},{7,6},{8,7},{9,8},{10,9... | collective-permute-start | bytes 331784 | tf_op jit(solution)/shard_map/ppermute | solution.py:317
  71.3 9.2 %collective-permute-start.14 = (f32[54,2,128]{2,1,0:T(2,128)S(1)}, f32[54,2,128]{2,1,0:T(2,128)S(1)}, u32[]{:S(2)}, u32[]{:S(2)}) collective-permute-start(f32[54,2,128]{2,1,0:T(2,128)S(1)} %get-tuple-element.79), channel_id=1, source_target_pairs={{0,176},{16,0},{32,16},{48,32},{64,48},{80,64},{96,80},{112,96},{1... | collective-permute-start | bytes 165896 | tf_op jit(solution)/shard_map/ppermute | solution.py:317
  76.0 6.0 %collective-permute-start.13 = (f32[54,2,128]{2,1,0:T(2,128)S(1)}, f32[54,2,128]{2,1,0:T(2,128)S(1)}, u32[]{:S(2)}, u32[]{:S(2)}) collective-permute-start(f32[54,2,128]{2,1,0:T(2,128)S(1)} %get-tuple-element.78), channel_id=1, source_target_pairs={{0,576},{192,0},{384,192},{576,384},{1,577},{193,1},{385,193},{577... | collective-permute-start | bytes 165896 | tf_op jit(solution)/shard_map/ppermute | solution.py:317
  82.3 9.3 %collective-permute-start.15 = (f32[27,4,128]{2,1,0:T(4,128)S(1)}, f32[27,4,128]{2,1,0:T(4,128)S(1)}, u32[]{:S(2)}, u32[]{:S(2)}) collective-permute-start(f32[27,4,128]{2,1,0:T(4,128)S(1)} %get-tuple-element.85), channel_id=1, source_target_pairs={{0,1},{1,2},{2,3},{3,4},{4,5},{5,6},{6,7},{7,8},{8,9},{9,10},{10,1... | collective-permute-start | bytes 165896 | tf_op jit(solution)/shard_map/ppermute | solution.py:317
  84.2 6.3 %collective-permute-start.16 = (f32[27,2,128]{2,1,0:T(2,128)S(1)}, f32[27,2,128]{2,1,0:T(2,128)S(1)}, u32[]{:S(2)}, u32[]{:S(2)}) collective-permute-start(f32[27,2,128]{2,1,0:T(2,128)S(1)} %get-tuple-element.86), channel_id=1, source_target_pairs={{0,16},{16,32},{32,48},{48,64},{64,80},{80,96},{96,112},{112,128},... | collective-permute-start | bytes 82952 | tf_op jit(solution)/shard_map/ppermute | solution.py:317
  86.1 4.4 %collective-permute-start.17 = (f32[27,2,128]{2,1,0:T(2,128)S(1)}, f32[27,2,128]{2,1,0:T(2,128)S(1)}, u32[]{:S(2)}, u32[]{:S(2)}) collective-permute-start(f32[27,2,128]{2,1,0:T(2,128)S(1)} %get-tuple-element.87), channel_id=1, source_target_pairs={{0,192},{192,384},{384,576},{576,0},{1,193},{193,385},{385,577},{5... | collective-permute-start | bytes 82952 | tf_op jit(solution)/shard_map/ppermute | solution.py:317

commit v3 on v2

--- a/solution.py
+++ b/solution.py
@@ -96,12 +96,13 @@
     return jnp.concatenate([own[1:2], halo[0:1], own[3:4], halo[1:2]], axis=0)
 
 
-def back_x(own, halo):
-    return jnp.concatenate([halo, own[0:2]], axis=0)
-
-
-def back_y(own, halo):
-    return jnp.concatenate([halo[0:1], own[0:1], halo[1:2], own[2:3]], axis=0)
+def back_x(halo):
+    return jnp.concatenate([halo, jnp.zeros((2, 128), F32)], axis=0)
+
+
+def back_y(halo):
+    gap = jnp.zeros((1, 128), F32)
+    return jnp.concatenate([halo[0:1], gap, halo[1:2], gap], axis=0)
 
 
 def face_z(u_ref, mz):
@@ -120,8 +121,34 @@
             mx[18 * n + c] = u_ref[18 * d + c, 0:2]
 
 
-def first_kernel(u_ref, my, mx):
-    faces(u_ref, my, mx)
+def first_kernel(u_ref, my, mx, sems):
+    copies = [pltpu.make_async_copy(u_ref.at[18:72, 0:2], mx, sems.at[0])]
+    for n, (source, size, to) in enumerate(((0, 18, 0), (36, 36, 18))):
+        for row in range(2):
+            copies.append(
+                pltpu.make_async_copy(
+                    u_ref.at[source : source + size, 2 * row], my.at[to : to + size, row], sems.at[1 + 2 * n + row]
+                )
+            )
+    for copy in copies:
+        copy.start()
+    for copy in copies:
+        copy.wait()
+
+
+def first_faces(u):
+    shapes = [jax.ShapeDtypeStruct((54, 2, 1, 128), F32)] * 2
+    my, mx = pl.pallas_call(
+        first_kernel,
+        out_shape=shapes,
+        in_specs=[pl.BlockSpec(memory_space=pltpu.HBM)],
+        out_specs=[pl.BlockSpec(memory_space=pltpu.VMEM)] * 2,
+        scratch_shapes=[pltpu.SemaphoreType.DMA((5,))],
+        name="first",
+        cost_estimate=pl.CostEstimate(flops=0, bytes_accessed=4 * 54 * 512 * 2, transcendentals=0),
+        compiler_params=pltpu.CompilerParams(vmem_limit_bytes=8 * 1024 * 1024),
+    )(pltpu.with_memory_space_constraint(u.reshape(72, 4, 1, 128), pltpu.HBM))
+    return my.reshape(54, 2, 128), mx.reshape(54, 2, 128)
 
 
 def local_kernel(u_ref, r_ref, copy_ref=None):
@@ -182,7 +209,7 @@
         tx[k] = own_x[k, 2:4]
 
 
-def upper_kernel(u_ref, rz, sx, sy, st, own_t, f_ref):
+def upper_kernel(u_ref, rz, sx, sy, st, own_x, own_y, own_t, f_ref):
     at = reader(sx, sy, rz, st)
     for k in range(27):
         f_ref[k] = pltpu.roll(own_t[k], 1, 1)
@@ -194,18 +221,25 @@
         for c, v in enumerate(anti(first, second, db=True)):
             f_ref[9 * mu + c] = f_ref[9 * mu + c] + v
             f_ref[9 * nu + c] = f_ref[9 * nu + c] - v
-
-
-def force_of(d, f_ref, tz, ty, tx, own_x, own_y):
+    for n, d in enumerate(OTHERS[0]):
+        for c in range(9):
+            f_ref[9 * d + c, 2:4] = f_ref[9 * d + c, 2:4] + own_x[9 * n + c, 0:2]
+    for n, d in enumerate(OTHERS[1]):
+        for c in range(9):
+            f_ref[9 * d + c, 1:2] = f_ref[9 * d + c, 1:2] + own_y[9 * n + c, 0:1]
+            f_ref[9 * d + c, 3:4] = f_ref[9 * d + c, 3:4] + own_y[9 * n + c, 2:3]
+
+
+def force_of(d, f_ref, tz, ty, tx):
     out = []
     for c in range(9):
         v = f_ref[9 * d + c]
         if d != 0:
             k = 9 * OTHERS[0].index(d) + c
-            v = v + back_x(own_x[k], tx[k])
+            v = v + back_x(tx[k])
         if d != 1:
             k = 9 * OTHERS[1].index(d) + c
-            v = v + back_y(own_y[k], ty[k])
+            v = v + back_y(ty[k])
         if d != 2:
             k = 9 * OTHERS[2].index(d) + c
             v = v + tz[k]
@@ -272,9 +306,9 @@
     return e
 
 
-def drift_kernel(factor, full, u_ref, p_ref, f_ref, tz, ty, tx, own_x, own_y, q_ref, v_ref, mz, my, mx):
+def drift_kernel(factor, full, u_ref, p_ref, f_ref, tz, ty, tx, q_ref, v_ref, mz, my, mx):
     for d in range(4):
-        force = force_of(d, f_ref, tz, ty, tx, own_x, own_y)
+        force = force_of(d, f_ref, tz, ty, tx)
         p = [a - (factor * BETA / 3.0) * b for a, b in zip(read_momenta(p_ref, d, full), force)]
         for c in range(9):
             q_ref[9 * d + c] = p[c]
@@ -283,9 +317,10 @@
     faces(v_ref, my, mx)
 
 
-def last_kernel(factor, p_ref, f_ref, tz, ty, tx, own_x, own_y, q_ref):
+def last_kernel(factor, p_ref, f_ref, tz, ty, tx, q_out, q_ref, sems):
+    copies = []
     for d in range(4):
-        force = force_of(d, f_ref, tz, ty, tx, own_x, own_y)
+        force = force_of(d, f_ref, tz, ty, tx)
         p = [a - (factor * BETA / 3.0) * b for a, b in zip(read_momenta(p_ref, d, False), force)]
         m = expand(p)
         for i in range(3):
@@ -293,6 +328,24 @@
                 re = jnp.zeros((4, 128), F32) if m[i][j][0] is None else m[i][j][0]
                 q_ref[18 * d + 6 * i + 2 * j] = re
                 q_ref[18 * d + 6 * i + 2 * j + 1] = m[i][j][1]
+        part = pl.ds(18 * d, 18)
+        copies.append(pltpu.make_async_copy(q_ref.at[part], q_out.at[part], sems.at[d]))
+        copies[-1].start()
+    for copy in copies:
+        copy.wait()
+
+
+def last_momenta(factor, *args):
+    return pl.pallas_call(
+        functools.partial(last_kernel, factor),
+        out_shape=jax.ShapeDtypeStruct((72, 4, 128), F32),
+        in_specs=[pl.BlockSpec(memory_space=pltpu.VMEM)] * len(args),
+        out_specs=pl.BlockSpec(memory_space=pl.ANY),
+        scratch_shapes=[pltpu.VMEM((72, 4, 128), F32), pltpu.SemaphoreType.DMA((4,))],
+        name="last",
+        cost_estimate=pl.CostEstimate(flops=100000, bytes_accessed=4 * 72 * 512 * 3, transcendentals=0),
+        compiler_params=pltpu.CompilerParams(vmem_limit_bytes=8 * 1024 * 1024),
+    )(*args)
 
 
 def call(kernel, outs, products):
@@ -330,7 +383,7 @@
 def body(gauge_links, momenta):
     u = gauge_links.reshape(72, 4, 128)
     p = momenta.reshape(72, 4, 128)
-    sent = (u, *call(first_kernel, FACES[1:], 1)(u))
+    sent = (u, *first_faces(u))
     for repeat in range(3):
         rz, ry, rx = exchange(*sent, -1)
         if repeat < 2:
@@ -342,14 +395,14 @@
             lower_x_kernel, ((27, 4), (27, 2), (27, 2), (54, 4), (27, 4), (27, 4), (27, 4)), 9
         )(u, r, rz, rx, sy, st, part)
         gz, gy, gx = exchange(tz, ty, tx, 1)
-        f = call(upper_kernel, ((36, 4),), 18)(u, rz, sx, sy, st, own_t)[0]
+        f = call(upper_kernel, ((36, 4),), 18)(u, rz, sx, sy, st, own_x, own_y, own_t)[0]
         factor = STEP if repeat == 1 else 0.5 * STEP
         if repeat < 2:
             p, u, *sent = call(
                 functools.partial(drift_kernel, factor, repeat == 0), ((36, 4), (72, 4)) + FACES, 16
-            )(u, p, f, gz, gy, gx, own_x, own_y)
+            )(u, p, f, gz, gy, gx)
         else:
-            p = call(functools.partial(last_kernel, factor), ((72, 4),), 2)(p, f, gz, gy, gx, own_x, own_y)[0]
+            p = last_momenta(factor, p, f, gz, gy, gx)
     shape = gauge_links.shape
     return new_links.reshape(shape), p.reshape(shape)
 

time: 92.9 us -> 93 us (level)
    pallas_call x0 -> x2, Pallas kernels: none -> 1.6 us  [the longest x1 0.88 us: first_faces(): pl.pallas_call(first_kernel, out_shape=shapes, in_specs=[pl.BlockSpec(mem...]
    pallas_call x16 -> x14, Pallas kernels: 5.91 us -> 5.23 us  [run(): pl.pallas_call(kernel, out_shape=[jax.ShapeDtypeStruct((o[0], o[1], 128),...]
  transfers between devices with their start and end apart: 18 -> 18, of which waited for: 9 -> 9; matrix products, arithmetic and copies ran while one was open for 0% -> 0% of each run, Pallas kernels for 4% -> 5%
where the time goes in v3:
time: 93 us; the launch traced here: 92.3 us
  starting transfers between devices  71 us (76%)
  waiting for transfers between devices  13.6 us (15%)
  Pallas kernels  6.83 us (7%)
    ppermute x18, starting transfers between devices, shifted(): lax.ppermute(value, axis, [(source, (source + steps) % count) for source...  71 us
    ppermute x18, waiting for transfers between devices, shifted(): lax.ppermute(value, axis, [(source, (source + steps) % count) for source...  13.6 us
    pallas_call x14, Pallas kernels, run(): pl.pallas_call(kernel, out_shape=[jax.ShapeDtypeStruct((o[0], o[1], 128),...  5.23 us
  transfers between devices with their start and end apart: 18, of which 9 were waited for; matrix products, arithmetic and copies ran while one was open for 0% of the time, Pallas kernels for 5%

profile of v3, /device:TPU:1, one launch (start us, length us, event | category | flops | bytes accessed | tf_op | source)
XLA Modules:
  0.0 92.3 jit_solution(1470899492998738710)
XLA Ops:
  0.6 8.5 %collective-permute-start = (f32[72,4,128]{2,1,0:T(4,128)}, f32[72,4,128]{2,1,0:T(4,128)S(1)}, u32[]{:S(2)}, u32[]{:S(2)}) collective-permute-start(f32[72,4,128]{2,1,0:T(4,128)} %bitcast.11), channel_id=1, source_target_pairs={{0,15},{1,0},{2,1},{3,2},{4,3},{5,4},{6,5},{7,6},{8,7},{9,8},{10,9... | collective-permute-start | bytes 442376 | tf_op jit(solution)/shard_map/ppermute | solution.py:370
  9.2 0.9 first.1
  10.0 14.3 %collective-permute-start.2 = (f32[54,2,128]{2,1,0:T(2,128)S(1)}, f32[54,2,128]{2,1,0:T(2,128)S(1)}, u32[]{:S(2)}, u32[]{:S(2)}) collective-permute-start(f32[54,2,128]{2,1,0:T(2,128)S(1)} %bitcast.20), channel_id=1, source_target_pairs={{0,176},{16,0},{32,16},{48,32},{64,48},{80,64},{96,80},{112,96},{1... | collective-permute-start | bytes 165896 | tf_op jit(solution)/shard_map/ppermute | solution.py:370
  24.3 3.1 %collective-permute-start.1 = (f32[54,2,128]{2,1,0:T(2,128)S(1)}, f32[54,2,128]{2,1,0:T(2,128)S(1)}, u32[]{:S(2)}, u32[]{:S(2)}) collective-permute-start(f32[54,2,128]{2,1,0:T(2,128)S(1)} %bitcast.19), channel_id=1, source_target_pairs={{0,576},{192,0},{384,192},{576,384},{1,577},{193,1},{385,193},{577... | collective-permute-start | bytes 165896 | tf_op jit(solution)/shard_map/ppermute | solution.py:370
  27.5 0.2 shard_map.41.r_ref
  27.7 0.0 collective-permute-done.2.ry
  27.7 0.3 shard_map.42
  28.0 1.8 %collective-permute-done.1.rx = f32[54,2,128]{2,1,0:T(2,128)S(1)} collective-permute-done((f32[54,2,128]{2,1,0:T(2,128)S(1)}, f32[54,2,128]{2,1,0:T(2,128)S(1)}, u32[]{:S(2)}, u32[]{:S(2)}) %collective-permute-start.1) | collective-permute-done | bytes 55328 | tf_op jit(solution)/shard_map/ppermute | solution.py:370
  29.8 0.3 shard_map.43
  30.1 1.9 %collective-permute-start.3 = (f32[27,4,128]{2,1,0:T(4,128)S(1)}, f32[27,4,128]{2,1,0:T(4,128)S(1)}, u32[]{:S(2)}, u32[]{:S(2)}) collective-permute-start(f32[27,4,128]{2,1,0:T(4,128)S(1)} %get-tuple-element.55), channel_id=1, source_target_pairs={{0,1},{1,2},{2,3},{3,4},{4,5},{5,6},{6,7},{7,8},{8,9},{9,10},{10,1... | collective-permute-start | bytes 165896 | tf_op jit(solution)/shard_map/ppermute | solution.py:370
  32.0 1.9 %collective-permute-start.4 = (f32[27,2,128]{2,1,0:T(2,128)S(1)}, f32[27,2,128]{2,1,0:T(2,128)S(1)}, u32[]{:S(2)}, u32[]{:S(2)}) collective-permute-start(f32[27,2,128]{2,1,0:T(2,128)S(1)} %get-tuple-element.56), channel_id=1, source_target_pairs={{0,16},{16,32},{32,48},{48,64},{64,80},{80,96},{96,112},{112,128},... | collective-permute-start | bytes 82952 | tf_op jit(solution)/shard_map/ppermute | solution.py:370
  34.0 1.9 %collective-permute-start.5 = (f32[27,2,128]{2,1,0:T(2,128)S(1)}, f32[27,2,128]{2,1,0:T(2,128)S(1)}, u32[]{:S(2)}, u32[]{:S(2)}) collective-permute-start(f32[27,2,128]{2,1,0:T(2,128)S(1)} %get-tuple-element.57), channel_id=1, source_target_pairs={{0,192},{192,384},{384,576},{576,0},{1,193},{193,385},{385,577},{5... | collective-permute-start | bytes 82952 | tf_op jit(solution)/shard_map/ppermute | solution.py:370
  35.9 0.0 copy-start.1
  35.9 0.5 shard_map.44.f_ref
  36.4 1.9 %collective-permute-done.4.ty = f32[27,2,128]{2,1,0:T(2,128)S(1)} collective-permute-done((f32[27,2,128]{2,1,0:T(2,128)S(1)}, f32[27,2,128]{2,1,0:T(2,128)S(1)}, u32[]{:S(2)}, u32[]{:S(2)}) %collective-permute-start.4) | collective-permute-done | bytes 27680 | tf_op jit(solution)/shard_map/ppermute | solution.py:370
  38.4 1.0 %collective-permute-done.3.tz = f32[27,4,128]{2,1,0:T(4,128)S(1)} collective-permute-done((f32[27,4,128]{2,1,0:T(4,128)S(1)}, f32[27,4,128]{2,1,0:T(4,128)S(1)}, u32[]{:S(2)}, u32[]{:S(2)}) %collective-permute-start.3) | collective-permute-done | bytes 55328 | tf_op jit(solution)/shard_map/ppermute | solution.py:370
  39.4 0.4 shard_map.45
  39.8 5.8 %collective-permute-start.6 = (f32[54,4,128]{2,1,0:T(4,128)S(1)}, f32[54,4,128]{2,1,0:T(4,128)S(1)}, u32[]{:S(2)}, u32[]{:S(2)}) collective-permute-start(f32[54,4,128]{2,1,0:T(4,128)S(1)} %get-tuple-element.60), channel_id=1, source_target_pairs={{0,15},{1,0},{2,1},{3,2},{4,3},{5,4},{6,5},{7,6},{8,7},{9,8},{10,9... | collective-permute-start | bytes 331784 | tf_op jit(solution)/shard_map/ppermute | solution.py:370
  45.6 4.3 %collective-permute-start.8 = (f32[54,2,128]{2,1,0:T(2,128)S(1)}, f32[54,2,128]{2,1,0:T(2,128)S(1)}, u32[]{:S(2)}, u32[]{:S(2)}) collective-permute-start(f32[54,2,128]{2,1,0:T(2,128)S(1)} %get-tuple-element.62), channel_id=1, source_target_pairs={{0,176},{16,0},{32,16},{48,32},{64,48},{80,64},{96,80},{112,96},{1... | collective-permute-start | bytes 165896 | tf_op jit(solution)/shard_map/ppermute | solution.py:370
  49.9 3.8 %collective-permute-start.7 = (f32[54,2,128]{2,1,0:T(2,128)S(1)}, f32[54,2,128]{2,1,0:T(2,128)S(1)}, u32[]{:S(2)}, u32[]{:S(2)}) collective-permute-start(f32[54,2,128]{2,1,0:T(2,128)S(1)} %get-tuple-element.61), channel_id=1, source_target_pairs={{0,576},{192,0},{384,192},{576,384},{1,577},{193,1},{385,193},{577... | collective-permute-start | bytes 165896 | tf_op jit(solution)/shard_map/ppermute | solution.py:370
  53.7 0.2 shard_map.46.r_ref
  53.9 0.0 collective-permute-done.8.ry
  53.9 0.0 collective-permute-done.6.rz
  53.9 0.3 shard_map.47
  54.2 1.7 %collective-permute-done.7.rx = f32[54,2,128]{2,1,0:T(2,128)S(1)} collective-permute-done((f32[54,2,128]{2,1,0:T(2,128)S(1)}, f32[54,2,128]{2,1,0:T(2,128)S(1)}, u32[]{:S(2)}, u32[]{:S(2)}) %collective-permute-start.7) | collective-permute-done | bytes 55328 | tf_op jit(solution)/shard_map/ppermute | solution.py:370
  55.9 0.3 shard_map.48
  56.2 1.9 %collective-permute-start.9 = (f32[27,4,128]{2,1,0:T(4,128)S(1)}, f32[27,4,128]{2,1,0:T(4,128)S(1)}, u32[]{:S(2)}, u32[]{:S(2)}) collective-permute-start(f32[27,4,128]{2,1,0:T(4,128)S(1)} %get-tuple-element.70), channel_id=1, source_target_pairs={{0,1},{1,2},{2,3},{3,4},{4,5},{5,6},{6,7},{7,8},{8,9},{9,10},{10,1... | collective-permute-start | bytes 165896 | tf_op jit(solution)/shard_map/ppermute | solution.py:370
  58.1 1.9 %collective-permute-start.10 = (f32[27,2,128]{2,1,0:T(2,128)S(1)}, f32[27,2,128]{2,1,0:T(2,128)S(1)}, u32[]{:S(2)}, u32[]{:S(2)}) collective-permute-start(f32[27,2,128]{2,1,0:T(2,128)S(1)} %get-tuple-element.71), channel_id=1, source_target_pairs={{0,16},{16,32},{32,48},{48,64},{64,80},{80,96},{96,112},{112,128},... | collective-permute-start | bytes 82952 | tf_op jit(solution)/shard_map/ppermute | solution.py:370
  60.1 1.9 %collective-permute-start.11 = (f32[27,2,128]{2,1,0:T(2,128)S(1)}, f32[27,2,128]{2,1,0:T(2,128)S(1)}, u32[]{:S(2)}, u32[]{:S(2)}) collective-permute-start(f32[27,2,128]{2,1,0:T(2,128)S(1)} %get-tuple-element.72), channel_id=1, source_target_pairs={{0,192},{192,384},{384,576},{576,0},{1,193},{193,385},{385,577},{5... | collective-permute-start | bytes 82952 | tf_op jit(solution)/shard_map/ppermute | solution.py:370
  62.0 0.5 shard_map.49.f_ref
  62.5 2.0 %collective-permute-done.10.ty = f32[27,2,128]{2,1,0:T(2,128)S(1)} collective-permute-done((f32[27,2,128]{2,1,0:T(2,128)S(1)}, f32[27,2,128]{2,1,0:T(2,128)S(1)}, u32[]{:S(2)}, u32[]{:S(2)}) %collective-permute-start.10) | collective-permute-done | bytes 27680 | tf_op jit(solution)/shard_map/ppermute | solution.py:370
  64.5 0.0 collective-permute-done.11.tx
  64.5 1.1 %collective-permute-done.9.tz = f32[27,4,128]{2,1,0:T(4,128)S(1)} collective-permute-done((f32[27,4,128]{2,1,0:T(4,128)S(1)}, f32[27,4,128]{2,1,0:T(4,128)S(1)}, u32[]{:S(2)}, u32[]{:S(2)}) %collective-permute-start.9) | collective-permute-done | bytes 55328 | tf_op jit(solution)/shard_map/ppermute | solution.py:370
  65.6 0.4 shard_map.50
  66.0 5.3 %collective-permute-start.12 = (f32[54,4,128]{2,1,0:T(4,128)S(1)}, f32[54,4,128]{2,1,0:T(4,128)S(1)}, u32[]{:S(2)}, u32[]{:S(2)}) collective-permute-start(f32[54,4,128]{2,1,0:T(4,128)S(1)} %get-tuple-element.76), channel_id=1, source_target_pairs={{0,15},{1,0},{2,1},{3,2},{4,3},{5,4},{6,5},{7,6},{8,7},{9,8},{10,9... | collective-permute-start | bytes 331784 | tf_op jit(solution)/shard_map/ppermute | solution.py:370
  71.3 4.7 %collective-permute-start.14 = (f32[54,2,128]{2,1,0:T(2,128)S(1)}, f32[54,2,128]{2,1,0:T(2,128)S(1)}, u32[]{:S(2)}, u32[]{:S(2)}) collective-permute-start(f32[54,2,128]{2,1,0:T(2,128)S(1)} %get-tuple-element.79), channel_id=1, source_target_pairs={{0,176},{16,0},{32,16},{48,32},{64,48},{80,64},{96,80},{112,96},{1... | collective-permute-start | bytes 165896 | tf_op jit(solution)/shard_map/ppermute | solution.py:370
  76.0 3.8 %collective-permute-start.13 = (f32[54,2,128]{2,1,0:T(2,128)S(1)}, f32[54,2,128]{2,1,0:T(2,128)S(1)}, u32[]{:S(2)}, u32[]{:S(2)}) collective-permute-start(f32[54,2,128]{2,1,0:T(2,128)S(1)} %get-tuple-element.78), channel_id=1, source_target_pairs={{0,576},{192,0},{384,192},{576,384},{1,577},{193,1},{385,193},{577... | collective-permute-start | bytes 165896 | tf_op jit(solution)/shard_map/ppermute | solution.py:370
  79.9 0.7 shard_map.51
  80.6 0.3 shard_map.52
  80.9 1.1 %collective-permute-done.13.rx = f32[54,2,128]{2,1,0:T(2,128)S(1)} collective-permute-done((f32[54,2,128]{2,1,0:T(2,128)S(1)}, f32[54,2,128]{2,1,0:T(2,128)S(1)}, u32[]{:S(2)}, u32[]{:S(2)}) %collective-permute-start.13) | collective-permute-done | bytes 55328 | tf_op jit(solution)/shard_map/ppermute | solution.py:370
  82.0 0.3 shard_map.53
  82.3 1.9 %collective-permute-start.15 = (f32[27,4,128]{2,1,0:T(4,128)S(1)}, f32[27,4,128]{2,1,0:T(4,128)S(1)}, u32[]{:S(2)}, u32[]{:S(2)}) collective-permute-start(f32[27,4,128]{2,1,0:T(4,128)S(1)} %get-tuple-element.87), channel_id=1, source_target_pairs={{0,1},{1,2},{2,3},{3,4},{4,5},{5,6},{6,7},{7,8},{8,9},{9,10},{10,1... | collective-permute-start | bytes 165896 | tf_op jit(solution)/shard_map/ppermute | solution.py:370
  84.2 1.9 %collective-permute-start.16 = (f32[27,2,128]{2,1,0:T(2,128)S(1)}, f32[27,2,128]{2,1,0:T(2,128)S(1)}, u32[]{:S(2)}, u32[]{:S(2)}) collective-permute-start(f32[27,2,128]{2,1,0:T(2,128)S(1)} %get-tuple-element.88), channel_id=1, source_target_pairs={{0,16},{16,32},{32,48},{48,64},{64,80},{80,96},{96,112},{112,128},... | collective-permute-start | bytes 82952 | tf_op jit(solution)/shard_map/ppermute | solution.py:370
  86.2 1.9 %collective-permute-start.17 = (f32[27,2,128]{2,1,0:T(2,128)S(1)}, f32[27,2,128]{2,1,0:T(2,128)S(1)}, u32[]{:S(2)}, u32[]{:S(2)}) collective-permute-start(f32[27,2,128]{2,1,0:T(2,128)S(1)} %get-tuple-element.89), channel_id=1, source_target_pairs={{0,192},{192,384},{384,576},{576,0},{1,193},{193,385},{385,577},{5... | collective-permute-start | bytes 82952 | tf_op jit(solution)/shard_map/ppermute | solution.py:370
  88.1 0.5 shard_map.54.f_ref
  88.6 1.9 %collective-permute-done.16.ty = f32[27,2,128]{2,1,0:T(2,128)S(1)} collective-permute-done((f32[27,2,128]{2,1,0:T(2,128)S(1)}, f32[27,2,128]{2,1,0:T(2,128)S(1)}, u32[]{:S(2)}, u32[]{:S(2)}) %collective-permute-start.16) | collective-permute-done | bytes 27680 | tf_op jit(solution)/shard_map/ppermute | solution.py:370
  90.5 1.1 %collective-permute-done.15.tz = f32[27,4,128]{2,1,0:T(4,128)S(1)} collective-permute-done((f32[27,4,128]{2,1,0:T(4,128)S(1)}, f32[27,4,128]{2,1,0:T(4,128)S(1)}, u32[]{:S(2)}, u32[]{:S(2)}) %collective-permute-start.15) | collective-permute-done | bytes 55328 | tf_op jit(solution)/shard_map/ppermute | solution.py:370
  91.6 0.7 last.1
  (8 shorter events, 0.0 us)
Async XLA Ops:
  0.6 26.9 %copy-start = (f32[4,3,3,2,2,2,1,128]{7,6,5,4,3,2,1,0:T(1,128)S(1)}, f32[4,3,3,2,2,2,1,128]{7,6,5,4,3,2,1,0:T(1,128)}, u32[]{:S(2)}) copy-start(f32[4,3,3,2,2,2,1,128]{7,6,5,4,3,2,1,0:T(1,128)} %param.2) | copy-start | bytes 442372
  0.6 27.1 %collective-permute-start = (f32[72,4,128]{2,1,0:T(4,128)}, f32[72,4,128]{2,1,0:T(4,128)S(1)}, u32[]{:S(2)}, u32[]{:S(2)}) collective-permute-start(f32[72,4,128]{2,1,0:T(4,128)} %bitcast.11), channel_id=1, source_target_pairs={{0,15},{1,0},{2,1},{3,2},{4,3},{5,4},{6,5},{7,6},{8,7},{9,8},{10,9... | collective-permute-start | bytes 442376 | tf_op jit(solution)/shard_map/ppermute | solution.py:370
  10.0 17.6 %collective-permute-start.2 = (f32[54,2,128]{2,1,0:T(2,128)S(1)}, f32[54,2,128]{2,1,0:T(2,128)S(1)}, u32[]{:S(2)}, u32[]{:S(2)}) collective-permute-start(f32[54,2,128]{2,1,0:T(2,128)S(1)} %bitcast.20), channel_id=1, source_target_pairs={{0,176},{16,0},{32,16},{48,32},{64,48},{80,64},{96,80},{112,96},{1... | collective-permute-start | bytes 165896 | tf_op jit(solution)/shard_map/ppermute | solution.py:370
  24.3 5.5 %collective-permute-start.1 = (f32[54,2,128]{2,1,0:T(2,128)S(1)}, f32[54,2,128]{2,1,0:T(2,128)S(1)}, u32[]{:S(2)}, u32[]{:S(2)}) collective-permute-start(f32[54,2,128]{2,1,0:T(2,128)S(1)} %bitcast.19), channel_id=1, source_target_pairs={{0,576},{192,0},{384,192},{576,384},{1,577},{193,1},{385,193},{577... | collective-permute-start | bytes 165896 | tf_op jit(solution)/shard_map/ppermute | solution.py:370
  30.1 9.3 %collective-permute-start.3 = (f32[27,4,128]{2,1,0:T(4,128)S(1)}, f32[27,4,128]{2,1,0:T(4,128)S(1)}, u32[]{:S(2)}, u32[]{:S(2)}) collective-permute-start(f32[27,4,128]{2,1,0:T(4,128)S(1)} %get-tuple-element.55), channel_id=1, source_target_pairs={{0,1},{1,2},{2,3},{3,4},{4,5},{5,6},{6,7},{7,8},{8,9},{9,10},{10,1... | collective-permute-start | bytes 165896 | tf_op jit(solution)/shard_map/ppermute | solution.py:370
  32.0 6.3 %collective-permute-start.4 = (f32[27,2,128]{2,1,0:T(2,128)S(1)}, f32[27,2,128]{2,1,0:T(2,128)S(1)}, u32[]{:S(2)}, u32[]{:S(2)}) collective-permute-start(f32[27,2,128]{2,1,0:T(2,128)S(1)} %get-tuple-element.56), channel_id=1, source_target_pairs={{0,16},{16,32},{32,48},{48,64},{64,80},{80,96},{96,112},{112,128},... | collective-permute-start | bytes 82952 | tf_op jit(solution)/shard_map/ppermute | solution.py:370
  34.0 4.4 %collective-permute-start.5 = (f32[27,2,128]{2,1,0:T(2,128)S(1)}, f32[27,2,128]{2,1,0:T(2,128)S(1)}, u32[]{:S(2)}, u32[]{:S(2)}) collective-permute-start(f32[27,2,128]{2,1,0:T(2,128)S(1)} %get-tuple-element.57), channel_id=1, source_target_pairs={{0,192},{192,384},{384,576},{576,0},{1,193},{193,385},{385,577},{5... | collective-permute-start | bytes 82952 | tf_op jit(solution)/shard_map/ppermute | solution.py:370
  35.9 3.5 %copy-start.1 = (f32[4,3,3,2,2,2,1,128]{7,6,5,4,3,2,1,0:T(1,128)S(1)}, f32[4,3,3,2,2,2,1,128]{7,6,5,4,3,2,1,0:T(1,128)}, u32[]{:S(2)}) copy-start(f32[4,3,3,2,2,2,1,128]{7,6,5,4,3,2,1,0:T(1,128)} %param.3) | copy-start | bytes 442372
  39.8 14.1 %collective-permute-start.6 = (f32[54,4,128]{2,1,0:T(4,128)S(1)}, f32[54,4,128]{2,1,0:T(4,128)S(1)}, u32[]{:S(2)}, u32[]{:S(2)}) collective-permute-start(f32[54,4,128]{2,1,0:T(4,128)S(1)} %get-tuple-element.60), channel_id=1, source_target_pairs={{0,15},{1,0},{2,1},{3,2},{4,3},{5,4},{6,5},{7,6},{8,7},{9,8},{10,9... | collective-permute-start | bytes 331784 | tf_op jit(solution)/shard_map/ppermute | solution.py:370
  45.6 8.3 %collective-permute-start.8 = (f32[54,2,128]{2,1,0:T(2,128)S(1)}, f32[54,2,128]{2,1,0:T(2,128)S(1)}, u32[]{:S(2)}, u32[]{:S(2)}) collective-permute-start(f32[54,2,128]{2,1,0:T(2,128)S(1)} %get-tuple-element.62), channel_id=1, source_target_pairs={{0,176},{16,0},{32,16},{48,32},{64,48},{80,64},{96,80},{112,96},{1... | collective-permute-start | bytes 165896 | tf_op jit(solution)/shard_map/ppermute | solution.py:370
  49.9 6.0 %collective-permute-start.7 = (f32[54,2,128]{2,1,0:T(2,128)S(1)}, f32[54,2,128]{2,1,0:T(2,128)S(1)}, u32[]{:S(2)}, u32[]{:S(2)}) collective-permute-start(f32[54,2,128]{2,1,0:T(2,128)S(1)} %get-tuple-element.61), channel_id=1, source_target_pairs={{0,576},{192,0},{384,192},{576,384},{1,577},{193,1},{385,193},{577... | collective-permute-start | bytes 165896 | tf_op jit(solution)/shard_map/ppermute | solution.py:370
  56.2 9.4 %collective-permute-start.9 = (f32[27,4,128]{2,1,0:T(4,128)S(1)}, f32[27,4,128]{2,1,0:T(4,128)S(1)}, u32[]{:S(2)}, u32[]{:S(2)}) collective-permute-start(f32[27,4,128]{2,1,0:T(4,128)S(1)} %get-tuple-element.70), channel_id=1, source_target_pairs={{0,1},{1,2},{2,3},{3,4},{4,5},{5,6},{6,7},{7,8},{8,9},{9,10},{10,1... | collective-permute-start | bytes 165896 | tf_op jit(solution)/shard_map/ppermute | solution.py:370
  58.1 6.4 %collective-permute-start.10 = (f32[27,2,128]{2,1,0:T(2,128)S(1)}, f32[27,2,128]{2,1,0:T(2,128)S(1)}, u32[]{:S(2)}, u32[]{:S(2)}) collective-permute-start(f32[27,2,128]{2,1,0:T(2,128)S(1)} %get-tuple-element.71), channel_id=1, source_target_pairs={{0,16},{16,32},{32,48},{48,64},{64,80},{80,96},{96,112},{112,128},... | collective-permute-start | bytes 82952 | tf_op jit(solution)/shard_map/ppermute | solution.py:370
  60.1 4.5 %collective-permute-start.11 = (f32[27,2,128]{2,1,0:T(2,128)S(1)}, f32[27,2,128]{2,1,0:T(2,128)S(1)}, u32[]{:S(2)}, u32[]{:S(2)}) collective-permute-start(f32[27,2,128]{2,1,0:T(2,128)S(1)} %get-tuple-element.72), channel_id=1, source_target_pairs={{0,192},{192,384},{384,576},{576,0},{1,193},{193,385},{385,577},{5... | collective-permute-start | bytes 82952 | tf_op jit(solution)/shard_map/ppermute | solution.py:370
  66.0 14.6 %collective-permute-start.12 = (f32[54,4,128]{2,1,0:T(4,128)S(1)}, f32[54,4,128]{2,1,0:T(4,128)S(1)}, u32[]{:S(2)}, u32[]{:S(2)}) collective-permute-start(f32[54,4,128]{2,1,0:T(4,128)S(1)} %get-tuple-element.76), channel_id=1, source_target_pairs={{0,15},{1,0},{2,1},{3,2},{4,3},{5,4},{6,5},{7,6},{8,7},{9,8},{10,9... | collective-permute-start | bytes 331784 | tf_op jit(solution)/shard_map/ppermute | solution.py:370
  71.3 9.2 %collective-permute-start.14 = (f32[54,2,128]{2,1,0:T(2,128)S(1)}, f32[54,2,128]{2,1,0:T(2,128)S(1)}, u32[]{:S(2)}, u32[]{:S(2)}) collective-permute-start(f32[54,2,128]{2,1,0:T(2,128)S(1)} %get-tuple-element.79), channel_id=1, source_target_pairs={{0,176},{16,0},{32,16},{48,32},{64,48},{80,64},{96,80},{112,96},{1... | collective-permute-start | bytes 165896 | tf_op jit(solution)/shard_map/ppermute | solution.py:370
  76.0 6.0 %collective-permute-start.13 = (f32[54,2,128]{2,1,0:T(2,128)S(1)}, f32[54,2,128]{2,1,0:T(2,128)S(1)}, u32[]{:S(2)}, u32[]{:S(2)}) collective-permute-start(f32[54,2,128]{2,1,0:T(2,128)S(1)} %get-tuple-element.78), channel_id=1, source_target_pairs={{0,576},{192,0},{384,192},{576,384},{1,577},{193,1},{385,193},{577... | collective-permute-start | bytes 165896 | tf_op jit(solution)/shard_map/ppermute | solution.py:370
  82.3 9.3 %collective-permute-start.15 = (f32[27,4,128]{2,1,0:T(4,128)S(1)}, f32[27,4,128]{2,1,0:T(4,128)S(1)}, u32[]{:S(2)}, u32[]{:S(2)}) collective-permute-start(f32[27,4,128]{2,1,0:T(4,128)S(1)} %get-tuple-element.87), channel_id=1, source_target_pairs={{0,1},{1,2},{2,3},{3,4},{4,5},{5,6},{6,7},{7,8},{8,9},{9,10},{10,1... | collective-permute-start | bytes 165896 | tf_op jit(solution)/shard_map/ppermute | solution.py:370
  84.2 6.3 %collective-permute-start.16 = (f32[27,2,128]{2,1,0:T(2,128)S(1)}, f32[27,2,128]{2,1,0:T(2,128)S(1)}, u32[]{:S(2)}, u32[]{:S(2)}) collective-permute-start(f32[27,2,128]{2,1,0:T(2,128)S(1)} %get-tuple-element.88), channel_id=1, source_target_pairs={{0,16},{16,32},{32,48},{48,64},{64,80},{80,96},{96,112},{112,128},... | collective-permute-start | bytes 82952 | tf_op jit(solution)/shard_map/ppermute | solution.py:370
  86.2 4.4 %collective-permute-start.17 = (f32[27,2,128]{2,1,0:T(2,128)S(1)}, f32[27,2,128]{2,1,0:T(2,128)S(1)}, u32[]{:S(2)}, u32[]{:S(2)}) collective-permute-start(f32[27,2,128]{2,1,0:T(2,128)S(1)} %get-tuple-element.89), channel_id=1, source_target_pairs={{0,192},{192,384},{384,576},{576,0},{1,193},{193,385},{385,577},{5... | collective-permute-start | bytes 82952 | tf_op jit(solution)/shard_map/ppermute | solution.py:370

commit v4 on v2

--- a/solution.py
+++ b/solution.py
@@ -120,7 +120,23 @@
             mx[18 * n + c] = u_ref[18 * d + c, 0:2]
 
 
-def first_kernel(u_ref, my, mx):
+def marker_kernel(u_ref, out):
+    out[...] = jnp.zeros_like(out)
+
+
+def marker(u):
+    return pl.pallas_call(
+        marker_kernel,
+        out_shape=jax.ShapeDtypeStruct((8, 128), F32),
+        in_specs=[pl.BlockSpec(memory_space=pl.ANY)],
+        out_specs=pl.BlockSpec(memory_space=pltpu.VMEM),
+        name="marker",
+        cost_estimate=pl.CostEstimate(flops=4000000000, bytes_accessed=40000000, transcendentals=0),
+        compiler_params=pltpu.CompilerParams(vmem_limit_bytes=1024 * 1024),
+    )(pltpu.with_memory_space_constraint(u, pltpu.HBM))
+
+
+def first_kernel(u_ref, mark, my, mx):
     faces(u_ref, my, mx)
 
 
@@ -330,7 +346,8 @@
 def body(gauge_links, momenta):
     u = gauge_links.reshape(72, 4, 128)
     p = momenta.reshape(72, 4, 128)
-    sent = (u, *call(first_kernel, FACES[1:], 1)(u))
+    mark = marker(u)
+    sent = (u, *call(first_kernel, FACES[1:], 1)(u, mark.reshape(1, 8, 128)))
     for repeat in range(3):
         rz, ry, rx = exchange(*sent, -1)
         if repeat < 2:

time: 92.9 us -> 92.2 us (level)
  no operation moved by 1% of the time
where the time goes in v4:
time: 92.2 us; the launch traced here: 91.6 us
  starting transfers between devices  71 us (77%)
  waiting for transfers between devices  13.7 us (15%)
  Pallas kernels  5.91 us (6%)
    ppermute x18, starting transfers between devices, shifted(): lax.ppermute(value, axis, [(source, (source + steps) % count) for source...  71 us
    ppermute x18, waiting for transfers between devices, shifted(): lax.ppermute(value, axis, [(source, (source + steps) % count) for source...  13.7 us
    pallas_call x16, Pallas kernels, run(): pl.pallas_call(kernel, out_shape=[jax.ShapeDtypeStruct((o[0], o[1], 128),...  5.91 us
  transfers between devices with their start and end apart: 18, of which 9 were waited for; matrix products, arithmetic and copies ran while one was open for 0% of the time, Pallas kernels for 4%

profile of v4, /device:TPU:1, one launch (start us, length us, event | category | flops | bytes accessed | tf_op | source)
XLA Modules:
  0.0 91.6 jit_solution(7810271162077829301)
XLA Ops:
  0.6 8.5 %collective-permute-start = (f32[72,4,128]{2,1,0:T(4,128)}, f32[72,4,128]{2,1,0:T(4,128)S(1)}, u32[]{:S(2)}, u32[]{:S(2)}) collective-permute-start(f32[72,4,128]{2,1,0:T(4,128)} %bitcast.9), channel_id=1, source_target_pairs={{0,15},{1,0},{2,1},{3,2},{4,3},{5,4},{6,5},{7,6},{8,7},{9,8},{10,9... | collective-permute-start | bytes 442376 | tf_op jit(solution)/shard_map/ppermute | solution.py:333
  9.2 0.1 shard_map.42
  9.2 14.3 %collective-permute-start.2 = (f32[54,2,128]{2,1,0:T(2,128)S(1)}, f32[54,2,128]{2,1,0:T(2,128)S(1)}, u32[]{:S(2)}, u32[]{:S(2)}) collective-permute-start(f32[54,2,128]{2,1,0:T(2,128)S(1)} %get-tuple-element.47), channel_id=1, source_target_pairs={{0,176},{16,0},{32,16},{48,32},{64,48},{80,64},{96,80},{112,96},{1... | collective-permute-start | bytes 165896 | tf_op jit(solution)/shard_map/ppermute | solution.py:333
  23.6 3.1 %collective-permute-start.1 = (f32[54,2,128]{2,1,0:T(2,128)S(1)}, f32[54,2,128]{2,1,0:T(2,128)S(1)}, u32[]{:S(2)}, u32[]{:S(2)}) collective-permute-start(f32[54,2,128]{2,1,0:T(2,128)S(1)} %get-tuple-element.46), channel_id=1, source_target_pairs={{0,576},{192,0},{384,192},{576,384},{1,577},{193,1},{385,193},{577... | collective-permute-start | bytes 165896 | tf_op jit(solution)/shard_map/ppermute | solution.py:333
  26.7 0.2 shard_map.41.r_ref
  26.9 0.0 collective-permute-done.2.ry
  26.9 0.0 collective-permute-done.rz
  26.9 0.3 shard_map.43
  27.2 1.8 %collective-permute-done.1.rx = f32[54,2,128]{2,1,0:T(2,128)S(1)} collective-permute-done((f32[54,2,128]{2,1,0:T(2,128)S(1)}, f32[54,2,128]{2,1,0:T(2,128)S(1)}, u32[]{:S(2)}, u32[]{:S(2)}) %collective-permute-start.1) | collective-permute-done | bytes 55328 | tf_op jit(solution)/shard_map/ppermute | solution.py:333
  29.0 0.3 shard_map.44
  29.3 1.9 %collective-permute-start.3 = (f32[27,4,128]{2,1,0:T(4,128)S(1)}, f32[27,4,128]{2,1,0:T(4,128)S(1)}, u32[]{:S(2)}, u32[]{:S(2)}) collective-permute-start(f32[27,4,128]{2,1,0:T(4,128)S(1)} %get-tuple-element.53), channel_id=1, source_target_pairs={{0,1},{1,2},{2,3},{3,4},{4,5},{5,6},{6,7},{7,8},{8,9},{9,10},{10,1... | collective-permute-start | bytes 165896 | tf_op jit(solution)/shard_map/ppermute | solution.py:333
  31.2 1.9 %collective-permute-start.4 = (f32[27,2,128]{2,1,0:T(2,128)S(1)}, f32[27,2,128]{2,1,0:T(2,128)S(1)}, u32[]{:S(2)}, u32[]{:S(2)}) collective-permute-start(f32[27,2,128]{2,1,0:T(2,128)S(1)} %get-tuple-element.54), channel_id=1, source_target_pairs={{0,16},{16,32},{32,48},{48,64},{64,80},{80,96},{96,112},{112,128},... | collective-permute-start | bytes 82952 | tf_op jit(solution)/shard_map/ppermute | solution.py:333
  33.2 1.9 %collective-permute-start.5 = (f32[27,2,128]{2,1,0:T(2,128)S(1)}, f32[27,2,128]{2,1,0:T(2,128)S(1)}, u32[]{:S(2)}, u32[]{:S(2)}) collective-permute-start(f32[27,2,128]{2,1,0:T(2,128)S(1)} %get-tuple-element.55), channel_id=1, source_target_pairs={{0,192},{192,384},{384,576},{576,0},{1,193},{193,385},{385,577},{5... | collective-permute-start | bytes 82952 | tf_op jit(solution)/shard_map/ppermute | solution.py:333
  35.1 0.0 copy-start.1
  35.1 0.5 shard_map.45.f_ref
  35.6 2.0 %collective-permute-done.4.ty = f32[27,2,128]{2,1,0:T(2,128)S(1)} collective-permute-done((f32[27,2,128]{2,1,0:T(2,128)S(1)}, f32[27,2,128]{2,1,0:T(2,128)S(1)}, u32[]{:S(2)}, u32[]{:S(2)}) %collective-permute-start.4) | collective-permute-done | bytes 27680 | tf_op jit(solution)/shard_map/ppermute | solution.py:333
  37.6 0.0 collective-permute-done.5.tx
  37.6 1.0 %collective-permute-done.3.tz = f32[27,4,128]{2,1,0:T(4,128)S(1)} collective-permute-done((f32[27,4,128]{2,1,0:T(4,128)S(1)}, f32[27,4,128]{2,1,0:T(4,128)S(1)}, u32[]{:S(2)}, u32[]{:S(2)}) %collective-permute-start.3) | collective-permute-done | bytes 55328 | tf_op jit(solution)/shard_map/ppermute | solution.py:333
  38.6 0.4 shard_map.46
  39.0 5.8 %collective-permute-start.6 = (f32[54,4,128]{2,1,0:T(4,128)S(1)}, f32[54,4,128]{2,1,0:T(4,128)S(1)}, u32[]{:S(2)}, u32[]{:S(2)}) collective-permute-start(f32[54,4,128]{2,1,0:T(4,128)S(1)} %get-tuple-element.60), channel_id=1, source_target_pairs={{0,15},{1,0},{2,1},{3,2},{4,3},{5,4},{6,5},{7,6},{8,7},{9,8},{10,9... | collective-permute-start | bytes 331784 | tf_op jit(solution)/shard_map/ppermute | solution.py:333
  44.8 4.3 %collective-permute-start.8 = (f32[54,2,128]{2,1,0:T(2,128)S(1)}, f32[54,2,128]{2,1,0:T(2,128)S(1)}, u32[]{:S(2)}, u32[]{:S(2)}) collective-permute-start(f32[54,2,128]{2,1,0:T(2,128)S(1)} %get-tuple-element.62), channel_id=1, source_target_pairs={{0,176},{16,0},{32,16},{48,32},{64,48},{80,64},{96,80},{112,96},{1... | collective-permute-start | bytes 165896 | tf_op jit(solution)/shard_map/ppermute | solution.py:333
  49.1 3.8 %collective-permute-start.7 = (f32[54,2,128]{2,1,0:T(2,128)S(1)}, f32[54,2,128]{2,1,0:T(2,128)S(1)}, u32[]{:S(2)}, u32[]{:S(2)}) collective-permute-start(f32[54,2,128]{2,1,0:T(2,128)S(1)} %get-tuple-element.61), channel_id=1, source_target_pairs={{0,576},{192,0},{384,192},{576,384},{1,577},{193,1},{385,193},{577... | collective-permute-start | bytes 165896 | tf_op jit(solution)/shard_map/ppermute | solution.py:333
  52.9 0.2 shard_map.47.r_ref
  53.1 0.0 collective-permute-done.8.ry
  53.1 0.3 shard_map.48
  53.4 1.7 %collective-permute-done.7.rx = f32[54,2,128]{2,1,0:T(2,128)S(1)} collective-permute-done((f32[54,2,128]{2,1,0:T(2,128)S(1)}, f32[54,2,128]{2,1,0:T(2,128)S(1)}, u32[]{:S(2)}, u32[]{:S(2)}) %collective-permute-start.7) | collective-permute-done | bytes 55328 | tf_op jit(solution)/shard_map/ppermute | solution.py:333
  55.1 0.3 shard_map.49
  55.4 1.9 %collective-permute-start.9 = (f32[27,4,128]{2,1,0:T(4,128)S(1)}, f32[27,4,128]{2,1,0:T(4,128)S(1)}, u32[]{:S(2)}, u32[]{:S(2)}) collective-permute-start(f32[27,4,128]{2,1,0:T(4,128)S(1)} %get-tuple-element.68), channel_id=1, source_target_pairs={{0,1},{1,2},{2,3},{3,4},{4,5},{5,6},{6,7},{7,8},{8,9},{9,10},{10,1... | collective-permute-start | bytes 165896 | tf_op jit(solution)/shard_map/ppermute | solution.py:333
  57.3 1.9 %collective-permute-start.10 = (f32[27,2,128]{2,1,0:T(2,128)S(1)}, f32[27,2,128]{2,1,0:T(2,128)S(1)}, u32[]{:S(2)}, u32[]{:S(2)}) collective-permute-start(f32[27,2,128]{2,1,0:T(2,128)S(1)} %get-tuple-element.69), channel_id=1, source_target_pairs={{0,16},{16,32},{32,48},{48,64},{64,80},{80,96},{96,112},{112,128},... | collective-permute-start | bytes 82952 | tf_op jit(solution)/shard_map/ppermute | solution.py:333
  59.3 1.9 %collective-permute-start.11 = (f32[27,2,128]{2,1,0:T(2,128)S(1)}, f32[27,2,128]{2,1,0:T(2,128)S(1)}, u32[]{:S(2)}, u32[]{:S(2)}) collective-permute-start(f32[27,2,128]{2,1,0:T(2,128)S(1)} %get-tuple-element.70), channel_id=1, source_target_pairs={{0,192},{192,384},{384,576},{576,0},{1,193},{193,385},{385,577},{5... | collective-permute-start | bytes 82952 | tf_op jit(solution)/shard_map/ppermute | solution.py:333
  61.2 0.5 shard_map.50.f_ref
  61.7 2.0 %collective-permute-done.10.ty = f32[27,2,128]{2,1,0:T(2,128)S(1)} collective-permute-done((f32[27,2,128]{2,1,0:T(2,128)S(1)}, f32[27,2,128]{2,1,0:T(2,128)S(1)}, u32[]{:S(2)}, u32[]{:S(2)}) %collective-permute-start.10) | collective-permute-done | bytes 27680 | tf_op jit(solution)/shard_map/ppermute | solution.py:333
  63.7 1.1 %collective-permute-done.9.tz = f32[27,4,128]{2,1,0:T(4,128)S(1)} collective-permute-done((f32[27,4,128]{2,1,0:T(4,128)S(1)}, f32[27,4,128]{2,1,0:T(4,128)S(1)}, u32[]{:S(2)}, u32[]{:S(2)}) %collective-permute-start.9) | collective-permute-done | bytes 55328 | tf_op jit(solution)/shard_map/ppermute | solution.py:333
  64.8 0.4 shard_map.51
  65.2 5.3 %collective-permute-start.12 = (f32[54,4,128]{2,1,0:T(4,128)S(1)}, f32[54,4,128]{2,1,0:T(4,128)S(1)}, u32[]{:S(2)}, u32[]{:S(2)}) collective-permute-start(f32[54,4,128]{2,1,0:T(4,128)S(1)} %get-tuple-element.76), channel_id=1, source_target_pairs={{0,15},{1,0},{2,1},{3,2},{4,3},{5,4},{6,5},{7,6},{8,7},{9,8},{10,9... | collective-permute-start | bytes 331784 | tf_op jit(solution)/shard_map/ppermute | solution.py:333
  70.5 4.7 %collective-permute-start.14 = (f32[54,2,128]{2,1,0:T(2,128)S(1)}, f32[54,2,128]{2,1,0:T(2,128)S(1)}, u32[]{:S(2)}, u32[]{:S(2)}) collective-permute-start(f32[54,2,128]{2,1,0:T(2,128)S(1)} %get-tuple-element.79), channel_id=1, source_target_pairs={{0,176},{16,0},{32,16},{48,32},{64,48},{80,64},{96,80},{112,96},{1... | collective-permute-start | bytes 165896 | tf_op jit(solution)/shard_map/ppermute | solution.py:333
  75.2 3.8 %collective-permute-start.13 = (f32[54,2,128]{2,1,0:T(2,128)S(1)}, f32[54,2,128]{2,1,0:T(2,128)S(1)}, u32[]{:S(2)}, u32[]{:S(2)}) collective-permute-start(f32[54,2,128]{2,1,0:T(2,128)S(1)} %get-tuple-element.78), channel_id=1, source_target_pairs={{0,576},{192,0},{384,192},{576,384},{1,577},{193,1},{385,193},{577... | collective-permute-start | bytes 165896 | tf_op jit(solution)/shard_map/ppermute | solution.py:333
  79.1 0.7 shard_map.52
  79.8 0.3 shard_map.53
  80.1 1.1 %collective-permute-done.13.rx = f32[54,2,128]{2,1,0:T(2,128)S(1)} collective-permute-done((f32[54,2,128]{2,1,0:T(2,128)S(1)}, f32[54,2,128]{2,1,0:T(2,128)S(1)}, u32[]{:S(2)}, u32[]{:S(2)}) %collective-permute-start.13) | collective-permute-done | bytes 55328 | tf_op jit(solution)/shard_map/ppermute | solution.py:333
  81.2 0.3 shard_map.54
  81.5 1.9 %collective-permute-start.15 = (f32[27,4,128]{2,1,0:T(4,128)S(1)}, f32[27,4,128]{2,1,0:T(4,128)S(1)}, u32[]{:S(2)}, u32[]{:S(2)}) collective-permute-start(f32[27,4,128]{2,1,0:T(4,128)S(1)} %get-tuple-element.85), channel_id=1, source_target_pairs={{0,1},{1,2},{2,3},{3,4},{4,5},{5,6},{6,7},{7,8},{8,9},{9,10},{10,1... | collective-permute-start | bytes 165896 | tf_op jit(solution)/shard_map/ppermute | solution.py:333
  83.5 1.9 %collective-permute-start.16 = (f32[27,2,128]{2,1,0:T(2,128)S(1)}, f32[27,2,128]{2,1,0:T(2,128)S(1)}, u32[]{:S(2)}, u32[]{:S(2)}) collective-permute-start(f32[27,2,128]{2,1,0:T(2,128)S(1)} %get-tuple-element.86), channel_id=1, source_target_pairs={{0,16},{16,32},{32,48},{48,64},{64,80},{80,96},{96,112},{112,128},... | collective-permute-start | bytes 82952 | tf_op jit(solution)/shard_map/ppermute | solution.py:333
  85.4 1.9 %collective-permute-start.17 = (f32[27,2,128]{2,1,0:T(2,128)S(1)}, f32[27,2,128]{2,1,0:T(2,128)S(1)}, u32[]{:S(2)}, u32[]{:S(2)}) collective-permute-start(f32[27,2,128]{2,1,0:T(2,128)S(1)} %get-tuple-element.87), channel_id=1, source_target_pairs={{0,192},{192,384},{384,576},{576,0},{1,193},{193,385},{385,577},{5... | collective-permute-start | bytes 82952 | tf_op jit(solution)/shard_map/ppermute | solution.py:333
  87.3 0.5 shard_map.55.f_ref
  87.8 1.9 %collective-permute-done.16.ty = f32[27,2,128]{2,1,0:T(2,128)S(1)} collective-permute-done((f32[27,2,128]{2,1,0:T(2,128)S(1)}, f32[27,2,128]{2,1,0:T(2,128)S(1)}, u32[]{:S(2)}, u32[]{:S(2)}) %collective-permute-start.16) | collective-permute-done | bytes 27680 | tf_op jit(solution)/shard_map/ppermute | solution.py:333
  89.8 1.1 %collective-permute-done.15.tz = f32[27,4,128]{2,1,0:T(4,128)S(1)} collective-permute-done((f32[27,4,128]{2,1,0:T(4,128)S(1)}, f32[27,4,128]{2,1,0:T(4,128)S(1)}, u32[]{:S(2)}, u32[]{:S(2)}) %collective-permute-start.15) | collective-permute-done | bytes 55328 | tf_op jit(solution)/shard_map/ppermute | solution.py:333
  90.8 0.7 shard_map.56
  (9 shorter events, 0.0 us)
Async XLA Ops:
  0.6 8.5 %copy-start = (f32[4,3,3,2,2,2,1,128]{7,6,5,4,3,2,1,0:T(1,128)S(1)}, f32[4,3,3,2,2,2,1,128]{7,6,5,4,3,2,1,0:T(1,128)}, u32[]{:S(2)}) copy-start(f32[4,3,3,2,2,2,1,128]{7,6,5,4,3,2,1,0:T(1,128)} %param.2) | copy-start | bytes 442372
  0.6 26.2 %collective-permute-start = (f32[72,4,128]{2,1,0:T(4,128)}, f32[72,4,128]{2,1,0:T(4,128)S(1)}, u32[]{:S(2)}, u32[]{:S(2)}) collective-permute-start(f32[72,4,128]{2,1,0:T(4,128)} %bitcast.9), channel_id=1, source_target_pairs={{0,15},{1,0},{2,1},{3,2},{4,3},{5,4},{6,5},{7,6},{8,7},{9,8},{10,9... | collective-permute-start | bytes 442376 | tf_op jit(solution)/shard_map/ppermute | solution.py:333
  9.2 17.6 %collective-permute-start.2 = (f32[54,2,128]{2,1,0:T(2,128)S(1)}, f32[54,2,128]{2,1,0:T(2,128)S(1)}, u32[]{:S(2)}, u32[]{:S(2)}) collective-permute-start(f32[54,2,128]{2,1,0:T(2,128)S(1)} %get-tuple-element.47), channel_id=1, source_target_pairs={{0,176},{16,0},{32,16},{48,32},{64,48},{80,64},{96,80},{112,96},{1... | collective-permute-start | bytes 165896 | tf_op jit(solution)/shard_map/ppermute | solution.py:333
  23.6 5.5 %collective-permute-start.1 = (f32[54,2,128]{2,1,0:T(2,128)S(1)}, f32[54,2,128]{2,1,0:T(2,128)S(1)}, u32[]{:S(2)}, u32[]{:S(2)}) collective-permute-start(f32[54,2,128]{2,1,0:T(2,128)S(1)} %get-tuple-element.46), channel_id=1, source_target_pairs={{0,576},{192,0},{384,192},{576,384},{1,577},{193,1},{385,193},{577... | collective-permute-start | bytes 165896 | tf_op jit(solution)/shard_map/ppermute | solution.py:333
  29.3 9.3 %collective-permute-start.3 = (f32[27,4,128]{2,1,0:T(4,128)S(1)}, f32[27,4,128]{2,1,0:T(4,128)S(1)}, u32[]{:S(2)}, u32[]{:S(2)}) collective-permute-start(f32[27,4,128]{2,1,0:T(4,128)S(1)} %get-tuple-element.53), channel_id=1, source_target_pairs={{0,1},{1,2},{2,3},{3,4},{4,5},{5,6},{6,7},{7,8},{8,9},{9,10},{10,1... | collective-permute-start | bytes 165896 | tf_op jit(solution)/shard_map/ppermute | solution.py:333
  31.2 6.3 %collective-permute-start.4 = (f32[27,2,128]{2,1,0:T(2,128)S(1)}, f32[27,2,128]{2,1,0:T(2,128)S(1)}, u32[]{:S(2)}, u32[]{:S(2)}) collective-permute-start(f32[27,2,128]{2,1,0:T(2,128)S(1)} %get-tuple-element.54), channel_id=1, source_target_pairs={{0,16},{16,32},{32,48},{48,64},{64,80},{80,96},{96,112},{112,128},... | collective-permute-start | bytes 82952 | tf_op jit(solution)/shard_map/ppermute | solution.py:333
  33.2 4.4 %collective-permute-start.5 = (f32[27,2,128]{2,1,0:T(2,128)S(1)}, f32[27,2,128]{2,1,0:T(2,128)S(1)}, u32[]{:S(2)}, u32[]{:S(2)}) collective-permute-start(f32[27,2,128]{2,1,0:T(2,128)S(1)} %get-tuple-element.55), channel_id=1, source_target_pairs={{0,192},{192,384},{384,576},{576,0},{1,193},{193,385},{385,577},{5... | collective-permute-start | bytes 82952 | tf_op jit(solution)/shard_map/ppermute | solution.py:333
  35.1 3.5 %copy-start.1 = (f32[4,3,3,2,2,2,1,128]{7,6,5,4,3,2,1,0:T(1,128)S(1)}, f32[4,3,3,2,2,2,1,128]{7,6,5,4,3,2,1,0:T(1,128)}, u32[]{:S(2)}) copy-start(f32[4,3,3,2,2,2,1,128]{7,6,5,4,3,2,1,0:T(1,128)} %param.3) | copy-start | bytes 442372
  39.0 14.1 %collective-permute-start.6 = (f32[54,4,128]{2,1,0:T(4,128)S(1)}, f32[54,4,128]{2,1,0:T(4,128)S(1)}, u32[]{:S(2)}, u32[]{:S(2)}) collective-permute-start(f32[54,4,128]{2,1,0:T(4,128)S(1)} %get-tuple-element.60), channel_id=1, source_target_pairs={{0,15},{1,0},{2,1},{3,2},{4,3},{5,4},{6,5},{7,6},{8,7},{9,8},{10,9... | collective-permute-start | bytes 331784 | tf_op jit(solution)/shard_map/ppermute | solution.py:333
  44.8 8.3 %collective-permute-start.8 = (f32[54,2,128]{2,1,0:T(2,128)S(1)}, f32[54,2,128]{2,1,0:T(2,128)S(1)}, u32[]{:S(2)}, u32[]{:S(2)}) collective-permute-start(f32[54,2,128]{2,1,0:T(2,128)S(1)} %get-tuple-element.62), channel_id=1, source_target_pairs={{0,176},{16,0},{32,16},{48,32},{64,48},{80,64},{96,80},{112,96},{1... | collective-permute-start | bytes 165896 | tf_op jit(solution)/shard_map/ppermute | solution.py:333
  49.1 6.0 %collective-permute-start.7 = (f32[54,2,128]{2,1,0:T(2,128)S(1)}, f32[54,2,128]{2,1,0:T(2,128)S(1)}, u32[]{:S(2)}, u32[]{:S(2)}) collective-permute-start(f32[54,2,128]{2,1,0:T(2,128)S(1)} %get-tuple-element.61), channel_id=1, source_target_pairs={{0,576},{192,0},{384,192},{576,384},{1,577},{193,1},{385,193},{577... | collective-permute-start | bytes 165896 | tf_op jit(solution)/shard_map/ppermute | solution.py:333
  55.4 9.4 %collective-permute-start.9 = (f32[27,4,128]{2,1,0:T(4,128)S(1)}, f32[27,4,128]{2,1,0:T(4,128)S(1)}, u32[]{:S(2)}, u32[]{:S(2)}) collective-permute-start(f32[27,4,128]{2,1,0:T(4,128)S(1)} %get-tuple-element.68), channel_id=1, source_target_pairs={{0,1},{1,2},{2,3},{3,4},{4,5},{5,6},{6,7},{7,8},{8,9},{9,10},{10,1... | collective-permute-start | bytes 165896 | tf_op jit(solution)/shard_map/ppermute | solution.py:333
  57.3 6.4 %collective-permute-start.10 = (f32[27,2,128]{2,1,0:T(2,128)S(1)}, f32[27,2,128]{2,1,0:T(2,128)S(1)}, u32[]{:S(2)}, u32[]{:S(2)}) collective-permute-start(f32[27,2,128]{2,1,0:T(2,128)S(1)} %get-tuple-element.69), channel_id=1, source_target_pairs={{0,16},{16,32},{32,48},{48,64},{64,80},{80,96},{96,112},{112,128},... | collective-permute-start | bytes 82952 | tf_op jit(solution)/shard_map/ppermute | solution.py:333
  59.3 4.5 %collective-permute-start.11 = (f32[27,2,128]{2,1,0:T(2,128)S(1)}, f32[27,2,128]{2,1,0:T(2,128)S(1)}, u32[]{:S(2)}, u32[]{:S(2)}) collective-permute-start(f32[27,2,128]{2,1,0:T(2,128)S(1)} %get-tuple-element.70), channel_id=1, source_target_pairs={{0,192},{192,384},{384,576},{576,0},{1,193},{193,385},{385,577},{5... | collective-permute-start | bytes 82952 | tf_op jit(solution)/shard_map/ppermute | solution.py:333
  65.2 14.6 %collective-permute-start.12 = (f32[54,4,128]{2,1,0:T(4,128)S(1)}, f32[54,4,128]{2,1,0:T(4,128)S(1)}, u32[]{:S(2)}, u32[]{:S(2)}) collective-permute-start(f32[54,4,128]{2,1,0:T(4,128)S(1)} %get-tuple-element.76), channel_id=1, source_target_pairs={{0,15},{1,0},{2,1},{3,2},{4,3},{5,4},{6,5},{7,6},{8,7},{9,8},{10,9... | collective-permute-start | bytes 331784 | tf_op jit(solution)/shard_map/ppermute | solution.py:333
  70.5 9.2 %collective-permute-start.14 = (f32[54,2,128]{2,1,0:T(2,128)S(1)}, f32[54,2,128]{2,1,0:T(2,128)S(1)}, u32[]{:S(2)}, u32[]{:S(2)}) collective-permute-start(f32[54,2,128]{2,1,0:T(2,128)S(1)} %get-tuple-element.79), channel_id=1, source_target_pairs={{0,176},{16,0},{32,16},{48,32},{64,48},{80,64},{96,80},{112,96},{1... | collective-permute-start | bytes 165896 | tf_op jit(solution)/shard_map/ppermute | solution.py:333
  75.2 6.0 %collective-permute-start.13 = (f32[54,2,128]{2,1,0:T(2,128)S(1)}, f32[54,2,128]{2,1,0:T(2,128)S(1)}, u32[]{:S(2)}, u32[]{:S(2)}) collective-permute-start(f32[54,2,128]{2,1,0:T(2,128)S(1)} %get-tuple-element.78), channel_id=1, source_target_pairs={{0,576},{192,0},{384,192},{576,384},{1,577},{193,1},{385,193},{577... | collective-permute-start | bytes 165896 | tf_op jit(solution)/shard_map/ppermute | solution.py:333
  81.5 9.3 %collective-permute-start.15 = (f32[27,4,128]{2,1,0:T(4,128)S(1)}, f32[27,4,128]{2,1,0:T(4,128)S(1)}, u32[]{:S(2)}, u32[]{:S(2)}) collective-permute-start(f32[27,4,128]{2,1,0:T(4,128)S(1)} %get-tuple-element.85), channel_id=1, source_target_pairs={{0,1},{1,2},{2,3},{3,4},{4,5},{5,6},{6,7},{7,8},{8,9},{9,10},{10,1... | collective-permute-start | bytes 165896 | tf_op jit(solution)/shard_map/ppermute | solution.py:333
  83.5 6.3 %collective-permute-start.16 = (f32[27,2,128]{2,1,0:T(2,128)S(1)}, f32[27,2,128]{2,1,0:T(2,128)S(1)}, u32[]{:S(2)}, u32[]{:S(2)}) collective-permute-start(f32[27,2,128]{2,1,0:T(2,128)S(1)} %get-tuple-element.86), channel_id=1, source_target_pairs={{0,16},{16,32},{32,48},{48,64},{64,80},{80,96},{96,112},{112,128},... | collective-permute-start | bytes 82952 | tf_op jit(solution)/shard_map/ppermute | solution.py:333
  85.4 4.4 %collective-permute-start.17 = (f32[27,2,128]{2,1,0:T(2,128)S(1)}, f32[27,2,128]{2,1,0:T(2,128)S(1)}, u32[]{:S(2)}, u32[]{:S(2)}) collective-permute-start(f32[27,2,128]{2,1,0:T(2,128)S(1)} %get-tuple-element.87), channel_id=1, source_target_pairs={{0,192},{192,384},{384,576},{576,0},{1,193},{193,385},{385,577},{5... | collective-permute-start | bytes 82952 | tf_op jit(solution)/shard_map/ppermute | solution.py:333

commit v5 on v3

--- a/solution.py
+++ b/solution.py
@@ -121,34 +121,24 @@
             mx[18 * n + c] = u_ref[18 * d + c, 0:2]
 
 
-def first_kernel(u_ref, my, mx, sems):
-    copies = [pltpu.make_async_copy(u_ref.at[18:72, 0:2], mx, sems.at[0])]
-    for n, (source, size, to) in enumerate(((0, 18, 0), (36, 36, 18))):
-        for row in range(2):
-            copies.append(
-                pltpu.make_async_copy(
-                    u_ref.at[source : source + size, 2 * row], my.at[to : to + size, row], sems.at[1 + 2 * n + row]
-                )
-            )
-    for copy in copies:
-        copy.start()
-    for copy in copies:
-        copy.wait()
-
-
-def first_faces(u):
-    shapes = [jax.ShapeDtypeStruct((54, 2, 1, 128), F32)] * 2
-    my, mx = pl.pallas_call(
-        first_kernel,
-        out_shape=shapes,
-        in_specs=[pl.BlockSpec(memory_space=pltpu.HBM)],
-        out_specs=[pl.BlockSpec(memory_space=pltpu.VMEM)] * 2,
-        scratch_shapes=[pltpu.SemaphoreType.DMA((5,))],
-        name="first",
-        cost_estimate=pl.CostEstimate(flops=0, bytes_accessed=4 * 54 * 512 * 2, transcendentals=0),
-        compiler_params=pltpu.CompilerParams(vmem_limit_bytes=8 * 1024 * 1024),
-    )(pltpu.with_memory_space_constraint(u.reshape(72, 4, 1, 128), pltpu.HBM))
-    return my.reshape(54, 2, 128), mx.reshape(54, 2, 128)
+def marker_kernel(u_ref, out):
+    out[...] = jnp.zeros_like(out)
+
+
+def marker(u):
+    return pl.pallas_call(
+        marker_kernel,
+        out_shape=jax.ShapeDtypeStruct((8, 128), F32),
+        in_specs=[pl.BlockSpec(memory_space=pl.ANY)],
+        out_specs=pl.BlockSpec(memory_space=pltpu.VMEM),
+        name="marker",
+        cost_estimate=pl.CostEstimate(flops=4000000000, bytes_accessed=40000000, transcendentals=0),
+        compiler_params=pltpu.CompilerParams(vmem_limit_bytes=1024 * 1024),
+    )(pltpu.with_memory_space_constraint(u, pltpu.HBM))
+
+
+def first_kernel(u_ref, mark, my, mx):
+    faces(u_ref, my, mx)
 
 
 def local_kernel(u_ref, r_ref, copy_ref=None):
@@ -383,7 +373,8 @@
 def body(gauge_links, momenta):
     u = gauge_links.reshape(72, 4, 128)
     p = momenta.reshape(72, 4, 128)
-    sent = (u, *first_faces(u))
+    mark = marker(u)
+    sent = (u, *call(first_kernel, FACES[1:], 1)(u, mark.reshape(1, 8, 128)))
     for repeat in range(3):
         rz, ry, rx = exchange(*sent, -1)
         if repeat < 2:

time: 93 us -> 92.1 us (level)
    pallas_call x14 -> x15, Pallas kernels: 5.23 us -> 5.29 us  [run(): pl.pallas_call(kernel, out_shape=[jax.ShapeDtypeStruct((o[0], o[1], 128),...]
  transfers between devices with their start and end apart: 18 -> 18, of which waited for: 9 -> 9; matrix products, arithmetic and copies ran while one was open for 0% -> 0% of each run, Pallas kernels for 5% -> 4%
where the time goes in v5:
time: 92.1 us; the launch traced here: 91.5 us
  starting transfers between devices  71 us (77%)
  waiting for transfers between devices  13.6 us (15%)
  Pallas kernels  6.01 us (7%)
    ppermute x18, starting transfers between devices, shifted(): lax.ppermute(value, axis, [(source, (source + steps) % count) for source...  71 us
    ppermute x18, waiting for transfers between devices, shifted(): lax.ppermute(value, axis, [(source, (source + steps) % count) for source...  13.6 us
    pallas_call x15, Pallas kernels, run(): pl.pallas_call(kernel, out_shape=[jax.ShapeDtypeStruct((o[0], o[1], 128),...  5.29 us
  transfers between devices with their start and end apart: 18, of which 9 were waited for; matrix products, arithmetic and copies ran while one was open for 0% of the time, Pallas kernels for 4%

profile of v5, /device:TPU:1, one launch (start us, length us, event | category | flops | bytes accessed | tf_op | source)
XLA Modules:
  0.0 91.5 jit_solution(15128294140212266704)
XLA Ops:
  0.6 8.5 %collective-permute-start = (f32[72,4,128]{2,1,0:T(4,128)}, f32[72,4,128]{2,1,0:T(4,128)S(1)}, u32[]{:S(2)}, u32[]{:S(2)}) collective-permute-start(f32[72,4,128]{2,1,0:T(4,128)} %bitcast.9), channel_id=1, source_target_pairs={{0,15},{1,0},{2,1},{3,2},{4,3},{5,4},{6,5},{7,6},{8,7},{9,8},{10,9... | collective-permute-start | bytes 442376 | tf_op jit(solution)/shard_map/ppermute | solution.py:360
  9.2 0.1 shard_map.42
  9.2 14.3 %collective-permute-start.2 = (f32[54,2,128]{2,1,0:T(2,128)S(1)}, f32[54,2,128]{2,1,0:T(2,128)S(1)}, u32[]{:S(2)}, u32[]{:S(2)}) collective-permute-start(f32[54,2,128]{2,1,0:T(2,128)S(1)} %get-tuple-element.47), channel_id=1, source_target_pairs={{0,176},{16,0},{32,16},{48,32},{64,48},{80,64},{96,80},{112,96},{1... | collective-permute-start | bytes 165896 | tf_op jit(solution)/shard_map/ppermute | solution.py:360
  23.6 3.1 %collective-permute-start.1 = (f32[54,2,128]{2,1,0:T(2,128)S(1)}, f32[54,2,128]{2,1,0:T(2,128)S(1)}, u32[]{:S(2)}, u32[]{:S(2)}) collective-permute-start(f32[54,2,128]{2,1,0:T(2,128)S(1)} %get-tuple-element.46), channel_id=1, source_target_pairs={{0,576},{192,0},{384,192},{576,384},{1,577},{193,1},{385,193},{577... | collective-permute-start | bytes 165896 | tf_op jit(solution)/shard_map/ppermute | solution.py:360
  26.7 0.2 shard_map.41.r_ref
  26.9 0.0 collective-permute-done.2.ry
  26.9 0.0 collective-permute-done.rz
  26.9 0.3 shard_map.43
  27.2 1.8 %collective-permute-done.1.rx = f32[54,2,128]{2,1,0:T(2,128)S(1)} collective-permute-done((f32[54,2,128]{2,1,0:T(2,128)S(1)}, f32[54,2,128]{2,1,0:T(2,128)S(1)}, u32[]{:S(2)}, u32[]{:S(2)}) %collective-permute-start.1) | collective-permute-done | bytes 55328 | tf_op jit(solution)/shard_map/ppermute | solution.py:360
  29.0 0.3 shard_map.44
  29.3 1.9 %collective-permute-start.3 = (f32[27,4,128]{2,1,0:T(4,128)S(1)}, f32[27,4,128]{2,1,0:T(4,128)S(1)}, u32[]{:S(2)}, u32[]{:S(2)}) collective-permute-start(f32[27,4,128]{2,1,0:T(4,128)S(1)} %get-tuple-element.55), channel_id=1, source_target_pairs={{0,1},{1,2},{2,3},{3,4},{4,5},{5,6},{6,7},{7,8},{8,9},{9,10},{10,1... | collective-permute-start | bytes 165896 | tf_op jit(solution)/shard_map/ppermute | solution.py:360
  31.2 1.9 %collective-permute-start.4 = (f32[27,2,128]{2,1,0:T(2,128)S(1)}, f32[27,2,128]{2,1,0:T(2,128)S(1)}, u32[]{:S(2)}, u32[]{:S(2)}) collective-permute-start(f32[27,2,128]{2,1,0:T(2,128)S(1)} %get-tuple-element.56), channel_id=1, source_target_pairs={{0,16},{16,32},{32,48},{48,64},{64,80},{80,96},{96,112},{112,128},... | collective-permute-start | bytes 82952 | tf_op jit(solution)/shard_map/ppermute | solution.py:360
  33.2 1.9 %collective-permute-start.5 = (f32[27,2,128]{2,1,0:T(2,128)S(1)}, f32[27,2,128]{2,1,0:T(2,128)S(1)}, u32[]{:S(2)}, u32[]{:S(2)}) collective-permute-start(f32[27,2,128]{2,1,0:T(2,128)S(1)} %get-tuple-element.57), channel_id=1, source_target_pairs={{0,192},{192,384},{384,576},{576,0},{1,193},{193,385},{385,577},{5... | collective-permute-start | bytes 82952 | tf_op jit(solution)/shard_map/ppermute | solution.py:360
  35.1 0.0 copy-start.1
  35.1 0.5 shard_map.45.f_ref
  35.6 1.9 %collective-permute-done.4.ty = f32[27,2,128]{2,1,0:T(2,128)S(1)} collective-permute-done((f32[27,2,128]{2,1,0:T(2,128)S(1)}, f32[27,2,128]{2,1,0:T(2,128)S(1)}, u32[]{:S(2)}, u32[]{:S(2)}) %collective-permute-start.4) | collective-permute-done | bytes 27680 | tf_op jit(solution)/shard_map/ppermute | solution.py:360
  37.6 0.0 collective-permute-done.5.tx
  37.6 1.0 %collective-permute-done.3.tz = f32[27,4,128]{2,1,0:T(4,128)S(1)} collective-permute-done((f32[27,4,128]{2,1,0:T(4,128)S(1)}, f32[27,4,128]{2,1,0:T(4,128)S(1)}, u32[]{:S(2)}, u32[]{:S(2)}) %collective-permute-start.3) | collective-permute-done | bytes 55328 | tf_op jit(solution)/shard_map/ppermute | solution.py:360
  38.6 0.4 shard_map.46
  39.0 5.8 %collective-permute-start.6 = (f32[54,4,128]{2,1,0:T(4,128)S(1)}, f32[54,4,128]{2,1,0:T(4,128)S(1)}, u32[]{:S(2)}, u32[]{:S(2)}) collective-permute-start(f32[54,4,128]{2,1,0:T(4,128)S(1)} %get-tuple-element.60), channel_id=1, source_target_pairs={{0,15},{1,0},{2,1},{3,2},{4,3},{5,4},{6,5},{7,6},{8,7},{9,8},{10,9... | collective-permute-start | bytes 331784 | tf_op jit(solution)/shard_map/ppermute | solution.py:360
  44.8 4.3 %collective-permute-start.8 = (f32[54,2,128]{2,1,0:T(2,128)S(1)}, f32[54,2,128]{2,1,0:T(2,128)S(1)}, u32[]{:S(2)}, u32[]{:S(2)}) collective-permute-start(f32[54,2,128]{2,1,0:T(2,128)S(1)} %get-tuple-element.62), channel_id=1, source_target_pairs={{0,176},{16,0},{32,16},{48,32},{64,48},{80,64},{96,80},{112,96},{1... | collective-permute-start | bytes 165896 | tf_op jit(solution)/shard_map/ppermute | solution.py:360
  49.1 3.8 %collective-permute-start.7 = (f32[54,2,128]{2,1,0:T(2,128)S(1)}, f32[54,2,128]{2,1,0:T(2,128)S(1)}, u32[]{:S(2)}, u32[]{:S(2)}) collective-permute-start(f32[54,2,128]{2,1,0:T(2,128)S(1)} %get-tuple-element.61), channel_id=1, source_target_pairs={{0,576},{192,0},{384,192},{576,384},{1,577},{193,1},{385,193},{577... | collective-permute-start | bytes 165896 | tf_op jit(solution)/shard_map/ppermute | solution.py:360
  52.9 0.2 shard_map.47.r_ref
  53.1 0.3 shard_map.48
  53.4 1.7 %collective-permute-done.7.rx = f32[54,2,128]{2,1,0:T(2,128)S(1)} collective-permute-done((f32[54,2,128]{2,1,0:T(2,128)S(1)}, f32[54,2,128]{2,1,0:T(2,128)S(1)}, u32[]{:S(2)}, u32[]{:S(2)}) %collective-permute-start.7) | collective-permute-done | bytes 55328 | tf_op jit(solution)/shard_map/ppermute | solution.py:360
  55.1 0.3 shard_map.49
  55.4 1.9 %collective-permute-start.9 = (f32[27,4,128]{2,1,0:T(4,128)S(1)}, f32[27,4,128]{2,1,0:T(4,128)S(1)}, u32[]{:S(2)}, u32[]{:S(2)}) collective-permute-start(f32[27,4,128]{2,1,0:T(4,128)S(1)} %get-tuple-element.70), channel_id=1, source_target_pairs={{0,1},{1,2},{2,3},{3,4},{4,5},{5,6},{6,7},{7,8},{8,9},{9,10},{10,1... | collective-permute-start | bytes 165896 | tf_op jit(solution)/shard_map/ppermute | solution.py:360
  57.3 1.9 %collective-permute-start.10 = (f32[27,2,128]{2,1,0:T(2,128)S(1)}, f32[27,2,128]{2,1,0:T(2,128)S(1)}, u32[]{:S(2)}, u32[]{:S(2)}) collective-permute-start(f32[27,2,128]{2,1,0:T(2,128)S(1)} %get-tuple-element.71), channel_id=1, source_target_pairs={{0,16},{16,32},{32,48},{48,64},{64,80},{80,96},{96,112},{112,128},... | collective-permute-start | bytes 82952 | tf_op jit(solution)/shard_map/ppermute | solution.py:360
  59.3 1.9 %collective-permute-start.11 = (f32[27,2,128]{2,1,0:T(2,128)S(1)}, f32[27,2,128]{2,1,0:T(2,128)S(1)}, u32[]{:S(2)}, u32[]{:S(2)}) collective-permute-start(f32[27,2,128]{2,1,0:T(2,128)S(1)} %get-tuple-element.72), channel_id=1, source_target_pairs={{0,192},{192,384},{384,576},{576,0},{1,193},{193,385},{385,577},{5... | collective-permute-start | bytes 82952 | tf_op jit(solution)/shard_map/ppermute | solution.py:360
  61.2 0.5 shard_map.50.f_ref
  61.7 2.0 %collective-permute-done.10.ty = f32[27,2,128]{2,1,0:T(2,128)S(1)} collective-permute-done((f32[27,2,128]{2,1,0:T(2,128)S(1)}, f32[27,2,128]{2,1,0:T(2,128)S(1)}, u32[]{:S(2)}, u32[]{:S(2)}) %collective-permute-start.10) | collective-permute-done | bytes 27680 | tf_op jit(solution)/shard_map/ppermute | solution.py:360
  63.7 1.1 %collective-permute-done.9.tz = f32[27,4,128]{2,1,0:T(4,128)S(1)} collective-permute-done((f32[27,4,128]{2,1,0:T(4,128)S(1)}, f32[27,4,128]{2,1,0:T(4,128)S(1)}, u32[]{:S(2)}, u32[]{:S(2)}) %collective-permute-start.9) | collective-permute-done | bytes 55328 | tf_op jit(solution)/shard_map/ppermute | solution.py:360
  64.8 0.4 shard_map.51
  65.2 5.3 %collective-permute-start.12 = (f32[54,4,128]{2,1,0:T(4,128)S(1)}, f32[54,4,128]{2,1,0:T(4,128)S(1)}, u32[]{:S(2)}, u32[]{:S(2)}) collective-permute-start(f32[54,4,128]{2,1,0:T(4,128)S(1)} %get-tuple-element.76), channel_id=1, source_target_pairs={{0,15},{1,0},{2,1},{3,2},{4,3},{5,4},{6,5},{7,6},{8,7},{9,8},{10,9... | collective-permute-start | bytes 331784 | tf_op jit(solution)/shard_map/ppermute | solution.py:360
  70.5 4.7 %collective-permute-start.14 = (f32[54,2,128]{2,1,0:T(2,128)S(1)}, f32[54,2,128]{2,1,0:T(2,128)S(1)}, u32[]{:S(2)}, u32[]{:S(2)}) collective-permute-start(f32[54,2,128]{2,1,0:T(2,128)S(1)} %get-tuple-element.79), channel_id=1, source_target_pairs={{0,176},{16,0},{32,16},{48,32},{64,48},{80,64},{96,80},{112,96},{1... | collective-permute-start | bytes 165896 | tf_op jit(solution)/shard_map/ppermute | solution.py:360
  75.2 3.8 %collective-permute-start.13 = (f32[54,2,128]{2,1,0:T(2,128)S(1)}, f32[54,2,128]{2,1,0:T(2,128)S(1)}, u32[]{:S(2)}, u32[]{:S(2)}) collective-permute-start(f32[54,2,128]{2,1,0:T(2,128)S(1)} %get-tuple-element.78), channel_id=1, source_target_pairs={{0,576},{192,0},{384,192},{576,384},{1,577},{193,1},{385,193},{577... | collective-permute-start | bytes 165896 | tf_op jit(solution)/shard_map/ppermute | solution.py:360
  79.1 0.7 shard_map.52
  79.8 0.0 collective-permute-done.14.ry
  79.8 0.3 shard_map.53
  80.1 1.1 %collective-permute-done.13.rx = f32[54,2,128]{2,1,0:T(2,128)S(1)} collective-permute-done((f32[54,2,128]{2,1,0:T(2,128)S(1)}, f32[54,2,128]{2,1,0:T(2,128)S(1)}, u32[]{:S(2)}, u32[]{:S(2)}) %collective-permute-start.13) | collective-permute-done | bytes 55328 | tf_op jit(solution)/shard_map/ppermute | solution.py:360
  81.2 0.3 shard_map.54
  81.5 1.9 %collective-permute-start.15 = (f32[27,4,128]{2,1,0:T(4,128)S(1)}, f32[27,4,128]{2,1,0:T(4,128)S(1)}, u32[]{:S(2)}, u32[]{:S(2)}) collective-permute-start(f32[27,4,128]{2,1,0:T(4,128)S(1)} %get-tuple-element.87), channel_id=1, source_target_pairs={{0,1},{1,2},{2,3},{3,4},{4,5},{5,6},{6,7},{7,8},{8,9},{9,10},{10,1... | collective-permute-start | bytes 165896 | tf_op jit(solution)/shard_map/ppermute | solution.py:360
  83.4 1.9 %collective-permute-start.16 = (f32[27,2,128]{2,1,0:T(2,128)S(1)}, f32[27,2,128]{2,1,0:T(2,128)S(1)}, u32[]{:S(2)}, u32[]{:S(2)}) collective-permute-start(f32[27,2,128]{2,1,0:T(2,128)S(1)} %get-tuple-element.88), channel_id=1, source_target_pairs={{0,16},{16,32},{32,48},{48,64},{64,80},{80,96},{96,112},{112,128},... | collective-permute-start | bytes 82952 | tf_op jit(solution)/shard_map/ppermute | solution.py:360
  85.4 1.9 %collective-permute-start.17 = (f32[27,2,128]{2,1,0:T(2,128)S(1)}, f32[27,2,128]{2,1,0:T(2,128)S(1)}, u32[]{:S(2)}, u32[]{:S(2)}) collective-permute-start(f32[27,2,128]{2,1,0:T(2,128)S(1)} %get-tuple-element.89), channel_id=1, source_target_pairs={{0,192},{192,384},{384,576},{576,0},{1,193},{193,385},{385,577},{5... | collective-permute-start | bytes 82952 | tf_op jit(solution)/shard_map/ppermute | solution.py:360
  87.3 0.5 shard_map.55.f_ref
  87.8 1.9 %collective-permute-done.16.ty = f32[27,2,128]{2,1,0:T(2,128)S(1)} collective-permute-done((f32[27,2,128]{2,1,0:T(2,128)S(1)}, f32[27,2,128]{2,1,0:T(2,128)S(1)}, u32[]{:S(2)}, u32[]{:S(2)}) %collective-permute-start.16) | collective-permute-done | bytes 27680 | tf_op jit(solution)/shard_map/ppermute | solution.py:360
  89.7 1.1 %collective-permute-done.15.tz = f32[27,4,128]{2,1,0:T(4,128)S(1)} collective-permute-done((f32[27,4,128]{2,1,0:T(4,128)S(1)}, f32[27,4,128]{2,1,0:T(4,128)S(1)}, u32[]{:S(2)}, u32[]{:S(2)}) %collective-permute-start.15) | collective-permute-done | bytes 55328 | tf_op jit(solution)/shard_map/ppermute | solution.py:360
  90.8 0.7 last.1
  (9 shorter events, 0.0 us)
Async XLA Ops:
  0.6 8.5 %copy-start = (f32[4,3,3,2,2,2,1,128]{7,6,5,4,3,2,1,0:T(1,128)S(1)}, f32[4,3,3,2,2,2,1,128]{7,6,5,4,3,2,1,0:T(1,128)}, u32[]{:S(2)}) copy-start(f32[4,3,3,2,2,2,1,128]{7,6,5,4,3,2,1,0:T(1,128)} %param.2) | copy-start | bytes 442372
  0.6 26.2 %collective-permute-start = (f32[72,4,128]{2,1,0:T(4,128)}, f32[72,4,128]{2,1,0:T(4,128)S(1)}, u32[]{:S(2)}, u32[]{:S(2)}) collective-permute-start(f32[72,4,128]{2,1,0:T(4,128)} %bitcast.9), channel_id=1, source_target_pairs={{0,15},{1,0},{2,1},{3,2},{4,3},{5,4},{6,5},{7,6},{8,7},{9,8},{10,9... | collective-permute-start | bytes 442376 | tf_op jit(solution)/shard_map/ppermute | solution.py:360
  9.2 17.6 %collective-permute-start.2 = (f32[54,2,128]{2,1,0:T(2,128)S(1)}, f32[54,2,128]{2,1,0:T(2,128)S(1)}, u32[]{:S(2)}, u32[]{:S(2)}) collective-permute-start(f32[54,2,128]{2,1,0:T(2,128)S(1)} %get-tuple-element.47), channel_id=1, source_target_pairs={{0,176},{16,0},{32,16},{48,32},{64,48},{80,64},{96,80},{112,96},{1... | collective-permute-start | bytes 165896 | tf_op jit(solution)/shard_map/ppermute | solution.py:360
  23.6 5.5 %collective-permute-start.1 = (f32[54,2,128]{2,1,0:T(2,128)S(1)}, f32[54,2,128]{2,1,0:T(2,128)S(1)}, u32[]{:S(2)}, u32[]{:S(2)}) collective-permute-start(f32[54,2,128]{2,1,0:T(2,128)S(1)} %get-tuple-element.46), channel_id=1, source_target_pairs={{0,576},{192,0},{384,192},{576,384},{1,577},{193,1},{385,193},{577... | collective-permute-start | bytes 165896 | tf_op jit(solution)/shard_map/ppermute | solution.py:360
  29.3 9.3 %collective-permute-start.3 = (f32[27,4,128]{2,1,0:T(4,128)S(1)}, f32[27,4,128]{2,1,0:T(4,128)S(1)}, u32[]{:S(2)}, u32[]{:S(2)}) collective-permute-start(f32[27,4,128]{2,1,0:T(4,128)S(1)} %get-tuple-element.55), channel_id=1, source_target_pairs={{0,1},{1,2},{2,3},{3,4},{4,5},{5,6},{6,7},{7,8},{8,9},{9,10},{10,1... | collective-permute-start | bytes 165896 | tf_op jit(solution)/shard_map/ppermute | solution.py:360
  31.2 6.3 %collective-permute-start.4 = (f32[27,2,128]{2,1,0:T(2,128)S(1)}, f32[27,2,128]{2,1,0:T(2,128)S(1)}, u32[]{:S(2)}, u32[]{:S(2)}) collective-permute-start(f32[27,2,128]{2,1,0:T(2,128)S(1)} %get-tuple-element.56), channel_id=1, source_target_pairs={{0,16},{16,32},{32,48},{48,64},{64,80},{80,96},{96,112},{112,128},... | collective-permute-start | bytes 82952 | tf_op jit(solution)/shard_map/ppermute | solution.py:360
  33.2 4.4 %collective-permute-start.5 = (f32[27,2,128]{2,1,0:T(2,128)S(1)}, f32[27,2,128]{2,1,0:T(2,128)S(1)}, u32[]{:S(2)}, u32[]{:S(2)}) collective-permute-start(f32[27,2,128]{2,1,0:T(2,128)S(1)} %get-tuple-element.57), channel_id=1, source_target_pairs={{0,192},{192,384},{384,576},{576,0},{1,193},{193,385},{385,577},{5... | collective-permute-start | bytes 82952 | tf_op jit(solution)/shard_map/ppermute | solution.py:360
  35.1 3.5 %copy-start.1 = (f32[4,3,3,2,2,2,1,128]{7,6,5,4,3,2,1,0:T(1,128)S(1)}, f32[4,3,3,2,2,2,1,128]{7,6,5,4,3,2,1,0:T(1,128)}, u32[]{:S(2)}) copy-start(f32[4,3,3,2,2,2,1,128]{7,6,5,4,3,2,1,0:T(1,128)} %param.3) | copy-start | bytes 442372
  39.0 14.1 %collective-permute-start.6 = (f32[54,4,128]{2,1,0:T(4,128)S(1)}, f32[54,4,128]{2,1,0:T(4,128)S(1)}, u32[]{:S(2)}, u32[]{:S(2)}) collective-permute-start(f32[54,4,128]{2,1,0:T(4,128)S(1)} %get-tuple-element.60), channel_id=1, source_target_pairs={{0,15},{1,0},{2,1},{3,2},{4,3},{5,4},{6,5},{7,6},{8,7},{9,8},{10,9... | collective-permute-start | bytes 331784 | tf_op jit(solution)/shard_map/ppermute | solution.py:360
  44.8 8.3 %collective-permute-start.8 = (f32[54,2,128]{2,1,0:T(2,128)S(1)}, f32[54,2,128]{2,1,0:T(2,128)S(1)}, u32[]{:S(2)}, u32[]{:S(2)}) collective-permute-start(f32[54,2,128]{2,1,0:T(2,128)S(1)} %get-tuple-element.62), channel_id=1, source_target_pairs={{0,176},{16,0},{32,16},{48,32},{64,48},{80,64},{96,80},{112,96},{1... | collective-permute-start | bytes 165896 | tf_op jit(solution)/shard_map/ppermute | solution.py:360
  49.1 6.0 %collective-permute-start.7 = (f32[54,2,128]{2,1,0:T(2,128)S(1)}, f32[54,2,128]{2,1,0:T(2,128)S(1)}, u32[]{:S(2)}, u32[]{:S(2)}) collective-permute-start(f32[54,2,128]{2,1,0:T(2,128)S(1)} %get-tuple-element.61), channel_id=1, source_target_pairs={{0,576},{192,0},{384,192},{576,384},{1,577},{193,1},{385,193},{577... | collective-permute-start | bytes 165896 | tf_op jit(solution)/shard_map/ppermute | solution.py:360
  55.4 9.4 %collective-permute-start.9 = (f32[27,4,128]{2,1,0:T(4,128)S(1)}, f32[27,4,128]{2,1,0:T(4,128)S(1)}, u32[]{:S(2)}, u32[]{:S(2)}) collective-permute-start(f32[27,4,128]{2,1,0:T(4,128)S(1)} %get-tuple-element.70), channel_id=1, source_target_pairs={{0,1},{1,2},{2,3},{3,4},{4,5},{5,6},{6,7},{7,8},{8,9},{9,10},{10,1... | collective-permute-start | bytes 165896 | tf_op jit(solution)/shard_map/ppermute | solution.py:360
  57.3 6.4 %collective-permute-start.10 = (f32[27,2,128]{2,1,0:T(2,128)S(1)}, f32[27,2,128]{2,1,0:T(2,128)S(1)}, u32[]{:S(2)}, u32[]{:S(2)}) collective-permute-start(f32[27,2,128]{2,1,0:T(2,128)S(1)} %get-tuple-element.71), channel_id=1, source_target_pairs={{0,16},{16,32},{32,48},{48,64},{64,80},{80,96},{96,112},{112,128},... | collective-permute-start | bytes 82952 | tf_op jit(solution)/shard_map/ppermute | solution.py:360
  59.3 4.5 %collective-permute-start.11 = (f32[27,2,128]{2,1,0:T(2,128)S(1)}, f32[27,2,128]{2,1,0:T(2,128)S(1)}, u32[]{:S(2)}, u32[]{:S(2)}) collective-permute-start(f32[27,2,128]{2,1,0:T(2,128)S(1)} %get-tuple-element.72), channel_id=1, source_target_pairs={{0,192},{192,384},{384,576},{576,0},{1,193},{193,385},{385,577},{5... | collective-permute-start | bytes 82952 | tf_op jit(solution)/shard_map/ppermute | solution.py:360
  65.2 14.6 %collective-permute-start.12 = (f32[54,4,128]{2,1,0:T(4,128)S(1)}, f32[54,4,128]{2,1,0:T(4,128)S(1)}, u32[]{:S(2)}, u32[]{:S(2)}) collective-permute-start(f32[54,4,128]{2,1,0:T(4,128)S(1)} %get-tuple-element.76), channel_id=1, source_target_pairs={{0,15},{1,0},{2,1},{3,2},{4,3},{5,4},{6,5},{7,6},{8,7},{9,8},{10,9... | collective-permute-start | bytes 331784 | tf_op jit(solution)/shard_map/ppermute | solution.py:360
  70.5 9.2 %collective-permute-start.14 = (f32[54,2,128]{2,1,0:T(2,128)S(1)}, f32[54,2,128]{2,1,0:T(2,128)S(1)}, u32[]{:S(2)}, u32[]{:S(2)}) collective-permute-start(f32[54,2,128]{2,1,0:T(2,128)S(1)} %get-tuple-element.79), channel_id=1, source_target_pairs={{0,176},{16,0},{32,16},{48,32},{64,48},{80,64},{96,80},{112,96},{1... | collective-permute-start | bytes 165896 | tf_op jit(solution)/shard_map/ppermute | solution.py:360
  75.2 6.0 %collective-permute-start.13 = (f32[54,2,128]{2,1,0:T(2,128)S(1)}, f32[54,2,128]{2,1,0:T(2,128)S(1)}, u32[]{:S(2)}, u32[]{:S(2)}) collective-permute-start(f32[54,2,128]{2,1,0:T(2,128)S(1)} %get-tuple-element.78), channel_id=1, source_target_pairs={{0,576},{192,0},{384,192},{576,384},{1,577},{193,1},{385,193},{577... | collective-permute-start | bytes 165896 | tf_op jit(solution)/shard_map/ppermute | solution.py:360
  81.5 9.3 %collective-permute-start.15 = (f32[27,4,128]{2,1,0:T(4,128)S(1)}, f32[27,4,128]{2,1,0:T(4,128)S(1)}, u32[]{:S(2)}, u32[]{:S(2)}) collective-permute-start(f32[27,4,128]{2,1,0:T(4,128)S(1)} %get-tuple-element.87), channel_id=1, source_target_pairs={{0,1},{1,2},{2,3},{3,4},{4,5},{5,6},{6,7},{7,8},{8,9},{9,10},{10,1... | collective-permute-start | bytes 165896 | tf_op jit(solution)/shard_map/ppermute | solution.py:360
  83.4 6.3 %collective-permute-start.16 = (f32[27,2,128]{2,1,0:T(2,128)S(1)}, f32[27,2,128]{2,1,0:T(2,128)S(1)}, u32[]{:S(2)}, u32[]{:S(2)}) collective-permute-start(f32[27,2,128]{2,1,0:T(2,128)S(1)} %get-tuple-element.88), channel_id=1, source_target_pairs={{0,16},{16,32},{32,48},{48,64},{64,80},{80,96},{96,112},{112,128},... | collective-permute-start | bytes 82952 | tf_op jit(solution)/shard_map/ppermute | solution.py:360
  85.4 4.4 %collective-permute-start.17 = (f32[27,2,128]{2,1,0:T(2,128)S(1)}, f32[27,2,128]{2,1,0:T(2,128)S(1)}, u32[]{:S(2)}, u32[]{:S(2)}) collective-permute-start(f32[27,2,128]{2,1,0:T(2,128)S(1)} %get-tuple-element.89), channel_id=1, source_target_pairs={{0,192},{192,384},{384,576},{576,0},{1,193},{193,385},{385,577},{5... | collective-permute-start | bytes 82952 | tf_op jit(solution)/shard_map/ppermute | solution.py:360
